TPU v7x, 32 devices: a whole 2x2x4 slice. The times are simulated.
32 devices in a mesh: occ: 8 (over y, x, core), vir: 4 (over z).
Axes of the slice: x: 2, y: 2, z: 4, core: 2. Of those that a mesh axis runs over, the one named last changes fastest.
Arguments:
- ints_alpha: bfloat16 [1536, 8, 1024], P('occ', None, 'vir'), may hold values from -0.71875 to 0.71875
- ints_beta: bfloat16 [1536, 8, 1024], P('occ', None, 'vir'), may hold values from -0.71875 to 0.71875
- metric: bfloat16 [1536, 1536], P('vir'), may hold values from -0.5 to 1.5, as said below
- e_occ_alpha: float32 [8], P('occ'), may hold values from -2 to -0.3
- e_occ_beta: float32 [8], replicated, may hold values from -2 to -0.3
- e_vir_alpha: float32 [1024], replicated, may hold values from 0.2 to 3
- e_vir_beta: float32 [1024], P('vir'), may hold values from 0.2 to 3
Outputs:
- gamma_alpha: bfloat16 [1536, 8, 1024], P(None, 'occ', 'vir')
- gamma_beta: bfloat16 [1536, 8, 1024], P(None, 'occ', 'vir')
Inputs may be any that keep to these rules, and one draw needn't show every extreme that they name: `metric`: symmetric and positive definite.
All inputs are finite; a program needn't handle non-finite values.
Results may differ from a plain program's by a relative error of at most 0.009.
Values may be sent and summed in bfloat16 or wider, within the bound.
No kernel may reach another device: no remote copies, remote signals or barrier semaphores. Data moves between devices by JAX's collectives and lax.ppermute only.
A program may use at most 64 MiB of HBM per device.

v0:
```python
import jax
import jax.numpy as jnp
from jax import lax
from jax.experimental import pallas as pl
from jax.experimental.pallas import tpu as pltpu
from jax.sharding import PartitionSpec as P

BF16, F32 = jnp.bfloat16, jnp.float32
VMEM = pl.BlockSpec(memory_space=pltpu.VMEM)
SMEM = pl.BlockSpec(memory_space=pltpu.SMEM)


def swap(value, axis, mask):
    pairs = [(source, source ^ mask) for source in range(lax.axis_size(axis))]
    return lax.ppermute(value, axis, pairs)


def alpha_of(device):
    return device ^ (2 * (device & 1))


def beta_of(device):
    return device ^ (2 * (1 - (device & 1)))


def shape_of(*dims, dtype=BF16):
    return jax.ShapeDtypeStruct(dims, dtype)


def call(kernel, shapes, *args, scratch=(), flops=0, specs=None):
    return pl.pallas_call(
        kernel,
        out_shape=shapes,
        in_specs=specs or [VMEM] * len(args),
        out_specs=jax.tree.map(lambda _: VMEM, shapes),
        scratch_shapes=scratch,
        cost_estimate=pl.CostEstimate(
            flops=flops, bytes_accessed=1 << 20, transcendentals=0
        ),
        compiler_params=pltpu.CompilerParams(vmem_limit_bytes=20 << 20),
    )(*args)


def dots(a, b, da, db):
    return lax.dot_general(a, b, (((da,), (db,)), ((), ())), preferred_element_type=F32)


def at(start, size):
    return pl.ds(pl.multiple_of(start, size), size)


def split_rows(index_of, chips, source, *refs):
    outs, table = refs[:-1], refs[-1]
    rows, blocks, cols = source.shape
    step = 16
    wide = step * blocks
    to = lax.broadcasted_iota(jnp.int32, (wide, wide), 0)
    by = lax.broadcasted_iota(jnp.int32, (wide, wide), 1)
    pick = jnp.where(by == (to % step) * blocks + to // step, 1.0, 0.0).astype(BF16)
    for q in range(0, rows, step):
        tile = dots(pick, source[q : q + step].reshape(wide, cols), 1, 0).astype(BF16)
        for d in range(blocks):
            table[d, q : q + step, :] = tile[d * step : (d + 1) * step]
    chip = lax.axis_index("occ") // 2
    for m in range(chips):
        for c in (0, 1):
            outs[m][c] = table[index_of(2 * (chip ^ m) + c)]


def give_rows(*refs):
    held, out = refs[:-1], refs[-1]
    core = lax.axis_index("occ") % 2
    for m, ref in enumerate(held):
        out[m] = ref[1 - core]


def place_rows(chips, *refs):
    held, take, out = refs[:chips], refs[chips], refs[-1]
    rows = take.shape[1]
    me = lax.axis_index("occ")
    chip, core = me // 2, me % 2
    for m in range(chips):
        start = 2 * (chip ^ m) * rows
        out[at(start + core * rows, rows), :] = held[m][core]
        out[at(start + (1 - core) * rows, rows), :] = take[m]


def regroup(ints, index_of):
    blocks = lax.axis_size("occ")
    chips = blocks // 2
    rows, _, cols = ints.shape
    if chips > 4:
        table = ints.transpose(1, 0, 2)
        table = jnp.stack([table[index_of(d)] for d in range(blocks)])
        got = lax.all_to_all(table, "occ", split_axis=0, concat_axis=0, tiled=True)
        return got.reshape(blocks * rows, cols)
    held = [*call(
        lambda *refs: split_rows(index_of, chips, *refs),
        [shape_of(2, rows, cols)] * chips,
        ints,
        scratch=[pltpu.VMEM((blocks, rows, cols), BF16)],
    )]
    for m in range(1, chips):
        held[m] = swap(held[m], "occ", 2 * m)
    give = call(give_rows, shape_of(chips, rows, cols), *held)
    take = swap(give, "occ", 1)
    place = lambda *refs: place_rows(chips, *refs)
    return call(place, shape_of(blocks * rows, cols), *held, take)


def halves_metric(metric):
    rows = metric.shape[0]
    half = rows // 2
    core, layer = lax.axis_index("occ") % 2, lax.axis_index("vir")
    mine = lax.dynamic_slice_in_dim(metric, core * half, half, 0)
    got = jnp.stack([swap(mine, "vir", k) for k in (1, 2, 3)])
    other = swap(got, "occ", 1)
    lo, hi = jnp.where(core == 0, got, other), jnp.where(core == 0, other, got)
    rest = jnp.concatenate([lo, hi], axis=1)
    pieces = [metric, rest[0], rest[1], rest[2]]
    return jnp.concatenate([lax.select_n(layer ^ k, *pieces) for k in range(4)], axis=0)


def place_metric(chips, *refs):
    own, mine, other, out = refs[0], refs[1 : 1 + chips], refs[1 + chips : 1 + 2 * chips], refs[-1]
    rows = own.shape[0]
    part = mine[0].shape[1]
    me, layer = lax.axis_index("occ"), lax.axis_index("vir")
    chip, core = me // 2, me % 2
    out[at(layer * rows, rows), :] = own[...]
    for k in (1, 2, 3):
        for m in range(chips):
            for c, held in ((core, mine), (1 - core, other)):
                start = (layer ^ k) * rows + (2 * (chip ^ m) + c) * part
                out[at(start, part), :] = held[m][k - 1]


def whole_metric(metric):
    rows, aux = metric.shape
    blocks = lax.axis_size("occ")
    chips = blocks // 2
    if chips > 4 or rows % (16 * blocks):
        return halves_metric(metric)
    part = rows // blocks
    mine = lax.dynamic_slice_in_dim(metric, lax.axis_index("occ") * part, part, 0)
    got = [swap(mine, "vir", k) for k in (1, 2, 3)]

    def pack(*refs):
        for k in range(3):
            refs[-1][k] = refs[k][...]

    got = call(pack, shape_of(3, part, aux), *got)
    plane = [got] + [swap(got, "occ", 2 * m) for m in range(1, chips)]
    other = [swap(p, "occ", 1) for p in plane]
    place = lambda *refs: place_metric(chips, *refs)
    return call(place, shape_of(aux, aux), metric, *plane, *other)


def row_chunks(rows, body, step=256):
    def one(i, carry):
        body(at(i * step, step))
        return carry

    lax.fori_loop(0, rows // step, one, 0)


def fit_rows(square, raw, out):
    def body(rows):
        out[rows, :] = dots(square[rows, :], raw[...], 1, 0).astype(BF16)

    row_chunks(square.shape[0], body)


def fit(square, raw):
    aux, unit = raw.shape
    return call(fit_rows, shape_of(aux, unit), square, raw, flops=2 * aux * aux * unit)


def tile_rows(occ_a, occ_o, occ_b, vir_a, vir_b, a0, a1, o0, o1, beta, amp, gamma, flip):
    layer, me = lax.axis_index("vir"), lax.axis_index("occ")
    unit = beta.shape[1]
    alphas = (a0, a1, o0, o1)
    flip[...] = beta[...].T
    right = occ_b[beta_of(me)] - vir_b[...]
    right = jnp.broadcast_to(right, (128, unit)).T[:, :1]
    for u, alpha in enumerate(alphas):
        row = vir_a[pl.ds(layer ^ (u % 2), 1), :]
        left = (occ_a, occ_a, occ_o, occ_o)[u][0] - row
        pair = dots(flip[...], alpha[...], 1, 0)
        amp[u] = (pair / (left + right)).astype(BF16)

    def body(rows):
        total = dots(a0[rows, :], amp[0], 1, 1)
        for u in (1, 2, 3):
            total = total + dots(alphas[u][rows, :], amp[u], 1, 1)
        gamma[rows, :] = total.astype(gamma.dtype)

    row_chunks(beta.shape[0], body)


def tile(energies, alphas, beta, dtype):
    aux, unit = beta.shape
    return call(
        tile_rows,
        [shape_of(4, unit, unit), shape_of(aux, unit, dtype=dtype)],
        *energies,
        *alphas,
        beta,
        scratch=[pltpu.VMEM((unit, aux), BF16)],
        flops=16 * aux * unit * unit,
        specs=[SMEM] * 3 + [VMEM] * 7,
    )


def term_rows(first, own, near, amp_own, amp_near, out):
    def body(rows):
        for u in (0, 1):
            cols = slice(u * own.shape[1], (u + 1) * own.shape[1])
            total = dots(own[rows, :], amp_own[first + u], 1, 0)
            total = total + dots(near[rows, :], amp_near[first + u], 1, 0)
            out[rows, cols] = total.astype(out.dtype)

    row_chunks(own.shape[0], body)


def term(first, own, near, amp_own, amp_near, dtype):
    aux, unit = own.shape
    kernel = lambda *refs: term_rows(first, *refs)
    shape = shape_of(aux, 2 * unit, dtype=dtype)
    flops = 8 * aux * unit * unit
    return call(kernel, shape, own, near, amp_own, amp_near, flops=flops)


def mix_rows(gamma_alpha, from_core, own, near, send_a, send_b, keep_a, keep_b):
    unit = own.shape[1]
    odd = lax.axis_index("occ") % 2 == 1

    def body(rows):
        alpha = gamma_alpha[rows, :] + from_core[rows, :].astype(F32)
        here, there = alpha[:, :unit], alpha[:, unit:].astype(BF16)
        beta, far = own[rows, :], near[rows, :]
        keep_a[rows, :] = jnp.where(odd, here, beta)
        keep_b[rows, :] = jnp.where(odd, beta, here)
        send_a[rows, :] = jnp.where(odd, there, far)
        send_b[rows, :] = jnp.where(odd, far, there)

    row_chunks(own.shape[0], body)


def ring(ints_alpha, ints_beta, metric, e_occ_alpha, e_occ_beta, e_vir_alpha, e_vir_beta):
    aux = metric.shape[1]
    unit = e_vir_beta.shape[0]
    blocks, layers = lax.axis_size("occ"), lax.axis_size("vir")
    assert layers == 4 and e_occ_alpha.shape[0] == 1
    core = lax.axis_index("occ") % 2

    square = whole_metric(metric)
    raw_beta = regroup(ints_beta, beta_of)
    raw_alpha = regroup(ints_alpha, alpha_of)

    occ_mine = lax.ppermute(e_occ_alpha, "occ", [(alpha_of(d), d) for d in range(blocks)])
    occ_other = swap(occ_mine, "occ", 1)
    vir_near = swap(e_vir_beta, "vir", 3)
    common = [occ_mine, occ_other, e_occ_beta, e_vir_alpha.reshape(layers, unit)]

    near_beta = swap(raw_beta, "vir", 3)
    near_alpha = swap(raw_alpha, "vir", 1)

    a0 = fit(square, raw_alpha)
    b0 = fit(square, raw_beta)
    a1 = fit(square, near_alpha)
    o0, o1 = swap(a0, "occ", 1), swap(a1, "occ", 1)
    alphas = (a0, a1, o0, o1)
    amp_own, gamma_own = tile(common + [e_vir_beta[None]], alphas, b0, F32)
    b1 = fit(square, near_beta)
    amp_near, gamma_near = tile(common + [vir_near[None]], alphas, b1, BF16)
    other_term = term(2, b0, b1, amp_own, amp_near, BF16)
    from_core = swap(other_term, "occ", 1)
    mine_term = term(0, b0, b1, amp_own, amp_near, F32)
    send_a, send_b, keep_a, keep_b = call(
        mix_rows,
        [shape_of(aux, unit)] * 2 + [shape_of(aux, unit, dtype=F32)] * 2,
        mine_term,
        from_core,
        gamma_own,
        gamma_near,
    )

    def back(send, keep, odd, even):
        pairs = [
            (d * layers + v, d * layers + (v ^ (odd if d % 2 else even)))
            for d in range(blocks)
            for v in range(layers)
        ]
        got = lax.ppermute(send, ("occ", "vir"), pairs)
        return (keep + got.astype(F32)).astype(BF16)

    done_a = back(send_a, keep_a, 1, 3)
    moved = swap(done_a, "occ", 2)
    kept = back(send_b, keep_b, 3, 1)
    out_alpha = jnp.where(core == 1, moved, kept).reshape(aux, 1, unit)
    out_beta = jnp.where(core == 1, kept, moved).reshape(aux, 1, unit)
    return out_alpha, out_beta


def solution(mesh):
    in_specs = (
        P("occ", None, "vir"),
        P("occ", None, "vir"),
        P("vir", None),
        P("occ"),
        P(),
        P(),
        P("vir"),
    )
    out_specs = (P(None, "occ", "vir"), P(None, "occ", "vir"))

    return jax.shard_map(ring, mesh=mesh, in_specs=in_specs, out_specs=out_specs, check_vma=False)
```

profile of v0, /device:TPU:12, one launch (start us, length us, event | category | flops | bytes accessed | tf_op | source)
XLA Modules:
  0.0 144.0 jit_solution(11657350783074112113)
XLA Ops:
  2.2 1.6 %collective-permute-start.17 = (bf16[2,192,256]{2,1,0:T(8,128)(2,1)S(1)}, bf16[2,192,256]{2,1,0:T(8,128)(2,1)S(1)}, u32[]{:S(2)}, u32[]{:S(2)}) collective-permute-start(bf16[2,192,256]{2,1,0:T(8,128)(2,1)S(1)} %get-tuple-element.23), channel_id=1, source_target_pairs={{0,8},{4,12},{8,0},{12,4},{16,24},{20,28},{24,16},{28,20},{1,9},{5... | collective-permute-start | bytes 589832 | tf_op jit(solution)/shard_map/ppermute | solution.py:15
  6.7 1.6 %collective-permute-start.2 = (bf16[48,1536]{1,0:T(8,128)(2,1)S(1)}, bf16[48,1536]{1,0:T(8,128)(2,1)S(1)}, u32[]{:S(2)}, u32[]{:S(2)}) collective-permute-start(bf16[48,1536]{1,0:T(8,128)(2,1)S(1)} %constant_dynamic-slice_fusion), channel_id=1, source_target_pairs={{0,3},{1,2},{2,1},{3,0},{4,7},{5,6},{6,5},{7,4},{8,11},{9,10},{10,... | collective-permute-start | bytes 442376 | tf_op jit(solution)/shard_map/ppermute | solution.py:15
  11.5 3.8 %collective-permute-done.18.refs_2_ = bf16[2,192,256]{2,1,0:T(8,128)(2,1)S(1)} collective-permute-done((bf16[2,192,256]{2,1,0:T(8,128)(2,1)S(1)}, bf16[2,192,256]{2,1,0:T(8,128)(2,1)S(1)}, u32[]{:S(2)}, u32[]{:S(2)}) %collective-permute-start.18) | collective-permute-done | bytes 196640 | tf_op jit(solution)/shard_map/ppermute | solution.py:15
  15.4 3.3 %collective-permute-done.2.refs_2_ = bf16[48,1536]{1,0:T(8,128)(2,1)S(1)} collective-permute-done((bf16[48,1536]{1,0:T(8,128)(2,1)S(1)}, bf16[48,1536]{1,0:T(8,128)(2,1)S(1)}, u32[]{:S(2)}, u32[]{:S(2)}) %collective-permute-start.2) | collective-permute-done | bytes 147488 | tf_op jit(solution)/shard_map/ppermute | solution.py:15
  21.5 2.4 %collective-permute-done.refs_0_ = bf16[48,1536]{1,0:T(8,128)(2,1)S(1)} collective-permute-done((bf16[48,1536]{1,0:T(8,128)(2,1)S(1)}, bf16[48,1536]{1,0:T(8,128)(2,1)S(1)}, u32[]{:S(2)}, u32[]{:S(2)}) %collective-permute-start) | collective-permute-done | bytes 147488 | tf_op jit(solution)/shard_map/ppermute | solution.py:15
  27.7 2.5 %collective-permute-start.21 = (bf16[1536,256]{1,0:T(8,128)(2,1)S(1)}, bf16[1536,256]{1,0:T(8,128)(2,1)S(1)}, u32[]{:S(2)}, u32[]{:S(2)}) collective-permute-start(bf16[1536,256]{1,0:T(8,128)(2,1)S(1)} %shard_map.95.raw), channel_id=1, source_target_pairs={{0,1},{1,0},{2,3},{3,2},{4,5},{5,4},{6,7},{7,6},{8,9},{9,8},{10,11... | collective-permute-start | bytes 2359304 | tf_op jit(solution)/shard_map/ppermute | solution.py:15
  30.2 7.7 %collective-permute-done.5.refs_4_ = bf16[3,48,1536]{2,1,0:T(8,128)(2,1)S(1)} collective-permute-done((bf16[3,48,1536]{2,1,0:T(8,128)(2,1)S(1)}, bf16[3,48,1536]{2,1,0:T(8,128)(2,1)S(1)}, u32[]{:S(2)}, u32[]{:S(2)}) %collective-permute-start.5) | collective-permute-done | bytes 442400 | tf_op jit(solution)/shard_map/ppermute | solution.py:15
  37.9 7.7 %collective-permute-done.4.refs_3_ = bf16[3,48,1536]{2,1,0:T(8,128)(2,1)S(1)} collective-permute-done((bf16[3,48,1536]{2,1,0:T(8,128)(2,1)S(1)}, bf16[3,48,1536]{2,1,0:T(8,128)(2,1)S(1)}, u32[]{:S(2)}, u32[]{:S(2)}) %collective-permute-start.4) | collective-permute-done | bytes 442400 | tf_op jit(solution)/shard_map/ppermute | solution.py:15
  49.0 2.2 %shard_map.96.a0 = bf16[1536,256]{1,0:T(8,128)(2,1)S(1)} custom-call(bf16[1536,1536]{1,0:T(8,128)(2,1)S(1)} %shard_map.87.square, bf16[1536,256]{1,0:T(8,128)(2,1)S(1)} %shard_map.95.raw), custom_call_target="tpu_custom_call" | custom-call | flops 1207959552 | bytes 1048576 | tf_op jit(solution)/shard_map/pallas_call | solution.py:31
  51.5 2.2 %shard_map.97.a1 = bf16[1536,256]{1,0:T(8,128)(2,1)S(1)} custom-call(bf16[1536,1536]{1,0:T(8,128)(2,1)S(1)} %shard_map.87.square, bf16[1536,256]{1,0:T(8,128)(2,1)S(1)} %collective-permute-done.21.raw), custom_call_target="tpu_custom_call" | custom-call | flops 1207959552 | bytes 1048576 | tf_op jit(solution)/shard_map/pallas_call | solution.py:31
  54.2 1.9 %collective-permute-start.15 = (f32[1]{0:T(128)}, f32[1]{0:T(128)}, u32[]{:S(2)}, u32[]{:S(2)}) collective-permute-start(f32[1]{0:T(128)} %param.10), channel_id=1, source_target_pairs={{0,0},{12,4},{8,8},{4,12},{16,16},{28,20},{24,24},{20,28},{1,1},{1... | collective-permute-start | bytes 20 | tf_op jit(solution)/shard_map/ppermute | solution.py:261
  56.9 2.1 %collective-permute-start.16 = (f32[1]{0:T(128)}, f32[1]{0:T(128)}, u32[]{:S(2)}, u32[]{:S(2)}) collective-permute-start(f32[1]{0:T(128)} %collective-permute-done.15.occ_a), channel_id=1, source_target_pairs={{0,4},{4,0},{8,12},{12,8},{16,20},{20,16},{24,28},{28,24},{1,5},{5... | collective-permute-start | bytes 20 | tf_op jit(solution)/shard_map/ppermute | solution.py:15
  59.0 2.3 %copy-done.1 = bf16[1536,1536]{1,0:T(8,128)(2,1)S(1)} copy-done((bf16[1536,1536]{1,0:T(8,128)(2,1)S(1)}, bf16[1536,1536]{1,0:T(8,128)(2,1)}, u32[]{:S(2)}) %copy-start.1) | copy-done | bytes 4718616
  61.4 2.2 %shard_map.91.beta.refs_0_ = bf16[1536,256]{1,0:T(8,128)(2,1)S(1)} custom-call(bf16[1536,1536]{1,0:T(8,128)(2,1)S(1)} %copy-done.1, bf16[1536,256]{1,0:T(8,128)(2,1)S(1)} %shard_map.90.raw), custom_call_target="tpu_custom_call" | custom-call | flops 1207959552 | bytes 1048576 | tf_op jit(solution)/shard_map/pallas_call | solution.py:31
  63.6 19.5 %collective-permute-done.14.raw = bf16[1536,256]{1,0:T(8,128)(2,1)S(1)} collective-permute-done((bf16[1536,256]{1,0:T(8,128)(2,1)S(1)}, bf16[1536,256]{1,0:T(8,128)(2,1)S(1)}, u32[]{:S(2)}, u32[]{:S(2)}) %collective-permute-start.14) | collective-permute-done | bytes 786464 | tf_op jit(solution)/shard_map/ppermute | solution.py:15
  83.1 2.2 %shard_map.92.beta.refs_1_ = bf16[1536,256]{1,0:T(8,128)(2,1)S(1)} custom-call(bf16[1536,1536]{1,0:T(8,128)(2,1)S(1)} %copy-done.1, bf16[1536,256]{1,0:T(8,128)(2,1)S(1)} %collective-permute-done.14.raw), custom_call_target="tpu_custom_call" | custom-call | flops 1207959552 | bytes 1048576 | tf_op jit(solution)/shard_map/pallas_call | solution.py:31
  85.4 5.6 %shard_map.99 = (bf16[4,256,256]{2,1,0:T(8,128)(2,1)S(1)}, bf16[1536,256]{1,0:T(8,128)(2,1)S(1)}) custom-call(f32[1]{0:T(128)} %collective-permute-done.15.occ_a, f32[1]{0:T(128)} %collective-permute-done.16.occ_o, f32[8]{0:T(128)S(1)} %copy-done.6, f32[4,256]{1,0:T(4,128)S(1)} %reshape.13.vir_a, f32[1,256]{1,0:T(1,128)S(1)} %bitcast.7, ...), custom_call_target="tpu_custom_call" | custom-call | flops 1610612736 | bytes 1048576 | tf_op jit(solution)/shard_map/pallas_call | solution.py:31
  91.0 5.6 %shard_map.98 = (bf16[4,256,256]{2,1,0:T(8,128)(2,1)S(1)}, f32[1536,256]{1,0:T(8,128)S(1)}) custom-call(f32[1]{0:T(128)} %collective-permute-done.15.occ_a, f32[1]{0:T(128)} %collective-permute-done.16.occ_o, f32[8]{0:T(128)S(1)} %copy-done.6, f32[4,256]{1,0:T(4,128)S(1)} %reshape.13.vir_a, f32[1,256]{1,0:T(1,128)S(1)} %bitcast.6, ...), custom_call_target="tpu_custom_call" | custom-call | flops 1610612736 | bytes 1048576 | tf_op jit(solution)/shard_map/pallas_call | solution.py:31
  96.6 1.8 %shard_map.101 = bf16[1536,512]{1,0:T(8,128)(2,1)S(1)} custom-call(bf16[1536,256]{1,0:T(8,128)(2,1)S(1)} %shard_map.91.beta.refs_0_, bf16[1536,256]{1,0:T(8,128)(2,1)S(1)} %shard_map.92.beta.refs_1_, bf16[4,256,256]{2,1,0:T(8,128)(2,1)S(1)} %get-tuple-element.26.refs_2_, bf16[4,256,256]{2,1,0:T(8,128)(2,1)S(1)} %get-tuple-element.27.refs_3_), custom_call_target="tpu_custom_call" | custom-call | flops 805306368 | bytes 1048576 | tf_op jit(solution)/shard_map/pallas_call | solution.py:31
  98.5 1.8 %shard_map.100.gamma_alpha = f32[1536,512]{1,0:T(8,128)S(1)} custom-call(bf16[1536,256]{1,0:T(8,128)(2,1)S(1)} %shard_map.91.beta.refs_0_, bf16[1536,256]{1,0:T(8,128)(2,1)S(1)} %shard_map.92.beta.refs_1_, bf16[4,256,256]{2,1,0:T(8,128)(2,1)S(1)} %get-tuple-element.26.refs_2_, bf16[4,256,256]{2,1,0:T(8,128)(2,1)S(1)} %get-tuple-element.27.refs_3_), custom_call_target="tpu_custom_call" | custom-call | flops 805306368 | bytes 1048576 | tf_op jit(solution)/shard_map/pallas_call | solution.py:31
  100.3 1.6 %collective-permute-done.25.from_core = bf16[1536,512]{1,0:T(8,128)(2,1)S(1)} collective-permute-done((bf16[1536,512]{1,0:T(8,128)(2,1)S(1)}, bf16[1536,512]{1,0:T(8,128)(2,1)S(1)}, u32[]{:S(2)}, u32[]{:S(2)}) %collective-permute-start.25) | collective-permute-done | bytes 1572896 | tf_op jit(solution)/shard_map/ppermute | solution.py:15
  103.4 20.6 %collective-permute-done.26 = bf16[1536,256]{1,0:T(8,128)(2,1)S(1)} collective-permute-done((bf16[1536,256]{1,0:T(8,128)(2,1)S(1)}, bf16[1536,256]{1,0:T(8,128)(2,1)S(1)}, u32[]{:S(2)}, u32[]{:S(2)}) %collective-permute-start.26) | collective-permute-done | bytes 786464 | tf_op jit(solution)/shard_map/ppermute | solution.py:295
  126.5 14.9 %collective-permute-done.27 = bf16[1536,256]{1,0:T(8,128)(2,1)} collective-permute-done((bf16[1536,256]{1,0:T(8,128)(2,1)}, bf16[1536,256]{1,0:T(8,128)(2,1)}, u32[]{:S(2)}, u32[]{:S(2)}) %collective-permute-start.27) | collective-permute-done | bytes 786464 | tf_op jit(solution)/shard_map/ppermute | solution.py:15
  141.4 2.6 %select_bitcast_fusion = (bf16[1536,1,256]{2,0,1:T(8,128)(2,1)}, bf16[1536,1,256]{2,0,1:T(8,128)(2,1)}) fusion(bf16[1536,256]{1,0:T(8,128)(2,1)} %collective-permute-done.27, pred[]{:T(512)S(6)} %eq.6, f32[1536,256]{1,0:T(8,128)S(1)} %get-tuple-element.32, bf16[1536,256]{1,0:T(8,128)(2,1)S(1)} %collective-permute-done.28), kind=kLoop, calls=%fused_computation.2 | loop fusion | flops 1966080 | bytes 4718593 | tf_op jit(solution)/shard_map/reshape | solution.py:302
  (71 shorter events, 23.4 us)
Async XLA Ops:
  2.2 7.8 %collective-permute-start.17 = (bf16[2,192,256]{2,1,0:T(8,128)(2,1)S(1)}, bf16[2,192,256]{2,1,0:T(8,128)(2,1)S(1)}, u32[]{:S(2)}, u32[]{:S(2)}) collective-permute-start(bf16[2,192,256]{2,1,0:T(8,128)(2,1)S(1)} %get-tuple-element.23), channel_id=1, source_target_pairs={{0,8},{4,12},{8,0},{12,4},{16,24},{20,28},{24,16},{28,20},{1,9},{5... | collective-permute-start | bytes 589832 | tf_op jit(solution)/shard_map/ppermute | solution.py:15
  3.7 11.6 %collective-permute-start.18 = (bf16[2,192,256]{2,1,0:T(8,128)(2,1)S(1)}, bf16[2,192,256]{2,1,0:T(8,128)(2,1)S(1)}, u32[]{:S(2)}, u32[]{:S(2)}) collective-permute-start(bf16[2,192,256]{2,1,0:T(8,128)(2,1)S(1)} %get-tuple-element.24), channel_id=1, source_target_pairs={{0,16},{4,20},{8,24},{12,28},{16,0},{20,4},{24,8},{28,12},{1,17},{... | collective-permute-start | bytes 589832 | tf_op jit(solution)/shard_map/ppermute | solution.py:15
  4.2 11.1 %collective-permute-start.19 = (bf16[2,192,256]{2,1,0:T(8,128)(2,1)S(1)}, bf16[2,192,256]{2,1,0:T(8,128)(2,1)S(1)}, u32[]{:S(2)}, u32[]{:S(2)}) collective-permute-start(bf16[2,192,256]{2,1,0:T(8,128)(2,1)S(1)} %get-tuple-element.25), channel_id=1, source_target_pairs={{0,24},{4,28},{8,16},{12,20},{16,8},{20,12},{24,0},{28,4},{1,25},{... | collective-permute-start | bytes 589832 | tf_op jit(solution)/shard_map/ppermute | solution.py:15
  6.7 12.1 %collective-permute-start.2 = (bf16[48,1536]{1,0:T(8,128)(2,1)S(1)}, bf16[48,1536]{1,0:T(8,128)(2,1)S(1)}, u32[]{:S(2)}, u32[]{:S(2)}) collective-permute-start(bf16[48,1536]{1,0:T(8,128)(2,1)S(1)} %constant_dynamic-slice_fusion), channel_id=1, source_target_pairs={{0,3},{1,2},{2,1},{3,0},{4,7},{5,6},{6,5},{7,4},{8,11},{9,10},{10,... | collective-permute-start | bytes 442376 | tf_op jit(solution)/shard_map/ppermute | solution.py:15
  8.3 11.8 %collective-permute-start.1 = (bf16[48,1536]{1,0:T(8,128)(2,1)S(1)}, bf16[48,1536]{1,0:T(8,128)(2,1)S(1)}, u32[]{:S(2)}, u32[]{:S(2)}) collective-permute-start(bf16[48,1536]{1,0:T(8,128)(2,1)S(1)} %constant_dynamic-slice_fusion), channel_id=1, source_target_pairs={{0,2},{1,3},{2,0},{3,1},{4,6},{5,7},{6,4},{7,5},{8,10},{9,11},{10,... | collective-permute-start | bytes 442376 | tf_op jit(solution)/shard_map/ppermute | solution.py:15
  10.0 15.4 %collective-permute-start.10 = (bf16[2,192,256]{2,1,0:T(8,128)(2,1)S(1)}, bf16[2,192,256]{2,1,0:T(8,128)(2,1)S(1)}, u32[]{:S(2)}, u32[]{:S(2)}) collective-permute-start(bf16[2,192,256]{2,1,0:T(8,128)(2,1)S(1)} %get-tuple-element.19), channel_id=1, source_target_pairs={{0,8},{4,12},{8,0},{12,4},{16,24},{20,28},{24,16},{28,20},{1,9},{5... | collective-permute-start | bytes 589832 | tf_op jit(solution)/shard_map/ppermute | solution.py:15
  15.3 11.6 %collective-permute-start.11 = (bf16[2,192,256]{2,1,0:T(8,128)(2,1)S(1)}, bf16[2,192,256]{2,1,0:T(8,128)(2,1)S(1)}, u32[]{:S(2)}, u32[]{:S(2)}) collective-permute-start(bf16[2,192,256]{2,1,0:T(8,128)(2,1)S(1)} %get-tuple-element.20), channel_id=1, source_target_pairs={{0,16},{4,20},{8,24},{12,28},{16,0},{20,4},{24,8},{28,12},{1,17},{... | collective-permute-start | bytes 589832 | tf_op jit(solution)/shard_map/ppermute | solution.py:15
  15.3 12.3 %collective-permute-start.20 = (bf16[4,192,256]{2,1,0:T(8,128)(2,1)S(1)}, bf16[4,192,256]{2,1,0:T(8,128)(2,1)S(1)}, u32[]{:S(2)}, u32[]{:S(2)}) collective-permute-start(bf16[4,192,256]{2,1,0:T(8,128)(2,1)S(1)} %shard_map.94), channel_id=1, source_target_pairs={{0,4},{4,0},{8,12},{12,8},{16,20},{20,16},{24,28},{28,24},{1,5},{5... | collective-permute-start | bytes 1179656 | tf_op jit(solution)/shard_map/ppermute | solution.py:15
  18.7 5.1 %collective-permute-start = (bf16[48,1536]{1,0:T(8,128)(2,1)S(1)}, bf16[48,1536]{1,0:T(8,128)(2,1)S(1)}, u32[]{:S(2)}, u32[]{:S(2)}) collective-permute-start(bf16[48,1536]{1,0:T(8,128)(2,1)S(1)} %constant_dynamic-slice_fusion), channel_id=1, source_target_pairs={{0,1},{1,0},{2,3},{3,2},{4,5},{5,4},{6,7},{7,6},{8,9},{9,8},{10,11... | collective-permute-start | bytes 442376 | tf_op jit(solution)/shard_map/ppermute | solution.py:15
  20.1 7.4 %collective-permute-start.12 = (bf16[2,192,256]{2,1,0:T(8,128)(2,1)S(1)}, bf16[2,192,256]{2,1,0:T(8,128)(2,1)S(1)}, u32[]{:S(2)}, u32[]{:S(2)}) collective-permute-start(bf16[2,192,256]{2,1,0:T(8,128)(2,1)S(1)} %get-tuple-element.21), channel_id=1, source_target_pairs={{0,24},{4,28},{8,16},{12,20},{16,8},{20,12},{24,0},{28,4},{1,25},{... | collective-permute-start | bytes 589832 | tf_op jit(solution)/shard_map/ppermute | solution.py:15
  23.9 14.0 %collective-permute-start.5 = (bf16[3,48,1536]{2,1,0:T(8,128)(2,1)S(1)}, bf16[3,48,1536]{2,1,0:T(8,128)(2,1)S(1)}, u32[]{:S(2)}, u32[]{:S(2)}) collective-permute-start(bf16[3,48,1536]{2,1,0:T(8,128)(2,1)S(1)} %shard_map.86.refs_1_), channel_id=1, source_target_pairs={{0,24},{4,28},{8,16},{12,20},{16,8},{20,12},{24,0},{28,4},{1,25},{... | collective-permute-start | bytes 1327112 | tf_op jit(solution)/shard_map/ppermute | solution.py:15
  25.4 20.2 %collective-permute-start.4 = (bf16[3,48,1536]{2,1,0:T(8,128)(2,1)S(1)}, bf16[3,48,1536]{2,1,0:T(8,128)(2,1)S(1)}, u32[]{:S(2)}, u32[]{:S(2)}) collective-permute-start(bf16[3,48,1536]{2,1,0:T(8,128)(2,1)S(1)} %shard_map.86.refs_1_), channel_id=1, source_target_pairs={{0,16},{4,20},{8,24},{12,28},{16,0},{20,4},{24,8},{28,12},{1,17},{... | collective-permute-start | bytes 1327112 | tf_op jit(solution)/shard_map/ppermute | solution.py:15
  26.9 18.7 %collective-permute-start.3 = (bf16[3,48,1536]{2,1,0:T(8,128)(2,1)S(1)}, bf16[3,48,1536]{2,1,0:T(8,128)(2,1)S(1)}, u32[]{:S(2)}, u32[]{:S(2)}) collective-permute-start(bf16[3,48,1536]{2,1,0:T(8,128)(2,1)S(1)} %shard_map.86.refs_1_), channel_id=1, source_target_pairs={{0,8},{4,12},{8,0},{12,4},{16,24},{20,28},{24,16},{28,20},{1,9},{5... | collective-permute-start | bytes 1327112 | tf_op jit(solution)/shard_map/ppermute | solution.py:15
  27.5 18.6 %collective-permute-start.13 = (bf16[4,192,256]{2,1,0:T(8,128)(2,1)S(1)}, bf16[4,192,256]{2,1,0:T(8,128)(2,1)S(1)}, u32[]{:S(2)}, u32[]{:S(2)}) collective-permute-start(bf16[4,192,256]{2,1,0:T(8,128)(2,1)S(1)} %shard_map.89), channel_id=1, source_target_pairs={{0,4},{4,0},{8,12},{12,8},{16,20},{20,16},{24,28},{28,24},{1,5},{5... | collective-permute-start | bytes 1179656 | tf_op jit(solution)/shard_map/ppermute | solution.py:15
  27.7 23.8 %collective-permute-start.21 = (bf16[1536,256]{1,0:T(8,128)(2,1)S(1)}, bf16[1536,256]{1,0:T(8,128)(2,1)S(1)}, u32[]{:S(2)}, u32[]{:S(2)}) collective-permute-start(bf16[1536,256]{1,0:T(8,128)(2,1)S(1)} %shard_map.95.raw), channel_id=1, source_target_pairs={{0,1},{1,0},{2,3},{3,2},{4,5},{5,4},{6,7},{7,6},{8,9},{9,8},{10,11... | collective-permute-start | bytes 2359304 | tf_op jit(solution)/shard_map/ppermute | solution.py:15
  37.9 8.4 %collective-permute-start.6 = (bf16[3,48,1536]{2,1,0:T(8,128)(2,1)S(1)}, bf16[3,48,1536]{2,1,0:T(8,128)(2,1)S(1)}, u32[]{:S(2)}, u32[]{:S(2)}) collective-permute-start(bf16[3,48,1536]{2,1,0:T(8,128)(2,1)S(1)} %shard_map.86.refs_1_), channel_id=1, source_target_pairs={{0,4},{4,0},{8,12},{12,8},{16,20},{20,16},{24,28},{28,24},{1,5},{5... | collective-permute-start | bytes 1327112 | tf_op jit(solution)/shard_map/ppermute | solution.py:15
  46.3 36.8 %collective-permute-start.14 = (bf16[1536,256]{1,0:T(8,128)(2,1)S(1)}, bf16[1536,256]{1,0:T(8,128)(2,1)S(1)}, u32[]{:S(2)}, u32[]{:S(2)}) collective-permute-start(bf16[1536,256]{1,0:T(8,128)(2,1)S(1)} %shard_map.90.raw), channel_id=1, source_target_pairs={{0,3},{1,2},{2,1},{3,0},{4,7},{5,6},{6,5},{7,4},{8,11},{9,10},{10,... | collective-permute-start | bytes 2359304 | tf_op jit(solution)/shard_map/ppermute | solution.py:15
  51.3 34.1 %collective-permute-start.22 = (bf16[1536,256]{1,0:T(8,128)(2,1)S(1)}, bf16[1536,256]{1,0:T(8,128)(2,1)}, u32[]{:S(2)}, u32[]{:S(2)}) collective-permute-start(bf16[1536,256]{1,0:T(8,128)(2,1)S(1)} %shard_map.96.a0), channel_id=1, source_target_pairs={{0,4},{4,0},{8,12},{12,8},{16,20},{20,16},{24,28},{28,24},{1,5},{5... | collective-permute-start | bytes 2359304 | tf_op jit(solution)/shard_map/ppermute | solution.py:15
  53.7 31.7 %collective-permute-start.23 = (bf16[1536,256]{1,0:T(8,128)(2,1)S(1)}, bf16[1536,256]{1,0:T(8,128)(2,1)}, u32[]{:S(2)}, u32[]{:S(2)}) collective-permute-start(bf16[1536,256]{1,0:T(8,128)(2,1)S(1)} %shard_map.97.a1), channel_id=1, source_target_pairs={{0,4},{4,0},{8,12},{12,8},{16,20},{20,16},{24,28},{28,24},{1,5},{5... | collective-permute-start | bytes 2359304 | tf_op jit(solution)/shard_map/ppermute | solution.py:15
  56.0 29.3 %collective-permute-start.24 = (f32[256]{0:T(256)S(1)}, f32[256]{0:T(256)S(1)}, u32[]{:S(2)}, u32[]{:S(2)}) collective-permute-start(f32[256]{0:T(256)S(1)} %copy-done.5), channel_id=1, source_target_pairs={{0,3},{1,2},{2,1},{3,0},{4,7},{5,6},{6,5},{7,4},{8,11},{9,10},{10,... | collective-permute-start | bytes 3080 | tf_op jit(solution)/shard_map/ppermute | solution.py:15
  56.9 28.5 %collective-permute-start.16 = (f32[1]{0:T(128)}, f32[1]{0:T(128)}, u32[]{:S(2)}, u32[]{:S(2)}) collective-permute-start(f32[1]{0:T(128)} %collective-permute-done.15.occ_a), channel_id=1, source_target_pairs={{0,4},{4,0},{8,12},{12,8},{16,20},{20,16},{24,28},{28,24},{1,5},{5... | collective-permute-start | bytes 20 | tf_op jit(solution)/shard_map/ppermute | solution.py:15
  102.5 21.5 %collective-permute-start.26 = (bf16[1536,256]{1,0:T(8,128)(2,1)S(1)}, bf16[1536,256]{1,0:T(8,128)(2,1)S(1)}, u32[]{:S(2)}, u32[]{:S(2)}) collective-permute-start(bf16[1536,256]{1,0:T(8,128)(2,1)S(1)} %get-tuple-element.31), channel_id=1, source_target_pairs={{0,3},{1,2},{2,1},{3,0},{4,5},{5,4},{6,7},{7,6},{8,11},{9,10},{10,... | collective-permute-start | bytes 2359304 | tf_op jit(solution)/shard_map/ppermute | solution.py:295
  103.4 23.2 %collective-permute-start.28 = (bf16[1536,256]{1,0:T(8,128)(2,1)S(1)}, bf16[1536,256]{1,0:T(8,128)(2,1)S(1)}, u32[]{:S(2)}, u32[]{:S(2)}) collective-permute-start(bf16[1536,256]{1,0:T(8,128)(2,1)S(1)} %get-tuple-element.33), channel_id=1, source_target_pairs={{0,1},{1,0},{2,3},{3,2},{4,7},{5,6},{6,5},{7,4},{8,9},{9,8},{10,11... | collective-permute-start | bytes 2359304 | tf_op jit(solution)/shard_map/ppermute | solution.py:295
  125.1 16.3 %collective-permute-start.27 = (bf16[1536,256]{1,0:T(8,128)(2,1)}, bf16[1536,256]{1,0:T(8,128)(2,1)}, u32[]{:S(2)}, u32[]{:S(2)}) collective-permute-start(bf16[1536,256]{1,0:T(8,128)(2,1)} %add_convert_fusion.1), channel_id=1, source_target_pairs={{0,8},{4,12},{8,0},{12,4},{16,24},{20,28},{24,16},{28,20},{1,9},{5... | collective-permute-start | bytes 2359304 | tf_op jit(solution)/shard_map/ppermute | solution.py:15
  (13 other events, 80.1 us)
where the time goes:
time: 144 us
  waiting for transfers between devices  84.3 us (59%)
  Pallas kernels  25.7 us (18%)
  starting transfers between devices  25 us (17%)
  local copies, waits for them, and re-layouts  4.42 us (3%)
  other arithmetic  3.69 us (3%)
    ppermute x26, waiting for transfers between devices, swap(): return lax.ppermute(value, axis, pairs)  63.7 us
    pallas_call x17, Pallas kernels, call(): pl.pallas_call(kernel, out_shape=shapes, in_specs=specs or [VMEM] * len(a...  25.7 us
    ppermute x26, starting transfers between devices, swap(): return lax.ppermute(value, axis, pairs)  22.2 us
    ppermute x2, waiting for transfers between devices, back(): got = lax.ppermute(send, ('occ', 'vir'), pairs)  20.6 us
    unnamed x16, local copies, waits for them, and re-layouts  3.5 us
  transfers between devices with their start and end apart: 29, of which 14 were waited for; matrix products, arithmetic and copies ran while one was open for 1% of the time, Pallas kernels for 8%

commit v1 on v0

--- a/solution.py
+++ b/solution.py
@@ -37,7 +37,7 @@
         cost_estimate=pl.CostEstimate(
             flops=flops, bytes_accessed=1 << 20, transcendentals=0
         ),
-        compiler_params=pltpu.CompilerParams(vmem_limit_bytes=20 << 20),
+        compiler_params=pltpu.CompilerParams(vmem_limit_bytes=16 << 20),
     )(*args)
 
 
@@ -121,47 +121,55 @@
     return jnp.concatenate([lax.select_n(layer ^ k, *pieces) for k in range(4)], axis=0)
 
 
-def place_metric(chips, *refs):
-    own, mine, other, out = refs[0], refs[1 : 1 + chips], refs[1 + chips : 1 + 2 * chips], refs[-1]
+def pack_metric(*refs):
+    for k, ref in enumerate(refs[:-1]):
+        refs[-1][k] = ref[...]
+
+
+def cut_metric(by_x, by_y, via_x, via_y):
+    half = via_x.shape[2]
+    via_x[...] = by_y[:, :, :half]
+    via_y[...] = by_x[:, :, half:]
+
+
+def place_metric(own, *refs):
+    refs, out = refs[:-1], refs[-1]
+    mine, other = refs[: len(refs) // 2], refs[len(refs) // 2 :]
     rows = own.shape[0]
-    part = mine[0].shape[1]
+    part, half = mine[0].shape[1], mine[-1].shape[2]
     me, layer = lax.axis_index("occ"), lax.axis_index("vir")
     chip, core = me // 2, me % 2
     out[at(layer * rows, rows), :] = own[...]
     for k in (1, 2, 3):
-        for m in range(chips):
-            for c, held in ((core, mine), (1 - core, other)):
-                start = (layer ^ k) * rows + (2 * (chip ^ m) + c) * part
-                out[at(start, part), :] = held[m][k - 1]
+        for c, held in ((core, mine), (1 - core, other)):
+            start = lambda m: (layer ^ k) * rows + (2 * (chip ^ m) + c) * part
+            for m in (0, 1, 2):
+                out[at(start(m), part), :] = held[m][k - 1]
+            out[at(start(3), part), :half] = held[3][k - 1]
+            out[at(start(3), part), half:] = held[4][k - 1]
 
 
 def whole_metric(metric):
     rows, aux = metric.shape
     blocks = lax.axis_size("occ")
-    chips = blocks // 2
-    if chips > 4 or rows % (16 * blocks):
+    if blocks != 8 or rows % (16 * blocks) or aux % 256:
         return halves_metric(metric)
     part = rows // blocks
     mine = lax.dynamic_slice_in_dim(metric, lax.axis_index("occ") * part, part, 0)
     got = [swap(mine, "vir", k) for k in (1, 2, 3)]
-
-    def pack(*refs):
-        for k in range(3):
-            refs[-1][k] = refs[k][...]
-
-    got = call(pack, shape_of(3, part, aux), *got)
-    plane = [got] + [swap(got, "occ", 2 * m) for m in range(1, chips)]
+    got = call(pack_metric, shape_of(3, part, aux), *got)
+    by_x, by_y = swap(got, "occ", 2), swap(got, "occ", 4)
+    halves = call(cut_metric, [shape_of(3, part, aux // 2)] * 2, by_x, by_y)
+    via_x, via_y = swap(halves[0], "occ", 2), swap(halves[1], "occ", 4)
+    plane = [got, by_x, by_y, via_x, via_y]
     other = [swap(p, "occ", 1) for p in plane]
-    place = lambda *refs: place_metric(chips, *refs)
-    return call(place, shape_of(aux, aux), metric, *plane, *other)
-
-
-def row_chunks(rows, body, step=256):
-    def one(i, carry):
-        body(at(i * step, step))
-        return carry
-
-    lax.fori_loop(0, rows // step, one, 0)
+    return call(place_metric, shape_of(aux, aux), metric, *plane, *other)
+
+
+def row_chunks(rows, body, step=512):
+    step = step if rows % step == 0 else rows
+    for start in range(0, rows, step):
+        body(slice(start, start + step))
 
 
 def fit_rows(square, raw, out):
@@ -184,7 +192,7 @@
     right = occ_b[beta_of(me)] - vir_b[...]
     right = jnp.broadcast_to(right, (128, unit)).T[:, :1]
     for u, alpha in enumerate(alphas):
-        row = vir_a[pl.ds(layer ^ (u % 2), 1), :]
+        row = vir_a[at((layer ^ (u % 2)) * unit, unit)].reshape(1, unit)
         left = (occ_a, occ_a, occ_o, occ_o)[u][0] - row
         pair = dots(flip[...], alpha[...], 1, 0)
         amp[u] = (pair / (left + right)).astype(BF16)
@@ -259,9 +267,9 @@
     raw_alpha = regroup(ints_alpha, alpha_of)
 
     occ_mine = lax.ppermute(e_occ_alpha, "occ", [(alpha_of(d), d) for d in range(blocks)])
+    vir_near = swap(e_vir_beta, "vir", 3)
     occ_other = swap(occ_mine, "occ", 1)
-    vir_near = swap(e_vir_beta, "vir", 3)
-    common = [occ_mine, occ_other, e_occ_beta, e_vir_alpha.reshape(layers, unit)]
+    common = [occ_mine, occ_other, e_occ_beta, e_vir_alpha]
 
     near_beta = swap(raw_beta, "vir", 3)
     near_alpha = swap(raw_alpha, "vir", 1)

time: 144 us -> 139 us (0.965)
  Pallas kernels: 25.7 us -> 17.1 us
  waiting for transfers between devices: 84.3 us -> 89.6 us
  local copies, waits for them, and re-layouts: 4.42 us -> 2.07 us
    pallas_call x17 -> x18, Pallas kernels: 25.7 us -> 17.1 us  [call(): pl.pallas_call(kernel, out_shape=shapes, in_specs=specs or [VMEM] * len(a...]
    ppermute x26 -> x28, waiting for transfers between devices: 63.7 us -> 68.7 us  [swap(): return lax.ppermute(value, axis, pairs)]
    unnamed x16 -> x12, local copies, waits for them, and re-layouts: 3.5 us -> 1.16 us
    ppermute x26 -> x28, starting transfers between devices: 22.2 us -> 22.3 us  [swap(): return lax.ppermute(value, axis, pairs)]
  transfers between devices with their start and end apart: 29 -> 31, of which waited for: 14 -> 14; matrix products, arithmetic and copies ran while one was open for 1% -> 1% of each run, Pallas kernels for 8% -> 5%
where the time goes in v1:
time: 139 us; the launch traced here: 138 us
  waiting for transfers between devices  89.6 us (64%)
  starting transfers between devices  24.9 us (18%)
  Pallas kernels  17.1 us (12%)
  other arithmetic  3.64 us (3%)
  local copies, waits for them, and re-layouts  2.07 us (1%)
    ppermute x28, waiting for transfers between devices, swap(): return lax.ppermute(value, axis, pairs)  68.7 us
    ppermute x28, starting transfers between devices, swap(): return lax.ppermute(value, axis, pairs)  22.3 us
    ppermute x2, waiting for transfers between devices, back(): got = lax.ppermute(send, ('occ', 'vir'), pairs)  20.9 us
    pallas_call x18, Pallas kernels, call(): pl.pallas_call(kernel, out_shape=shapes, in_specs=specs or [VMEM] * len(a...  17.1 us
  transfers between devices with their start and end apart: 31, of which 14 were waited for; matrix products, arithmetic and copies ran while one was open for 1% of the time, Pallas kernels for 5%

profile of v1, /device:TPU:12, one launch (start us, length us, event | category | flops | bytes accessed | tf_op | source)
XLA Modules:
  0.0 138.3 jit_solution(18438910469547472536)
XLA Ops:
  2.2 1.6 %collective-permute-start.19 = (bf16[2,192,256]{2,1,0:T(8,128)(2,1)S(1)}, bf16[2,192,256]{2,1,0:T(8,128)(2,1)S(1)}, u32[]{:S(2)}, u32[]{:S(2)}) collective-permute-start(bf16[2,192,256]{2,1,0:T(8,128)(2,1)S(1)} %get-tuple-element.27), channel_id=1, source_target_pairs={{0,8},{4,12},{8,0},{12,4},{16,24},{20,28},{24,16},{28,20},{1,9},{5... | collective-permute-start | bytes 589832 | tf_op jit(solution)/shard_map/ppermute | solution.py:15
  4.2 1.5 %collective-permute-start.21 = (bf16[2,192,256]{2,1,0:T(8,128)(2,1)S(1)}, bf16[2,192,256]{2,1,0:T(8,128)(2,1)S(1)}, u32[]{:S(2)}, u32[]{:S(2)}) collective-permute-start(bf16[2,192,256]{2,1,0:T(8,128)(2,1)S(1)} %get-tuple-element.29), channel_id=1, source_target_pairs={{0,24},{4,28},{8,16},{12,20},{16,8},{20,12},{24,0},{28,4},{1,25},{... | collective-permute-start | bytes 589832 | tf_op jit(solution)/shard_map/ppermute | solution.py:15
  6.7 1.6 %collective-permute-start.2 = (bf16[48,1536]{1,0:T(8,128)(2,1)S(1)}, bf16[48,1536]{1,0:T(8,128)(2,1)S(1)}, u32[]{:S(2)}, u32[]{:S(2)}) collective-permute-start(bf16[48,1536]{1,0:T(8,128)(2,1)S(1)} %constant_dynamic-slice_fusion), channel_id=1, source_target_pairs={{0,3},{1,2},{2,1},{3,0},{4,7},{5,6},{6,5},{7,4},{8,11},{9,10},{10,... | collective-permute-start | bytes 442376 | tf_op jit(solution)/shard_map/ppermute | solution.py:15
  10.0 1.5 %collective-permute-start.12 = (bf16[2,192,256]{2,1,0:T(8,128)(2,1)S(1)}, bf16[2,192,256]{2,1,0:T(8,128)(2,1)S(1)}, u32[]{:S(2)}, u32[]{:S(2)}) collective-permute-start(bf16[2,192,256]{2,1,0:T(8,128)(2,1)S(1)} %get-tuple-element.23), channel_id=1, source_target_pairs={{0,8},{4,12},{8,0},{12,4},{16,24},{20,28},{24,16},{28,20},{1,9},{5... | collective-permute-start | bytes 589832 | tf_op jit(solution)/shard_map/ppermute | solution.py:15
  11.5 3.8 %collective-permute-done.20.refs_2_ = bf16[2,192,256]{2,1,0:T(8,128)(2,1)S(1)} collective-permute-done((bf16[2,192,256]{2,1,0:T(8,128)(2,1)S(1)}, bf16[2,192,256]{2,1,0:T(8,128)(2,1)S(1)}, u32[]{:S(2)}, u32[]{:S(2)}) %collective-permute-start.20) | collective-permute-done | bytes 196640 | tf_op jit(solution)/shard_map/ppermute | solution.py:15
  15.4 3.3 %collective-permute-done.2.refs_2_ = bf16[48,1536]{1,0:T(8,128)(2,1)S(1)} collective-permute-done((bf16[48,1536]{1,0:T(8,128)(2,1)S(1)}, bf16[48,1536]{1,0:T(8,128)(2,1)S(1)}, u32[]{:S(2)}, u32[]{:S(2)}) %collective-permute-start.2) | collective-permute-done | bytes 147488 | tf_op jit(solution)/shard_map/ppermute | solution.py:15
  20.1 1.4 %collective-permute-start.14 = (bf16[2,192,256]{2,1,0:T(8,128)(2,1)S(1)}, bf16[2,192,256]{2,1,0:T(8,128)(2,1)S(1)}, u32[]{:S(2)}, u32[]{:S(2)}) collective-permute-start(bf16[2,192,256]{2,1,0:T(8,128)(2,1)S(1)} %get-tuple-element.25), channel_id=1, source_target_pairs={{0,24},{4,28},{8,16},{12,20},{16,8},{20,12},{24,0},{28,4},{1,25},{... | collective-permute-start | bytes 589832 | tf_op jit(solution)/shard_map/ppermute | solution.py:15
  21.5 2.4 %collective-permute-done.refs_0_ = bf16[48,1536]{1,0:T(8,128)(2,1)S(1)} collective-permute-done((bf16[48,1536]{1,0:T(8,128)(2,1)S(1)}, bf16[48,1536]{1,0:T(8,128)(2,1)S(1)}, u32[]{:S(2)}, u32[]{:S(2)}) %collective-permute-start) | collective-permute-done | bytes 147488 | tf_op jit(solution)/shard_map/ppermute | solution.py:15
  24.5 1.5 %collective-permute-start.3 = (bf16[3,48,1536]{2,1,0:T(8,128)(2,1)S(1)}, bf16[3,48,1536]{2,1,0:T(8,128)(2,1)S(1)}, u32[]{:S(2)}, u32[]{:S(2)}) collective-permute-start(bf16[3,48,1536]{2,1,0:T(8,128)(2,1)S(1)} %shard_map.86.refs_0_), channel_id=1, source_target_pairs={{0,8},{4,12},{8,0},{12,4},{16,24},{20,28},{24,16},{28,20},{1,9},{5... | collective-permute-start | bytes 1327112 | tf_op jit(solution)/shard_map/ppermute | solution.py:15
  27.0 2.9 %collective-permute-start.23 = (bf16[1536,256]{1,0:T(8,128)(2,1)S(1)}, bf16[1536,256]{1,0:T(8,128)(2,1)S(1)}, u32[]{:S(2)}, u32[]{:S(2)}) collective-permute-start(bf16[1536,256]{1,0:T(8,128)(2,1)S(1)} %shard_map.96.raw), channel_id=1, source_target_pairs={{0,1},{1,0},{2,3},{3,2},{4,5},{5,4},{6,7},{7,6},{8,9},{9,8},{10,11... | collective-permute-start | bytes 2359304 | tf_op jit(solution)/shard_map/ppermute | solution.py:15
  29.9 6.3 %collective-permute-done.4.by_y.refs_2_ = bf16[3,48,1536]{2,1,0:T(8,128)(2,1)S(1)} collective-permute-done((bf16[3,48,1536]{2,1,0:T(8,128)(2,1)S(1)}, bf16[3,48,1536]{2,1,0:T(8,128)(2,1)S(1)}, u32[]{:S(2)}, u32[]{:S(2)}) %collective-permute-start.4) | collective-permute-done | bytes 442400 | tf_op jit(solution)/shard_map/ppermute | solution.py:15
  36.2 1.6 %collective-permute-start.5 = (bf16[3,48,768]{2,1,0:T(8,128)(2,1)S(1)}, bf16[3,48,768]{2,1,0:T(8,128)(2,1)S(1)}, u32[]{:S(2)}, u32[]{:S(2)}) collective-permute-start(bf16[3,48,768]{2,1,0:T(8,128)(2,1)S(1)} %get-tuple-element.20), channel_id=1, source_target_pairs={{0,8},{4,12},{8,0},{12,4},{16,24},{20,28},{24,16},{28,20},{1,9},{5... | collective-permute-start | bytes 663560 | tf_op jit(solution)/shard_map/ppermute | solution.py:15
  38.5 4.3 %collective-permute-done.5.refs_3_ = bf16[3,48,768]{2,1,0:T(8,128)(2,1)S(1)} collective-permute-done((bf16[3,48,768]{2,1,0:T(8,128)(2,1)S(1)}, bf16[3,48,768]{2,1,0:T(8,128)(2,1)S(1)}, u32[]{:S(2)}, u32[]{:S(2)}) %collective-permute-start.5) | collective-permute-done | bytes 221216 | tf_op jit(solution)/shard_map/ppermute | solution.py:15
  42.8 2.8 %collective-permute-done.6.refs_4_ = bf16[3,48,768]{2,1,0:T(8,128)(2,1)S(1)} collective-permute-done((bf16[3,48,768]{2,1,0:T(8,128)(2,1)S(1)}, bf16[3,48,768]{2,1,0:T(8,128)(2,1)S(1)}, u32[]{:S(2)}, u32[]{:S(2)}) %collective-permute-start.6) | collective-permute-done | bytes 221216 | tf_op jit(solution)/shard_map/ppermute | solution.py:15
  47.4 1.4 %shard_map.97.a0 = bf16[1536,256]{1,0:T(8,128)(2,1)S(1)} custom-call(bf16[1536,1536]{1,0:T(8,128)(2,1)S(1)} %shard_map.88.square, bf16[1536,256]{1,0:T(8,128)(2,1)S(1)} %shard_map.96.raw), custom_call_target="tpu_custom_call" | custom-call | flops 1207959552 | bytes 1048576 | tf_op jit(solution)/shard_map/pallas_call | solution.py:31
  50.8 1.8 %collective-permute-start.17 = (f32[1]{0:T(128)}, f32[1]{0:T(128)}, u32[]{:S(2)}, u32[]{:S(2)}) collective-permute-start(f32[1]{0:T(128)} %param.10), channel_id=1, source_target_pairs={{0,0},{12,4},{8,8},{4,12},{16,16},{28,20},{24,24},{20,28},{1,1},{1... | collective-permute-start | bytes 20 | tf_op jit(solution)/shard_map/ppermute | solution.py:269
  53.6 2.7 %collective-permute-start.18 = (f32[1]{0:T(128)}, f32[1]{0:T(128)}, u32[]{:S(2)}, u32[]{:S(2)}) collective-permute-start(f32[1]{0:T(128)} %collective-permute-done.17.occ_a), channel_id=1, source_target_pairs={{0,4},{4,0},{8,12},{12,8},{16,20},{20,16},{24,28},{28,24},{1,5},{5... | collective-permute-start | bytes 20 | tf_op jit(solution)/shard_map/ppermute | solution.py:15
  57.7 24.9 %collective-permute-done.16.raw = bf16[1536,256]{1,0:T(8,128)(2,1)S(1)} collective-permute-done((bf16[1536,256]{1,0:T(8,128)(2,1)S(1)}, bf16[1536,256]{1,0:T(8,128)(2,1)S(1)}, u32[]{:S(2)}, u32[]{:S(2)}) %collective-permute-start.16) | collective-permute-done | bytes 786464 | tf_op jit(solution)/shard_map/ppermute | solution.py:15
  84.0 3.7 %shard_map.100 = (bf16[4,256,256]{2,1,0:T(8,128)(2,1)S(1)}, bf16[1536,256]{1,0:T(8,128)(2,1)S(1)}) custom-call(f32[1]{0:T(128)} %collective-permute-done.17.occ_a, f32[1]{0:T(128)} %collective-permute-done.18.occ_o, f32[8]{0:T(128)S(1)} %copy-done.5, f32[1024]{0:T(1024)S(1)} %copy-done.3, f32[1,256]{1,0:T(1,128)S(1)} %bitcast.7, ...), custom_call_target="tpu_custom_call" | custom-call | flops 1610612736 | bytes 1048576 | tf_op jit(solution)/shard_map/pallas_call | solution.py:31
  87.8 3.7 %shard_map.99 = (bf16[4,256,256]{2,1,0:T(8,128)(2,1)S(1)}, f32[1536,256]{1,0:T(8,128)S(1)}) custom-call(f32[1]{0:T(128)} %collective-permute-done.17.occ_a, f32[1]{0:T(128)} %collective-permute-done.18.occ_o, f32[8]{0:T(128)S(1)} %copy-done.5, f32[1024]{0:T(1024)S(1)} %copy-done.3, f32[1,256]{1,0:T(1,128)S(1)} %bitcast.6, ...), custom_call_target="tpu_custom_call" | custom-call | flops 1610612736 | bytes 1048576 | tf_op jit(solution)/shard_map/pallas_call | solution.py:31
  93.6 2.4 %collective-permute-done.27.from_core = bf16[1536,512]{1,0:T(8,128)(2,1)S(1)} collective-permute-done((bf16[1536,512]{1,0:T(8,128)(2,1)S(1)}, bf16[1536,512]{1,0:T(8,128)(2,1)S(1)}, u32[]{:S(2)}, u32[]{:S(2)}) %collective-permute-start.27) | collective-permute-done | bytes 1572896 | tf_op jit(solution)/shard_map/ppermute | solution.py:15
  97.5 20.9 %collective-permute-done.28 = bf16[1536,256]{1,0:T(8,128)(2,1)S(1)} collective-permute-done((bf16[1536,256]{1,0:T(8,128)(2,1)S(1)}, bf16[1536,256]{1,0:T(8,128)(2,1)S(1)}, u32[]{:S(2)}, u32[]{:S(2)}) %collective-permute-start.28) | collective-permute-done | bytes 786464 | tf_op jit(solution)/shard_map/ppermute | solution.py:303
  119.8 15.9 %collective-permute-done.29 = bf16[1536,256]{1,0:T(8,128)(2,1)} collective-permute-done((bf16[1536,256]{1,0:T(8,128)(2,1)}, bf16[1536,256]{1,0:T(8,128)(2,1)}, u32[]{:S(2)}, u32[]{:S(2)}) %collective-permute-start.29) | collective-permute-done | bytes 786464 | tf_op jit(solution)/shard_map/ppermute | solution.py:15
  135.7 2.6 %select_bitcast_fusion = (bf16[1536,1,256]{2,0,1:T(8,128)(2,1)}, bf16[1536,1,256]{2,0,1:T(8,128)(2,1)}) fusion(bf16[1536,256]{1,0:T(8,128)(2,1)} %collective-permute-done.29, pred[]{:T(512)S(6)} %eq.6, f32[1536,256]{1,0:T(8,128)S(1)} %get-tuple-element.36, bf16[1536,256]{1,0:T(8,128)(2,1)S(1)} %collective-permute-done.30), kind=kLoop, calls=%fused_computation.2 | loop fusion | flops 1966080 | bytes 4718593 | tf_op jit(solution)/shard_map/reshape | solution.py:310
  (71 shorter events, 21.0 us)
Async XLA Ops:
  2.2 7.8 %collective-permute-start.19 = (bf16[2,192,256]{2,1,0:T(8,128)(2,1)S(1)}, bf16[2,192,256]{2,1,0:T(8,128)(2,1)S(1)}, u32[]{:S(2)}, u32[]{:S(2)}) collective-permute-start(bf16[2,192,256]{2,1,0:T(8,128)(2,1)S(1)} %get-tuple-element.27), channel_id=1, source_target_pairs={{0,8},{4,12},{8,0},{12,4},{16,24},{20,28},{24,16},{28,20},{1,9},{5... | collective-permute-start | bytes 589832 | tf_op jit(solution)/shard_map/ppermute | solution.py:15
  3.7 11.6 %collective-permute-start.20 = (bf16[2,192,256]{2,1,0:T(8,128)(2,1)S(1)}, bf16[2,192,256]{2,1,0:T(8,128)(2,1)S(1)}, u32[]{:S(2)}, u32[]{:S(2)}) collective-permute-start(bf16[2,192,256]{2,1,0:T(8,128)(2,1)S(1)} %get-tuple-element.28), channel_id=1, source_target_pairs={{0,16},{4,20},{8,24},{12,28},{16,0},{20,4},{24,8},{28,12},{1,17},{... | collective-permute-start | bytes 589832 | tf_op jit(solution)/shard_map/ppermute | solution.py:15
  4.2 11.1 %collective-permute-start.21 = (bf16[2,192,256]{2,1,0:T(8,128)(2,1)S(1)}, bf16[2,192,256]{2,1,0:T(8,128)(2,1)S(1)}, u32[]{:S(2)}, u32[]{:S(2)}) collective-permute-start(bf16[2,192,256]{2,1,0:T(8,128)(2,1)S(1)} %get-tuple-element.29), channel_id=1, source_target_pairs={{0,24},{4,28},{8,16},{12,20},{16,8},{20,12},{24,0},{28,4},{1,25},{... | collective-permute-start | bytes 589832 | tf_op jit(solution)/shard_map/ppermute | solution.py:15
  6.7 12.1 %collective-permute-start.2 = (bf16[48,1536]{1,0:T(8,128)(2,1)S(1)}, bf16[48,1536]{1,0:T(8,128)(2,1)S(1)}, u32[]{:S(2)}, u32[]{:S(2)}) collective-permute-start(bf16[48,1536]{1,0:T(8,128)(2,1)S(1)} %constant_dynamic-slice_fusion), channel_id=1, source_target_pairs={{0,3},{1,2},{2,1},{3,0},{4,7},{5,6},{6,5},{7,4},{8,11},{9,10},{10,... | collective-permute-start | bytes 442376 | tf_op jit(solution)/shard_map/ppermute | solution.py:15
  8.3 11.8 %collective-permute-start.1 = (bf16[48,1536]{1,0:T(8,128)(2,1)S(1)}, bf16[48,1536]{1,0:T(8,128)(2,1)S(1)}, u32[]{:S(2)}, u32[]{:S(2)}) collective-permute-start(bf16[48,1536]{1,0:T(8,128)(2,1)S(1)} %constant_dynamic-slice_fusion), channel_id=1, source_target_pairs={{0,2},{1,3},{2,0},{3,1},{4,6},{5,7},{6,4},{7,5},{8,10},{9,11},{10,... | collective-permute-start | bytes 442376 | tf_op jit(solution)/shard_map/ppermute | solution.py:15
  10.0 14.5 %collective-permute-start.12 = (bf16[2,192,256]{2,1,0:T(8,128)(2,1)S(1)}, bf16[2,192,256]{2,1,0:T(8,128)(2,1)S(1)}, u32[]{:S(2)}, u32[]{:S(2)}) collective-permute-start(bf16[2,192,256]{2,1,0:T(8,128)(2,1)S(1)} %get-tuple-element.23), channel_id=1, source_target_pairs={{0,8},{4,12},{8,0},{12,4},{16,24},{20,28},{24,16},{28,20},{1,9},{5... | collective-permute-start | bytes 589832 | tf_op jit(solution)/shard_map/ppermute | solution.py:15
  15.3 10.7 %collective-permute-start.13 = (bf16[2,192,256]{2,1,0:T(8,128)(2,1)S(1)}, bf16[2,192,256]{2,1,0:T(8,128)(2,1)S(1)}, u32[]{:S(2)}, u32[]{:S(2)}) collective-permute-start(bf16[2,192,256]{2,1,0:T(8,128)(2,1)S(1)} %get-tuple-element.24), channel_id=1, source_target_pairs={{0,16},{4,20},{8,24},{12,28},{16,0},{20,4},{24,8},{28,12},{1,17},{... | collective-permute-start | bytes 589832 | tf_op jit(solution)/shard_map/ppermute | solution.py:15
  15.3 11.5 %collective-permute-start.22 = (bf16[4,192,256]{2,1,0:T(8,128)(2,1)S(1)}, bf16[4,192,256]{2,1,0:T(8,128)(2,1)S(1)}, u32[]{:S(2)}, u32[]{:S(2)}) collective-permute-start(bf16[4,192,256]{2,1,0:T(8,128)(2,1)S(1)} %shard_map.95), channel_id=1, source_target_pairs={{0,4},{4,0},{8,12},{12,8},{16,20},{20,16},{24,28},{28,24},{1,5},{5... | collective-permute-start | bytes 1179656 | tf_op jit(solution)/shard_map/ppermute | solution.py:15
  23.9 12.2 %collective-permute-start.4 = (bf16[3,48,1536]{2,1,0:T(8,128)(2,1)S(1)}, bf16[3,48,1536]{2,1,0:T(8,128)(2,1)S(1)}, u32[]{:S(2)}, u32[]{:S(2)}) collective-permute-start(bf16[3,48,1536]{2,1,0:T(8,128)(2,1)S(1)} %shard_map.86.refs_0_), channel_id=1, source_target_pairs={{0,16},{4,20},{8,24},{12,28},{16,0},{20,4},{24,8},{28,12},{1,17},{... | collective-permute-start | bytes 1327112 | tf_op jit(solution)/shard_map/ppermute | solution.py:15
  24.5 11.7 %collective-permute-start.3 = (bf16[3,48,1536]{2,1,0:T(8,128)(2,1)S(1)}, bf16[3,48,1536]{2,1,0:T(8,128)(2,1)S(1)}, u32[]{:S(2)}, u32[]{:S(2)}) collective-permute-start(bf16[3,48,1536]{2,1,0:T(8,128)(2,1)S(1)} %shard_map.86.refs_0_), channel_id=1, source_target_pairs={{0,8},{4,12},{8,0},{12,4},{16,24},{20,28},{24,16},{28,20},{1,9},{5... | collective-permute-start | bytes 1327112 | tf_op jit(solution)/shard_map/ppermute | solution.py:15
  26.0 11.8 %collective-permute-start.7 = (bf16[3,48,1536]{2,1,0:T(8,128)(2,1)S(1)}, bf16[3,48,1536]{2,1,0:T(8,128)(2,1)S(1)}, u32[]{:S(2)}, u32[]{:S(2)}) collective-permute-start(bf16[3,48,1536]{2,1,0:T(8,128)(2,1)S(1)} %shard_map.86.refs_0_), channel_id=1, source_target_pairs={{0,4},{4,0},{8,12},{12,8},{16,20},{20,16},{24,28},{28,24},{1,5},{5... | collective-permute-start | bytes 1327112 | tf_op jit(solution)/shard_map/ppermute | solution.py:15
  26.8 11.5 %collective-permute-start.15 = (bf16[4,192,256]{2,1,0:T(8,128)(2,1)S(1)}, bf16[4,192,256]{2,1,0:T(8,128)(2,1)S(1)}, u32[]{:S(2)}, u32[]{:S(2)}) collective-permute-start(bf16[4,192,256]{2,1,0:T(8,128)(2,1)S(1)} %shard_map.90), channel_id=1, source_target_pairs={{0,4},{4,0},{8,12},{12,8},{16,20},{20,16},{24,28},{28,24},{1,5},{5... | collective-permute-start | bytes 1179656 | tf_op jit(solution)/shard_map/ppermute | solution.py:15
  27.0 22.0 %collective-permute-start.23 = (bf16[1536,256]{1,0:T(8,128)(2,1)S(1)}, bf16[1536,256]{1,0:T(8,128)(2,1)S(1)}, u32[]{:S(2)}, u32[]{:S(2)}) collective-permute-start(bf16[1536,256]{1,0:T(8,128)(2,1)S(1)} %shard_map.96.raw), channel_id=1, source_target_pairs={{0,1},{1,0},{2,3},{3,2},{4,5},{5,4},{6,7},{7,6},{8,9},{9,8},{10,11... | collective-permute-start | bytes 2359304 | tf_op jit(solution)/shard_map/ppermute | solution.py:15
  37.7 7.9 %collective-permute-start.9 = (bf16[3,48,1536]{2,1,0:T(8,128)(2,1)S(1)}, bf16[3,48,1536]{2,1,0:T(8,128)(2,1)S(1)}, u32[]{:S(2)}, u32[]{:S(2)}) collective-permute-start(bf16[3,48,1536]{2,1,0:T(8,128)(2,1)S(1)} %collective-permute-done.4.by_y.refs_2_), channel_id=1, source_target_pairs={{0,4},{4,0},{8,12},{12,8},{16,20},{20,16},{24,28},{28,24},{1,5},{5... | collective-permute-start | bytes 1327112 | tf_op jit(solution)/shard_map/ppermute | solution.py:15
  37.7 7.8 %collective-permute-start.6 = (bf16[3,48,768]{2,1,0:T(8,128)(2,1)S(1)}, bf16[3,48,768]{2,1,0:T(8,128)(2,1)S(1)}, u32[]{:S(2)}, u32[]{:S(2)}) collective-permute-start(bf16[3,48,768]{2,1,0:T(8,128)(2,1)S(1)} %get-tuple-element.21), channel_id=1, source_target_pairs={{0,16},{4,20},{8,24},{12,28},{16,0},{20,4},{24,8},{28,12},{1,17},{... | collective-permute-start | bytes 663560 | tf_op jit(solution)/shard_map/ppermute | solution.py:15
  38.3 8.8 %collective-permute-start.8 = (bf16[3,48,1536]{2,1,0:T(8,128)(2,1)S(1)}, bf16[3,48,1536]{2,1,0:T(8,128)(2,1)S(1)}, u32[]{:S(2)}, u32[]{:S(2)}) collective-permute-start(bf16[3,48,1536]{2,1,0:T(8,128)(2,1)S(1)} %collective-permute-done.3.by_x.refs_1_), channel_id=1, source_target_pairs={{0,4},{4,0},{8,12},{12,8},{16,20},{20,16},{24,28},{28,24},{1,5},{5... | collective-permute-start | bytes 1327112 | tf_op jit(solution)/shard_map/ppermute | solution.py:15
  45.7 36.9 %collective-permute-start.16 = (bf16[1536,256]{1,0:T(8,128)(2,1)S(1)}, bf16[1536,256]{1,0:T(8,128)(2,1)S(1)}, u32[]{:S(2)}, u32[]{:S(2)}) collective-permute-start(bf16[1536,256]{1,0:T(8,128)(2,1)S(1)} %shard_map.91.raw), channel_id=1, source_target_pairs={{0,3},{1,2},{2,1},{3,0},{4,7},{5,6},{6,5},{7,4},{8,11},{9,10},{10,... | collective-permute-start | bytes 2359304 | tf_op jit(solution)/shard_map/ppermute | solution.py:15
  48.8 35.2 %collective-permute-start.24 = (bf16[1536,256]{1,0:T(8,128)(2,1)S(1)}, bf16[1536,256]{1,0:T(8,128)(2,1)S(1)}, u32[]{:S(2)}, u32[]{:S(2)}) collective-permute-start(bf16[1536,256]{1,0:T(8,128)(2,1)S(1)} %shard_map.97.a0), channel_id=1, source_target_pairs={{0,4},{4,0},{8,12},{12,8},{16,20},{20,16},{24,28},{28,24},{1,5},{5... | collective-permute-start | bytes 2359304 | tf_op jit(solution)/shard_map/ppermute | solution.py:15
  50.4 33.6 %collective-permute-start.25 = (bf16[1536,256]{1,0:T(8,128)(2,1)S(1)}, bf16[1536,256]{1,0:T(8,128)(2,1)S(1)}, u32[]{:S(2)}, u32[]{:S(2)}) collective-permute-start(bf16[1536,256]{1,0:T(8,128)(2,1)S(1)} %shard_map.98.a1), channel_id=1, source_target_pairs={{0,4},{4,0},{8,12},{12,8},{16,20},{20,16},{24,28},{28,24},{1,5},{5... | collective-permute-start | bytes 2359304 | tf_op jit(solution)/shard_map/ppermute | solution.py:15
  52.7 31.3 %collective-permute-start.26 = (f32[256]{0:T(256)S(1)}, f32[256]{0:T(256)S(1)}, u32[]{:S(2)}, u32[]{:S(2)}) collective-permute-start(f32[256]{0:T(256)S(1)} %copy-done.4), channel_id=1, source_target_pairs={{0,3},{1,2},{2,1},{3,0},{4,7},{5,6},{6,5},{7,4},{8,11},{9,10},{10,... | collective-permute-start | bytes 3080 | tf_op jit(solution)/shard_map/ppermute | solution.py:15
  53.6 30.3 %collective-permute-start.18 = (f32[1]{0:T(128)}, f32[1]{0:T(128)}, u32[]{:S(2)}, u32[]{:S(2)}) collective-permute-start(f32[1]{0:T(128)} %collective-permute-done.17.occ_a), channel_id=1, source_target_pairs={{0,4},{4,0},{8,12},{12,8},{16,20},{20,16},{24,28},{28,24},{1,5},{5... | collective-permute-start | bytes 20 | tf_op jit(solution)/shard_map/ppermute | solution.py:15
  96.7 21.7 %collective-permute-start.28 = (bf16[1536,256]{1,0:T(8,128)(2,1)S(1)}, bf16[1536,256]{1,0:T(8,128)(2,1)S(1)}, u32[]{:S(2)}, u32[]{:S(2)}) collective-permute-start(bf16[1536,256]{1,0:T(8,128)(2,1)S(1)} %get-tuple-element.35), channel_id=1, source_target_pairs={{0,3},{1,2},{2,1},{3,0},{4,5},{5,4},{6,7},{7,6},{8,11},{9,10},{10,... | collective-permute-start | bytes 2359304 | tf_op jit(solution)/shard_map/ppermute | solution.py:303
  97.5 22.3 %collective-permute-start.30 = (bf16[1536,256]{1,0:T(8,128)(2,1)S(1)}, bf16[1536,256]{1,0:T(8,128)(2,1)S(1)}, u32[]{:S(2)}, u32[]{:S(2)}) collective-permute-start(bf16[1536,256]{1,0:T(8,128)(2,1)S(1)} %get-tuple-element.37), channel_id=1, source_target_pairs={{0,1},{1,0},{2,3},{3,2},{4,7},{5,6},{6,5},{7,4},{8,9},{9,8},{10,11... | collective-permute-start | bytes 2359304 | tf_op jit(solution)/shard_map/ppermute | solution.py:303
  119.5 16.2 %collective-permute-start.29 = (bf16[1536,256]{1,0:T(8,128)(2,1)}, bf16[1536,256]{1,0:T(8,128)(2,1)}, u32[]{:S(2)}, u32[]{:S(2)}) collective-permute-start(bf16[1536,256]{1,0:T(8,128)(2,1)} %add_convert_fusion.1), channel_id=1, source_target_pairs={{0,8},{4,12},{8,0},{12,4},{16,24},{20,28},{24,16},{28,20},{1,9},{5... | collective-permute-start | bytes 2359304 | tf_op jit(solution)/shard_map/ppermute | solution.py:15
  (13 other events, 115.5 us)

commit v2 on v1

--- a/solution.py
+++ b/solution.py
@@ -75,17 +75,19 @@
 
 
 def place_rows(chips, *refs):
-    held, take, out = refs[:chips], refs[chips], refs[-1]
+    held, take, outs = refs[:chips], refs[chips], refs[chips + 1 :]
     rows = take.shape[1]
     me = lax.axis_index("occ")
     chip, core = me // 2, me % 2
     for m in range(chips):
         start = 2 * (chip ^ m) * rows
-        out[at(start + core * rows, rows), :] = held[m][core]
-        out[at(start + (1 - core) * rows, rows), :] = take[m]
-
-
-def regroup(ints, index_of):
+        for i, out in enumerate(outs):
+            cols = slice(i * out.shape[1], (i + 1) * out.shape[1])
+            out[at(start + core * rows, rows), :] = held[m][core, :, cols]
+            out[at(start + (1 - core) * rows, rows), :] = take[m, :, cols]
+
+
+def regroup(ints, index_of, parts):
     blocks = lax.axis_size("occ")
     chips = blocks // 2
     rows, _, cols = ints.shape
@@ -93,7 +95,7 @@
         table = ints.transpose(1, 0, 2)
         table = jnp.stack([table[index_of(d)] for d in range(blocks)])
         got = lax.all_to_all(table, "occ", split_axis=0, concat_axis=0, tiled=True)
-        return got.reshape(blocks * rows, cols)
+        return jnp.split(got.reshape(blocks * rows, cols), parts, axis=1)
     held = [*call(
         lambda *refs: split_rows(index_of, chips, *refs),
         [shape_of(2, rows, cols)] * chips,
@@ -105,7 +107,8 @@
     give = call(give_rows, shape_of(chips, rows, cols), *held)
     take = swap(give, "occ", 1)
     place = lambda *refs: place_rows(chips, *refs)
-    return call(place, shape_of(blocks * rows, cols), *held, take)
+    shapes = [shape_of(blocks * rows, cols // parts)] * parts
+    return call(place, shapes, *held, take)
 
 
 def halves_metric(metric):
@@ -172,30 +175,42 @@
         body(slice(start, start + step))
 
 
-def fit_rows(square, raw, out):
+def fit_rows(square, *refs):
+    raws, out = refs[:-1], refs[-1]
+    raw = jnp.concatenate([r[...] for r in raws], axis=1)
+
     def body(rows):
-        out[rows, :] = dots(square[rows, :], raw[...], 1, 0).astype(BF16)
+        out[rows, :] = dots(square[rows, :], raw, 1, 0).astype(BF16)
 
     row_chunks(square.shape[0], body)
 
 
-def fit(square, raw):
-    aux, unit = raw.shape
-    return call(fit_rows, shape_of(aux, unit), square, raw, flops=2 * aux * aux * unit)
-
-
-def tile_rows(occ_a, occ_o, occ_b, vir_a, vir_b, a0, a1, o0, o1, beta, amp, gamma, flip):
+def fit(square, *raws):
+    aux = square.shape[0]
+    unit = sum(raw.shape[1] for raw in raws)
+    return call(fit_rows, shape_of(aux, unit), square, *raws, flops=2 * aux * aux * unit)
+
+
+def energy_rows(occ_a, occ_o, occ_b, vir_a, vir_b, vir_n, left, right, *near):
     layer, me = lax.axis_index("vir"), lax.axis_index("occ")
-    unit = beta.shape[1]
+    unit = vir_b.shape[1]
+    for u, occ in enumerate((occ_a, occ_a, occ_o, occ_o)):
+        row = vir_a[at((layer ^ (u % 2)) * unit, unit)].reshape(1, unit)
+        left[u : u + 1, :] = occ[0] - row
+    column = lambda vir: jnp.broadcast_to(occ_b[beta_of(me)] - vir[...], (128, unit)).T
+    right[...] = column(vir_b)
+    half = unit // 2
+    for i, out in enumerate(near):
+        out[...] = column(vir_n)[i * half : (i + 1) * half]
+
+
+def tile_rows(a0, a1, o0, o1, beta, left, right, amp, gamma, flip):
     alphas = (a0, a1, o0, o1)
     flip[...] = beta[...].T
-    right = occ_b[beta_of(me)] - vir_b[...]
-    right = jnp.broadcast_to(right, (128, unit)).T[:, :1]
+    column = right[:, :1]
     for u, alpha in enumerate(alphas):
-        row = vir_a[at((layer ^ (u % 2)) * unit, unit)].reshape(1, unit)
-        left = (occ_a, occ_a, occ_o, occ_o)[u][0] - row
         pair = dots(flip[...], alpha[...], 1, 0)
-        amp[u] = (pair / (left + right)).astype(BF16)
+        amp[u] = (pair / (left[u : u + 1, :] + column)).astype(BF16)
 
     def body(rows):
         total = dots(a0[rows, :], amp[0], 1, 1)
@@ -206,109 +221,190 @@
     row_chunks(beta.shape[0], body)
 
 
-def tile(energies, alphas, beta, dtype):
-    aux, unit = beta.shape
+def tile(alphas, beta, left, right, dtype):
+    aux, width = beta.shape
+    unit = alphas[0].shape[1]
     return call(
         tile_rows,
-        [shape_of(4, unit, unit), shape_of(aux, unit, dtype=dtype)],
-        *energies,
+        [shape_of(4, width, unit), shape_of(aux, width, dtype=dtype)],
         *alphas,
         beta,
-        scratch=[pltpu.VMEM((unit, aux), BF16)],
-        flops=16 * aux * unit * unit,
-        specs=[SMEM] * 3 + [VMEM] * 7,
+        left,
+        right,
+        scratch=[pltpu.VMEM((width, aux), BF16)],
+        flops=16 * aux * unit * width,
     )
 
 
-def term_rows(first, own, near, amp_own, amp_near, out):
+def early_rows(own, near, amp_own, amp_near, out):
+    unit = amp_own.shape[2]
+
+    def body(rows):
+        for u in range(4):
+            total = dots(own[rows, :], amp_own[u], 1, 0) + dots(near[rows, :], amp_near[u], 1, 0)
+            out[rows, u * unit : (u + 1) * unit] = total
+
+    row_chunks(own.shape[0], body)
+
+
+def late_rows(early, near, amp, out):
+    unit = amp.shape[2]
+
     def body(rows):
         for u in (0, 1):
-            cols = slice(u * own.shape[1], (u + 1) * own.shape[1])
-            total = dots(own[rows, :], amp_own[first + u], 1, 0)
-            total = total + dots(near[rows, :], amp_near[first + u], 1, 0)
-            out[rows, cols] = total.astype(out.dtype)
-
-    row_chunks(own.shape[0], body)
-
-
-def term(first, own, near, amp_own, amp_near, dtype):
-    aux, unit = own.shape
-    kernel = lambda *refs: term_rows(first, *refs)
-    shape = shape_of(aux, 2 * unit, dtype=dtype)
-    flops = 8 * aux * unit * unit
-    return call(kernel, shape, own, near, amp_own, amp_near, flops=flops)
-
-
-def mix_rows(gamma_alpha, from_core, own, near, send_a, send_b, keep_a, keep_b):
-    unit = own.shape[1]
+            total = early[rows, (2 + u) * unit : (3 + u) * unit] + dots(near[rows, :], amp[2 + u], 1, 0)
+            out[rows, u * unit : (u + 1) * unit] = total.astype(BF16)
+
+    row_chunks(near.shape[0], body)
+
+
+def mix_rows(early, near, amp, core_term, own_gamma, near_gamma, *outs):
+    unit = amp.shape[2]
+    half = unit // 2
     odd = lax.axis_index("occ") % 2 == 1
 
     def body(rows):
-        alpha = gamma_alpha[rows, :] + from_core[rows, :].astype(F32)
-        here, there = alpha[:, :unit], alpha[:, unit:].astype(BF16)
-        beta, far = own[rows, :], near[rows, :]
-        keep_a[rows, :] = jnp.where(odd, here, beta)
-        keep_b[rows, :] = jnp.where(odd, beta, here)
-        send_a[rows, :] = jnp.where(odd, there, far)
-        send_b[rows, :] = jnp.where(odd, far, there)
-
-    row_chunks(own.shape[0], body)
+        alpha = []
+        for u in (0, 1):
+            cols = slice(u * unit, (u + 1) * unit)
+            total = early[rows, cols] + dots(near[rows, :], amp[u], 1, 0)
+            alpha.append(total + core_term[rows, cols].astype(F32))
+        here, there = alpha[0], alpha[1].astype(BF16)
+        beta, far = own_gamma[rows, half:], near_gamma[rows, :]
+        pick = lambda a, b: jnp.where(odd, a, b)
+        outs[0][rows, :] = pick(there[:, :half], far)
+        outs[1][rows, :] = pick(there[:, half:], there[:, :half])
+        outs[2][rows, :] = pick(far, there[:, half:])
+        outs[3][rows, :] = pick(here[:, :half], beta)
+        outs[4][rows, :] = pick(here[:, half:], here[:, :half])
+        outs[5][rows, :] = pick(beta, here[:, half:])
+
+    row_chunks(near.shape[0], body, 256)
+
+
+def sum_one(own_gamma, got, out):
+    out[...] = (own_gamma[:, : out.shape[1]] + got[...].astype(F32)).astype(BF16)
+
+
+def sum_two(keep, got, first, out, send):
+    odd = lax.axis_index("occ") % 2 == 1
+    total = (keep[...] + got[...].astype(F32)).astype(BF16)
+    out[...] = total
+    send[...] = jnp.where(odd, total, first[...])
+
+
+def sum_three(keep, got, second, out, send):
+    odd = lax.axis_index("occ") % 2 == 1
+    total = (keep[...] + got[...].astype(F32)).astype(BF16)
+    out[...] = total
+    send[...] = jnp.where(odd, total, second[...])
+
+
+def last_rows(keep, got, first, third, move_a, move_b, alpha, beta):
+    odd = lax.axis_index("occ") % 2 == 1
+    half = keep.shape[1]
+    final = (keep[...] + got[...].astype(F32)).astype(BF16)
+    side = jnp.where(odd, first[...], third[...])
+    a, b = move_a[...], move_b[...]
+    alpha[:, :half] = jnp.where(odd, a, side)
+    alpha[:, half:] = jnp.where(odd, b, final)
+    beta[:, :half] = jnp.where(odd, side, a)
+    beta[:, half:] = jnp.where(odd, final, b)
+
+
+def last(*arrays):
+    aux, half = arrays[0].shape
+    step = 256 if aux % 256 == 0 else aux
+    spec = lambda width: pl.BlockSpec((step, width), lambda i: (i, 0))
+    return pl.pallas_call(
+        last_rows,
+        grid=(aux // step,),
+        out_shape=[shape_of(aux, 2 * half)] * 2,
+        in_specs=[spec(half)] * len(arrays),
+        out_specs=[spec(2 * half)] * 2,
+        compiler_params=pltpu.CompilerParams(vmem_limit_bytes=8 << 20),
+    )(*arrays)
 
 
 def ring(ints_alpha, ints_beta, metric, e_occ_alpha, e_occ_beta, e_vir_alpha, e_vir_beta):
     aux = metric.shape[1]
     unit = e_vir_beta.shape[0]
+    half = unit // 2
     blocks, layers = lax.axis_size("occ"), lax.axis_size("vir")
     assert layers == 4 and e_occ_alpha.shape[0] == 1
-    core = lax.axis_index("occ") % 2
 
     square = whole_metric(metric)
-    raw_beta = regroup(ints_beta, beta_of)
-    raw_alpha = regroup(ints_alpha, alpha_of)
+    raw_beta = regroup(ints_beta, beta_of, 2)
+    (raw_alpha,) = regroup(ints_alpha, alpha_of, 1)
 
     occ_mine = lax.ppermute(e_occ_alpha, "occ", [(alpha_of(d), d) for d in range(blocks)])
     vir_near = swap(e_vir_beta, "vir", 3)
     occ_other = swap(occ_mine, "occ", 1)
-    common = [occ_mine, occ_other, e_occ_beta, e_vir_alpha]
-
-    near_beta = swap(raw_beta, "vir", 3)
+    left, right, right_zero, right_one = call(
+        energy_rows,
+        [shape_of(4, unit, dtype=F32)] + [shape_of(n, 128, dtype=F32) for n in (unit, half, half)],
+        occ_mine,
+        occ_other,
+        e_occ_beta,
+        e_vir_alpha,
+        e_vir_beta[None],
+        vir_near[None],
+        specs=[SMEM] * 3 + [VMEM] * 3,
+    )
+
+    near_beta = []
+    for raw in raw_beta:
+        near_beta.append(swap(raw, "vir", 3))
     near_alpha = swap(raw_alpha, "vir", 1)
 
     a0 = fit(square, raw_alpha)
-    b0 = fit(square, raw_beta)
+    o0 = swap(a0, "occ", 1)
+    b0 = fit(square, *raw_beta)
     a1 = fit(square, near_alpha)
-    o0, o1 = swap(a0, "occ", 1), swap(a1, "occ", 1)
+    o1 = swap(a1, "occ", 1)
     alphas = (a0, a1, o0, o1)
-    amp_own, gamma_own = tile(common + [e_vir_beta[None]], alphas, b0, F32)
-    b1 = fit(square, near_beta)
-    amp_near, gamma_near = tile(common + [vir_near[None]], alphas, b1, BF16)
-    other_term = term(2, b0, b1, amp_own, amp_near, BF16)
-    from_core = swap(other_term, "occ", 1)
-    mine_term = term(0, b0, b1, amp_own, amp_near, F32)
-    send_a, send_b, keep_a, keep_b = call(
-        mix_rows,
-        [shape_of(aux, unit)] * 2 + [shape_of(aux, unit, dtype=F32)] * 2,
-        mine_term,
-        from_core,
-        gamma_own,
-        gamma_near,
-    )
-
-    def back(send, keep, odd, even):
+    amp_own, gamma_own = tile(alphas, b0, left, right, F32)
+    b1 = fit(square, near_beta[0])
+    amp_zero, gamma_zero = tile(alphas, b1, left, right_zero, BF16)
+
+    def back(send, odd, even):
         pairs = [
             (d * layers + v, d * layers + (v ^ (odd if d % 2 else even)))
             for d in range(blocks)
             for v in range(layers)
         ]
-        got = lax.ppermute(send, ("occ", "vir"), pairs)
-        return (keep + got.astype(F32)).astype(BF16)
-
-    done_a = back(send_a, keep_a, 1, 3)
-    moved = swap(done_a, "occ", 2)
-    kept = back(send_b, keep_b, 3, 1)
-    out_alpha = jnp.where(core == 1, moved, kept).reshape(aux, 1, unit)
-    out_beta = jnp.where(core == 1, kept, moved).reshape(aux, 1, unit)
-    return out_alpha, out_beta
+        return lax.ppermute(send, ("occ", "vir"), pairs)
+
+    got_one = back(gamma_zero, 3, 3)
+    wide = shape_of(aux, 4 * unit, dtype=F32)
+    early = call(early_rows, wide, b0, b1, amp_own, amp_zero, flops=12 * aux * unit * unit)
+    b2 = fit(square, near_beta[1])
+    amp_one, gamma_one = tile(alphas, b2, left, right_one, BF16)
+    pair = shape_of(aux, 2 * unit)
+    term = call(late_rows, pair, early, b2, amp_one, flops=2 * aux * unit * unit)
+    from_core = swap(term, "occ", 1)
+    thin, thin32 = shape_of(aux, half), shape_of(aux, half, dtype=F32)
+    send2, send3, send4, keep2, keep3, keep4 = call(
+        mix_rows,
+        [thin] * 3 + [thin32] * 3,
+        early,
+        b2,
+        amp_one,
+        from_core,
+        gamma_own,
+        gamma_one,
+        flops=2 * aux * unit * unit,
+    )
+    got_two = back(send2, 1, 3)
+    got_three = back(send3, 1, 1)
+    got_four = back(send4, 3, 1)
+    first = call(sum_one, thin, gamma_own, got_one)
+    second, send_a = call(sum_two, [thin] * 2, keep2, got_two, first)
+    move_a = swap(send_a, "occ", 2)
+    third, send_b = call(sum_three, [thin] * 2, keep3, got_three, second)
+    move_b = swap(send_b, "occ", 2)
+    out_alpha, out_beta = last(keep4, got_four, first, third, move_a, move_b)
+    return out_alpha.reshape(aux, 1, unit), out_beta.reshape(aux, 1, unit)
 
 
 def solution(mesh):

time: 139 us -> 142 us (1.022)
  the two profiles are of different devices: /device:TPU:12 before, /device:TPU:11 now
where the time goes in v2:
time: 142 us
  waiting for transfers between devices  75.3 us (53%)
  starting transfers between devices  42.3 us (30%)
  Pallas kernels  21.1 us (15%)
  local copies, waits for them, and re-layouts  2.09 us (1%)
    ppermute x30, waiting for transfers between devices, swap(): return lax.ppermute(value, axis, pairs)  58.6 us
    ppermute x30, starting transfers between devices, swap(): return lax.ppermute(value, axis, pairs)  36 us
    pallas_call x24, Pallas kernels, call(): pl.pallas_call(kernel, out_shape=shapes, in_specs=specs or [VMEM] * len(a...  18.8 us
    ppermute x4, waiting for transfers between devices, back(): return lax.ppermute(send, ('occ', 'vir'), pairs)  14.1 us
    ppermute x4, starting transfers between devices, back(): return lax.ppermute(send, ('occ', 'vir'), pairs)  4.2 us
  transfers between devices with their start and end apart: 35, of which 15 were waited for; matrix products, arithmetic and copies ran while one was open for 0% of the time, Pallas kernels for 8%

profile of v2, /device:TPU:11, one launch (start us, length us, event | category | flops | bytes accessed | tf_op | source)
XLA Modules:
  0.0 141.8 jit_solution(10965200777134553363)
XLA Ops:
  8.2 1.5 %collective-permute-done.2.refs_2_ = bf16[48,1536]{1,0:T(8,128)(2,1)S(1)} collective-permute-done((bf16[48,1536]{1,0:T(8,128)(2,1)S(1)}, bf16[48,1536]{1,0:T(8,128)(2,1)S(1)}, u32[]{:S(2)}, u32[]{:S(2)}) %collective-permute-start.2) | collective-permute-done | bytes 147488 | tf_op jit(solution)/shard_map/ppermute | solution.py:15
  9.7 5.2 %collective-permute-done.1.refs_1_ = bf16[48,1536]{1,0:T(8,128)(2,1)S(1)} collective-permute-done((bf16[48,1536]{1,0:T(8,128)(2,1)S(1)}, bf16[48,1536]{1,0:T(8,128)(2,1)S(1)}, u32[]{:S(2)}, u32[]{:S(2)}) %collective-permute-start.1) | collective-permute-done | bytes 147488 | tf_op jit(solution)/shard_map/ppermute | solution.py:15
  17.1 3.4 %collective-permute-start.20 = (bf16[4,192,256]{2,1,0:T(8,128)(2,1)S(1)}, bf16[4,192,256]{2,1,0:T(8,128)(2,1)S(1)}, u32[]{:S(2)}, u32[]{:S(2)}) collective-permute-start(bf16[4,192,256]{2,1,0:T(8,128)(2,1)S(1)} %shard_map.95), channel_id=1, source_target_pairs={{0,4},{4,0},{8,12},{12,8},{16,20},{20,16},{24,28},{28,24},{1,5},{5... | collective-permute-start | bytes 1179656 | tf_op jit(solution)/shard_map/ppermute | solution.py:15
  21.9 1.5 %collective-permute-start.21 = (bf16[1536,256]{1,0:T(8,128)(2,1)S(1)}, bf16[1536,256]{1,0:T(8,128)(2,1)S(1)}, u32[]{:S(2)}, u32[]{:S(2)}) collective-permute-start(bf16[1536,256]{1,0:T(8,128)(2,1)S(1)} %shard_map.96.refs_0_), channel_id=1, source_target_pairs={{0,1},{1,0},{2,3},{3,2},{4,5},{5,4},{6,7},{7,6},{8,9},{9,8},{10,11... | collective-permute-start | bytes 2359304 | tf_op jit(solution)/shard_map/ppermute | solution.py:15
  26.6 4.2 %collective-permute-done.12.refs_1_ = bf16[2,192,256]{2,1,0:T(8,128)(2,1)S(1)} collective-permute-done((bf16[2,192,256]{2,1,0:T(8,128)(2,1)S(1)}, bf16[2,192,256]{2,1,0:T(8,128)(2,1)S(1)}, u32[]{:S(2)}, u32[]{:S(2)}) %collective-permute-start.12) | collective-permute-done | bytes 196640 | tf_op jit(solution)/shard_map/ppermute | solution.py:15
  32.1 3.8 %collective-permute-start.9 = (bf16[3,48,1536]{2,1,0:T(8,128)(2,1)S(1)}, bf16[3,48,1536]{2,1,0:T(8,128)(2,1)S(1)}, u32[]{:S(2)}, u32[]{:S(2)}) collective-permute-start(bf16[3,48,1536]{2,1,0:T(8,128)(2,1)S(1)} %collective-permute-done.4.by_y.refs_2_), channel_id=1, source_target_pairs={{0,4},{4,0},{8,12},{12,8},{16,20},{20,16},{24,28},{28,24},{1,5},{5... | collective-permute-start | bytes 1327112 | tf_op jit(solution)/shard_map/ppermute | solution.py:15
  35.8 1.4 %collective-permute-start.6 = (bf16[3,48,768]{2,1,0:T(8,128)(2,1)S(1)}, bf16[3,48,768]{2,1,0:T(8,128)(2,1)S(1)}, u32[]{:S(2)}, u32[]{:S(2)}) collective-permute-start(bf16[3,48,768]{2,1,0:T(8,128)(2,1)S(1)} %get-tuple-element.37), channel_id=1, source_target_pairs={{0,16},{4,20},{8,24},{12,28},{16,0},{20,4},{24,8},{28,12},{1,17},{... | collective-permute-start | bytes 663560 | tf_op jit(solution)/shard_map/ppermute | solution.py:15
  37.3 4.2 %collective-permute-start.8 = (bf16[3,48,1536]{2,1,0:T(8,128)(2,1)S(1)}, bf16[3,48,1536]{2,1,0:T(8,128)(2,1)S(1)}, u32[]{:S(2)}, u32[]{:S(2)}) collective-permute-start(bf16[3,48,1536]{2,1,0:T(8,128)(2,1)S(1)} %collective-permute-done.3.by_x.refs_1_), channel_id=1, source_target_pairs={{0,4},{4,0},{8,12},{12,8},{16,20},{20,16},{24,28},{28,24},{1,5},{5... | collective-permute-start | bytes 1327112 | tf_op jit(solution)/shard_map/ppermute | solution.py:15
  42.5 3.6 %collective-permute-start.11 = (bf16[3,48,768]{2,1,0:T(8,128)(2,1)S(1)}, bf16[3,48,768]{2,1,0:T(8,128)(2,1)S(1)}, u32[]{:S(2)}, u32[]{:S(2)}) collective-permute-start(bf16[3,48,768]{2,1,0:T(8,128)(2,1)S(1)} %collective-permute-done.6.refs_4_), channel_id=1, source_target_pairs={{0,4},{4,0},{8,12},{12,8},{16,20},{20,16},{24,28},{28,24},{1,5},{5... | collective-permute-start | bytes 663560 | tf_op jit(solution)/shard_map/ppermute | solution.py:15
  52.7 2.1 %collective-permute-start.24 = (f32[1]{0:T(128)}, f32[1]{0:T(128)}, u32[]{:S(2)}, u32[]{:S(2)}) collective-permute-start(f32[1]{0:T(128)} %param.10), channel_id=1, source_target_pairs={{0,0},{12,4},{8,8},{4,12},{16,16},{28,20},{24,24},{20,28},{1,1},{1... | collective-permute-start | bytes 20 | tf_op jit(solution)/shard_map/ppermute | solution.py:340
  54.8 2.6 %collective-permute-done.24.occ_a = f32[1]{0:T(128)} collective-permute-done((f32[1]{0:T(128)}, f32[1]{0:T(128)}, u32[]{:S(2)}, u32[]{:S(2)}) %collective-permute-start.24) | collective-permute-done | bytes 36 | tf_op jit(solution)/shard_map/ppermute | solution.py:340
  60.1 26.8 %collective-permute-done.26 = f32[256]{0:T(256)S(1)} collective-permute-done((f32[256]{0:T(256)S(1)}, f32[256]{0:T(256)S(1)}, u32[]{:S(2)}, u32[]{:S(2)}) %collective-permute-start.26) | collective-permute-done | bytes 1056 | tf_op jit(solution)/shard_map/ppermute | solution.py:15
  86.8 1.9 %shard_map.99 = (f32[4,256]{1,0:T(4,128)S(1)}, f32[256,128]{1,0:T(8,128)S(1)}, f32[128,128]{1,0:T(8,128)S(1)}, f32[128,128]{1,0:T(8,128)S(1)}) custom-call(f32[1]{0:T(128)} %collective-permute-done.24.occ_a, f32[1]{0:T(128)} %collective-permute-done.25.occ_o, f32[8]{0:T(128)S(1)} %copy-done.5, f32[1024]{0:T(1024)S(1)} %copy-done.3, f32[1,256]{1,0:T(1,128)S(1)} %bitcast.4, ...), custom_call_target="tpu_custom_call" | custom-call | bytes 1048576 | tf_op jit(solution)/shard_map/pallas_call | solution.py:31
  92.9 1.5 %shard_map.101 = (bf16[4,128,256]{2,1,0:T(8,128)(2,1)S(1)}, bf16[1536,128]{1,0:T(8,128)(2,1)S(1)}) custom-call(bf16[1536,256]{1,0:T(8,128)(2,1)S(1)} %shard_map.97.a0, bf16[1536,256]{1,0:T(8,128)(2,1)S(1)} %shard_map.98.a1, bf16[1536,256]{1,0:T(8,128)(2,1)S(1)} %collective-permute-done.22.o0, bf16[1536,256]{1,0:T(8,128)(2,1)S(1)} %collective-permute-done.23.o1, ...), custom_call_target="tpu_custom_call" | custom-call | flops 805306368 | bytes 1048576 | tf_op jit(solution)/shard_map/pallas_call | solution.py:31
  94.5 1.9 %shard_map.100 = (bf16[4,256,256]{2,1,0:T(8,128)(2,1)S(1)}, f32[1536,256]{1,0:T(8,128)S(1)}) custom-call(bf16[1536,256]{1,0:T(8,128)(2,1)S(1)} %shard_map.97.a0, bf16[1536,256]{1,0:T(8,128)(2,1)S(1)} %shard_map.98.a1, bf16[1536,256]{1,0:T(8,128)(2,1)S(1)} %collective-permute-done.22.o0, bf16[1536,256]{1,0:T(8,128)(2,1)S(1)} %collective-permute-done.23.o1, ...), custom_call_target="tpu_custom_call" | custom-call | flops 1610612736 | bytes 1048576 | tf_op jit(solution)/shard_map/pallas_call | solution.py:31
  96.4 1.8 %shard_map.102.early = f32[1536,1024]{1,0:T(8,128)S(1)} custom-call(bf16[1536,256]{1,0:T(8,128)(2,1)S(1)} %shard_map.92.beta.own, bf16[1536,128]{1,0:T(8,128)(2,1)S(1)} %shard_map.93.beta.near, bf16[4,256,256]{2,1,0:T(8,128)(2,1)S(1)} %get-tuple-element.50.amp_own, bf16[4,128,256]{2,1,0:T(8,128)(2,1)S(1)} %get-tuple-element.52.amp_near), custom_call_target="tpu_custom_call" | custom-call | flops 1207959552 | bytes 1048576 | tf_op jit(solution)/shard_map/pallas_call | solution.py:31
  98.2 1.6 %shard_map.104 = (bf16[4,128,256]{2,1,0:T(8,128)(2,1)S(1)}, bf16[1536,128]{1,0:T(8,128)(2,1)S(1)}) custom-call(bf16[1536,256]{1,0:T(8,128)(2,1)S(1)} %shard_map.97.a0, bf16[1536,256]{1,0:T(8,128)(2,1)S(1)} %shard_map.98.a1, bf16[1536,256]{1,0:T(8,128)(2,1)S(1)} %collective-permute-done.22.o0, bf16[1536,256]{1,0:T(8,128)(2,1)S(1)} %collective-permute-done.23.o1, ...), custom_call_target="tpu_custom_call" | custom-call | flops 805306368 | bytes 1048576 | tf_op jit(solution)/shard_map/pallas_call | solution.py:31
  103.0 1.7 %collective-permute-done.28.core_term = bf16[1536,512]{1,0:T(8,128)(2,1)S(1)} collective-permute-done((bf16[1536,512]{1,0:T(8,128)(2,1)S(1)}, bf16[1536,512]{1,0:T(8,128)(2,1)S(1)}, u32[]{:S(2)}, u32[]{:S(2)}) %collective-permute-start.28) | collective-permute-done | bytes 1572896 | tf_op jit(solution)/shard_map/ppermute | solution.py:15
  105.6 1.5 %collective-permute-start.31 = (bf16[1536,128]{1,0:T(8,128)(2,1)S(1)}, bf16[1536,128]{1,0:T(8,128)(2,1)S(1)}, u32[]{:S(2)}, u32[]{:S(2)}) collective-permute-start(bf16[1536,128]{1,0:T(8,128)(2,1)S(1)} %get-tuple-element.61), channel_id=1, source_target_pairs={{0,1},{1,0},{2,3},{3,2},{4,5},{5,4},{6,7},{7,6},{8,9},{9,8},{10,11... | collective-permute-start | bytes 1179656 | tf_op jit(solution)/shard_map/ppermute | solution.py:376
  107.1 5.2 %collective-permute-done.30.got = bf16[1536,128]{1,0:T(8,128)(2,1)S(1)} collective-permute-done((bf16[1536,128]{1,0:T(8,128)(2,1)S(1)}, bf16[1536,128]{1,0:T(8,128)(2,1)S(1)}, u32[]{:S(2)}, u32[]{:S(2)}) %collective-permute-start.30) | collective-permute-done | bytes 393248 | tf_op jit(solution)/shard_map/ppermute | solution.py:376
  114.4 8.3 %collective-permute-done.31.got = bf16[1536,128]{1,0:T(8,128)(2,1)S(1)} collective-permute-done((bf16[1536,128]{1,0:T(8,128)(2,1)S(1)}, bf16[1536,128]{1,0:T(8,128)(2,1)S(1)}, u32[]{:S(2)}, u32[]{:S(2)}) %collective-permute-start.31) | collective-permute-done | bytes 393248 | tf_op jit(solution)/shard_map/ppermute | solution.py:376
  124.4 9.7 %collective-permute-done.34.move_b = bf16[1536,128]{1,0:T(8,128)(2,1)S(1)} collective-permute-done((bf16[1536,128]{1,0:T(8,128)(2,1)S(1)}, bf16[1536,128]{1,0:T(8,128)(2,1)S(1)}, u32[]{:S(2)}, u32[]{:S(2)}) %collective-permute-start.34) | collective-permute-done | bytes 393248 | tf_op jit(solution)/shard_map/ppermute | solution.py:15
  134.1 5.4 %collective-permute-done.33.move_a = bf16[1536,128]{1,0:T(8,128)(2,1)S(1)} collective-permute-done((bf16[1536,128]{1,0:T(8,128)(2,1)S(1)}, bf16[1536,128]{1,0:T(8,128)(2,1)S(1)}, u32[]{:S(2)}, u32[]{:S(2)}) %collective-permute-start.33) | collective-permute-done | bytes 393248 | tf_op jit(solution)/shard_map/ppermute | solution.py:15
  139.4 2.3 %shard_map.110 = (bf16[1536,256]{1,0:T(8,128)(2,1)}, bf16[1536,256]{1,0:T(8,128)(2,1)}) custom-call(f32[1536,128]{1,0:T(8,128)S(1)} %get-tuple-element.57.keep, bf16[1536,128]{1,0:T(8,128)(2,1)S(1)} %collective-permute-done.29.got, bf16[1536,128]{1,0:T(8,128)(2,1)S(1)} %shard_map.107.first, bf16[1536,128]{1,0:T(8,128)(2,1)S(1)} %get-tuple-element.65.third, ...), custom_call_target="tpu_custom_call" | custom-call | tf_op jit(solution)/shard_map/pallas_call | solution.py:319
  (84 shorter events, 37.7 us)
Async XLA Ops:
  1.6 8.1 %collective-permute-start.2 = (bf16[48,1536]{1,0:T(8,128)(2,1)S(1)}, bf16[48,1536]{1,0:T(8,128)(2,1)S(1)}, u32[]{:S(2)}, u32[]{:S(2)}) collective-permute-start(bf16[48,1536]{1,0:T(8,128)(2,1)S(1)} %constant_dynamic-slice_fusion), channel_id=1, source_target_pairs={{0,3},{1,2},{2,1},{3,0},{4,7},{5,6},{6,5},{7,4},{8,11},{9,10},{10,... | collective-permute-start | bytes 442376 | tf_op jit(solution)/shard_map/ppermute | solution.py:15
  4.5 12.5 %collective-permute-start.17 = (bf16[2,192,256]{2,1,0:T(8,128)(2,1)S(1)}, bf16[2,192,256]{2,1,0:T(8,128)(2,1)S(1)}, u32[]{:S(2)}, u32[]{:S(2)}) collective-permute-start(bf16[2,192,256]{2,1,0:T(8,128)(2,1)S(1)} %get-tuple-element.45), channel_id=1, source_target_pairs={{0,8},{4,12},{8,0},{12,4},{16,24},{20,28},{24,16},{28,20},{1,9},{5... | collective-permute-start | bytes 589832 | tf_op jit(solution)/shard_map/ppermute | solution.py:15
  4.8 12.2 %collective-permute-start.18 = (bf16[2,192,256]{2,1,0:T(8,128)(2,1)S(1)}, bf16[2,192,256]{2,1,0:T(8,128)(2,1)S(1)}, u32[]{:S(2)}, u32[]{:S(2)}) collective-permute-start(bf16[2,192,256]{2,1,0:T(8,128)(2,1)S(1)} %get-tuple-element.46), channel_id=1, source_target_pairs={{0,16},{4,20},{8,24},{12,28},{16,0},{20,4},{24,8},{28,12},{1,17},{... | collective-permute-start | bytes 589832 | tf_op jit(solution)/shard_map/ppermute | solution.py:15
  6.0 11.0 %collective-permute-start.19 = (bf16[2,192,256]{2,1,0:T(8,128)(2,1)S(1)}, bf16[2,192,256]{2,1,0:T(8,128)(2,1)S(1)}, u32[]{:S(2)}, u32[]{:S(2)}) collective-permute-start(bf16[2,192,256]{2,1,0:T(8,128)(2,1)S(1)} %get-tuple-element.47), channel_id=1, source_target_pairs={{0,24},{4,28},{8,16},{12,20},{16,8},{20,12},{24,0},{28,4},{1,25},{... | collective-permute-start | bytes 589832 | tf_op jit(solution)/shard_map/ppermute | solution.py:15
  7.2 7.7 %collective-permute-start.1 = (bf16[48,1536]{1,0:T(8,128)(2,1)S(1)}, bf16[48,1536]{1,0:T(8,128)(2,1)S(1)}, u32[]{:S(2)}, u32[]{:S(2)}) collective-permute-start(bf16[48,1536]{1,0:T(8,128)(2,1)S(1)} %constant_dynamic-slice_fusion), channel_id=1, source_target_pairs={{0,2},{1,3},{2,0},{3,1},{4,6},{5,7},{6,4},{7,5},{8,10},{9,11},{10,... | collective-permute-start | bytes 442376 | tf_op jit(solution)/shard_map/ppermute | solution.py:15
  15.4 9.7 %collective-permute-start.4 = (bf16[3,48,1536]{2,1,0:T(8,128)(2,1)S(1)}, bf16[3,48,1536]{2,1,0:T(8,128)(2,1)S(1)}, u32[]{:S(2)}, u32[]{:S(2)}) collective-permute-start(bf16[3,48,1536]{2,1,0:T(8,128)(2,1)S(1)} %shard_map.86.refs_0_), channel_id=1, source_target_pairs={{0,16},{4,20},{8,24},{12,28},{16,0},{20,4},{24,8},{28,12},{1,17},{... | collective-permute-start | bytes 1327112 | tf_op jit(solution)/shard_map/ppermute | solution.py:15
  16.7 8.9 %collective-permute-start.3 = (bf16[3,48,1536]{2,1,0:T(8,128)(2,1)S(1)}, bf16[3,48,1536]{2,1,0:T(8,128)(2,1)S(1)}, u32[]{:S(2)}, u32[]{:S(2)}) collective-permute-start(bf16[3,48,1536]{2,1,0:T(8,128)(2,1)S(1)} %shard_map.86.refs_0_), channel_id=1, source_target_pairs={{0,8},{4,12},{8,0},{12,4},{16,24},{20,28},{24,16},{28,20},{1,9},{5... | collective-permute-start | bytes 1327112 | tf_op jit(solution)/shard_map/ppermute | solution.py:15
  20.5 16.8 %collective-permute-start.7 = (bf16[3,48,1536]{2,1,0:T(8,128)(2,1)S(1)}, bf16[3,48,1536]{2,1,0:T(8,128)(2,1)S(1)}, u32[]{:S(2)}, u32[]{:S(2)}) collective-permute-start(bf16[3,48,1536]{2,1,0:T(8,128)(2,1)S(1)} %shard_map.86.refs_0_), channel_id=1, source_target_pairs={{0,4},{4,0},{8,12},{12,8},{16,20},{20,16},{24,28},{28,24},{1,5},{5... | collective-permute-start | bytes 1327112 | tf_op jit(solution)/shard_map/ppermute | solution.py:15
  21.9 27.5 %collective-permute-start.21 = (bf16[1536,256]{1,0:T(8,128)(2,1)S(1)}, bf16[1536,256]{1,0:T(8,128)(2,1)S(1)}, u32[]{:S(2)}, u32[]{:S(2)}) collective-permute-start(bf16[1536,256]{1,0:T(8,128)(2,1)S(1)} %shard_map.96.refs_0_), channel_id=1, source_target_pairs={{0,1},{1,0},{2,3},{3,2},{4,5},{5,4},{6,7},{7,6},{8,9},{9,8},{10,11... | collective-permute-start | bytes 2359304 | tf_op jit(solution)/shard_map/ppermute | solution.py:15
  25.7 10.2 %collective-permute-start.14 = (bf16[2,192,256]{2,1,0:T(8,128)(2,1)S(1)}, bf16[2,192,256]{2,1,0:T(8,128)(2,1)S(1)}, u32[]{:S(2)}, u32[]{:S(2)}) collective-permute-start(bf16[2,192,256]{2,1,0:T(8,128)(2,1)S(1)} %get-tuple-element.41), channel_id=1, source_target_pairs={{0,24},{4,28},{8,16},{12,20},{16,8},{20,12},{24,0},{28,4},{1,25},{... | collective-permute-start | bytes 589832 | tf_op jit(solution)/shard_map/ppermute | solution.py:15
  30.8 10.7 %collective-permute-start.5 = (bf16[3,48,768]{2,1,0:T(8,128)(2,1)S(1)}, bf16[3,48,768]{2,1,0:T(8,128)(2,1)S(1)}, u32[]{:S(2)}, u32[]{:S(2)}) collective-permute-start(bf16[3,48,768]{2,1,0:T(8,128)(2,1)S(1)} %get-tuple-element.36), channel_id=1, source_target_pairs={{0,8},{4,12},{8,0},{12,4},{16,24},{20,28},{24,16},{28,20},{1,9},{5... | collective-permute-start | bytes 663560 | tf_op jit(solution)/shard_map/ppermute | solution.py:15
  32.1 14.1 %collective-permute-start.9 = (bf16[3,48,1536]{2,1,0:T(8,128)(2,1)S(1)}, bf16[3,48,1536]{2,1,0:T(8,128)(2,1)S(1)}, u32[]{:S(2)}, u32[]{:S(2)}) collective-permute-start(bf16[3,48,1536]{2,1,0:T(8,128)(2,1)S(1)} %collective-permute-done.4.by_y.refs_2_), channel_id=1, source_target_pairs={{0,4},{4,0},{8,12},{12,8},{16,20},{20,16},{24,28},{28,24},{1,5},{5... | collective-permute-start | bytes 1327112 | tf_op jit(solution)/shard_map/ppermute | solution.py:15
  37.3 9.9 %collective-permute-start.8 = (bf16[3,48,1536]{2,1,0:T(8,128)(2,1)S(1)}, bf16[3,48,1536]{2,1,0:T(8,128)(2,1)S(1)}, u32[]{:S(2)}, u32[]{:S(2)}) collective-permute-start(bf16[3,48,1536]{2,1,0:T(8,128)(2,1)S(1)} %collective-permute-done.3.by_x.refs_1_), channel_id=1, source_target_pairs={{0,4},{4,0},{8,12},{12,8},{16,20},{20,16},{24,28},{28,24},{1,5},{5... | collective-permute-start | bytes 1327112 | tf_op jit(solution)/shard_map/ppermute | solution.py:15
  48.9 43.9 %collective-permute-start.22 = (bf16[1536,256]{1,0:T(8,128)(2,1)S(1)}, bf16[1536,256]{1,0:T(8,128)(2,1)S(1)}, u32[]{:S(2)}, u32[]{:S(2)}) collective-permute-start(bf16[1536,256]{1,0:T(8,128)(2,1)S(1)} %shard_map.97.a0), channel_id=1, source_target_pairs={{0,4},{4,0},{8,12},{12,8},{16,20},{20,16},{24,28},{28,24},{1,5},{5... | collective-permute-start | bytes 2359304 | tf_op jit(solution)/shard_map/ppermute | solution.py:15
  50.8 42.1 %collective-permute-start.23 = (bf16[1536,256]{1,0:T(8,128)(2,1)S(1)}, bf16[1536,256]{1,0:T(8,128)(2,1)S(1)}, u32[]{:S(2)}, u32[]{:S(2)}) collective-permute-start(bf16[1536,256]{1,0:T(8,128)(2,1)S(1)} %shard_map.98.a1), channel_id=1, source_target_pairs={{0,4},{4,0},{8,12},{12,8},{16,20},{20,16},{24,28},{28,24},{1,5},{5... | collective-permute-start | bytes 2359304 | tf_op jit(solution)/shard_map/ppermute | solution.py:15
  51.1 37.6 %collective-permute-start.27 = (bf16[1536,128]{1,0:T(8,128)(2,1)S(1)}, bf16[1536,128]{1,0:T(8,128)(2,1)S(1)}, u32[]{:S(2)}, u32[]{:S(2)}) collective-permute-start(bf16[1536,128]{1,0:T(8,128)(2,1)S(1)} %get-tuple-element.43.refs_1_), channel_id=1, source_target_pairs={{0,3},{1,2},{2,1},{3,0},{4,7},{5,6},{6,5},{7,4},{8,11},{9,10},{10,... | collective-permute-start | bytes 1179656 | tf_op jit(solution)/shard_map/ppermute | solution.py:15
  52.5 37.6 %collective-permute-start.16 = (bf16[1536,128]{1,0:T(8,128)(2,1)S(1)}, bf16[1536,128]{1,0:T(8,128)(2,1)S(1)}, u32[]{:S(2)}, u32[]{:S(2)}) collective-permute-start(bf16[1536,128]{1,0:T(8,128)(2,1)S(1)} %get-tuple-element.42.refs_0_), channel_id=1, source_target_pairs={{0,3},{1,2},{2,1},{3,0},{4,7},{5,6},{6,5},{7,4},{8,11},{9,10},{10,... | collective-permute-start | bytes 1179656 | tf_op jit(solution)/shard_map/ppermute | solution.py:15
  58.8 28.1 %collective-permute-start.26 = (f32[256]{0:T(256)S(1)}, f32[256]{0:T(256)S(1)}, u32[]{:S(2)}, u32[]{:S(2)}) collective-permute-start(f32[256]{0:T(256)S(1)} %copy-done.4), channel_id=1, source_target_pairs={{0,3},{1,2},{2,1},{3,0},{4,7},{5,6},{6,5},{7,4},{8,11},{9,10},{10,... | collective-permute-start | bytes 3080 | tf_op jit(solution)/shard_map/ppermute | solution.py:15
  101.7 10.6 %collective-permute-start.30 = (bf16[1536,128]{1,0:T(8,128)(2,1)S(1)}, bf16[1536,128]{1,0:T(8,128)(2,1)S(1)}, u32[]{:S(2)}, u32[]{:S(2)}) collective-permute-start(bf16[1536,128]{1,0:T(8,128)(2,1)S(1)} %get-tuple-element.59), channel_id=1, source_target_pairs={{0,3},{1,2},{2,1},{3,0},{4,7},{5,6},{6,5},{7,4},{8,11},{9,10},{10,... | collective-permute-start | bytes 1179656 | tf_op jit(solution)/shard_map/ppermute | solution.py:376
  105.5 8.8 %collective-permute-start.32 = (bf16[1536,128]{1,0:T(8,128)(2,1)S(1)}, bf16[1536,128]{1,0:T(8,128)(2,1)S(1)}, u32[]{:S(2)}, u32[]{:S(2)}) collective-permute-start(bf16[1536,128]{1,0:T(8,128)(2,1)S(1)} %get-tuple-element.63), channel_id=1, source_target_pairs={{0,3},{1,2},{2,1},{3,0},{4,5},{5,4},{6,7},{7,6},{8,11},{9,10},{10,... | collective-permute-start | bytes 1179656 | tf_op jit(solution)/shard_map/ppermute | solution.py:376
  105.6 17.1 %collective-permute-start.31 = (bf16[1536,128]{1,0:T(8,128)(2,1)S(1)}, bf16[1536,128]{1,0:T(8,128)(2,1)S(1)}, u32[]{:S(2)}, u32[]{:S(2)}) collective-permute-start(bf16[1536,128]{1,0:T(8,128)(2,1)S(1)} %get-tuple-element.61), channel_id=1, source_target_pairs={{0,1},{1,0},{2,3},{3,2},{4,5},{5,4},{6,7},{7,6},{8,9},{9,8},{10,11... | collective-permute-start | bytes 1179656 | tf_op jit(solution)/shard_map/ppermute | solution.py:376
  112.4 12.0 %collective-permute-start.29 = (bf16[1536,128]{1,0:T(8,128)(2,1)S(1)}, bf16[1536,128]{1,0:T(8,128)(2,1)S(1)}, u32[]{:S(2)}, u32[]{:S(2)}) collective-permute-start(bf16[1536,128]{1,0:T(8,128)(2,1)S(1)} %get-tuple-element.58), channel_id=1, source_target_pairs={{0,1},{1,0},{2,3},{3,2},{4,7},{5,6},{6,5},{7,4},{8,9},{9,8},{10,11... | collective-permute-start | bytes 1179656 | tf_op jit(solution)/shard_map/ppermute | solution.py:376
  122.9 11.2 %collective-permute-start.34 = (bf16[1536,128]{1,0:T(8,128)(2,1)S(1)}, bf16[1536,128]{1,0:T(8,128)(2,1)S(1)}, u32[]{:S(2)}, u32[]{:S(2)}) collective-permute-start(bf16[1536,128]{1,0:T(8,128)(2,1)S(1)} %get-tuple-element.67), channel_id=1, source_target_pairs={{0,8},{4,12},{8,0},{12,4},{16,24},{20,28},{24,16},{28,20},{1,9},{5... | collective-permute-start | bytes 1179656 | tf_op jit(solution)/shard_map/ppermute | solution.py:15
  123.0 16.4 %collective-permute-start.33 = (bf16[1536,128]{1,0:T(8,128)(2,1)S(1)}, bf16[1536,128]{1,0:T(8,128)(2,1)S(1)}, u32[]{:S(2)}, u32[]{:S(2)}) collective-permute-start(bf16[1536,128]{1,0:T(8,128)(2,1)S(1)} %get-tuple-element.66), channel_id=1, source_target_pairs={{0,8},{4,12},{8,0},{12,4},{16,24},{20,28},{24,16},{28,20},{1,9},{5... | collective-permute-start | bytes 1179656 | tf_op jit(solution)/shard_map/ppermute | solution.py:15
  (17 other events, 174.3 us)

commit v3 on v2

--- a/solution.py
+++ b/solution.py
@@ -300,28 +300,39 @@
     send[...] = jnp.where(odd, total, second[...])
 
 
-def last_rows(keep, got, first, third, move_a, move_b, alpha, beta):
+def last_rows(keep, got, first, third, move_a, move_b, alpha, beta, hold_a, hold_b, sems):
     odd = lax.axis_index("occ") % 2 == 1
-    half = keep.shape[1]
-    final = (keep[...] + got[...].astype(F32)).astype(BF16)
-    side = jnp.where(odd, first[...], third[...])
-    a, b = move_a[...], move_b[...]
-    alpha[:, :half] = jnp.where(odd, a, side)
-    alpha[:, half:] = jnp.where(odd, b, final)
-    beta[:, :half] = jnp.where(odd, side, a)
-    beta[:, half:] = jnp.where(odd, final, b)
+    aux, half = keep.shape
+    step = aux // sems.shape[1]
+    copies = []
+    for i, start in enumerate(range(0, aux, step)):
+        rows = slice(start, start + step)
+        final = (keep[rows, :] + got[rows, :].astype(F32)).astype(BF16)
+        side = jnp.where(odd, first[rows, :], third[rows, :])
+        a, b = move_a[rows, :], move_b[rows, :]
+        hold_a[rows, :half] = jnp.where(odd, a, side)
+        hold_a[rows, half:] = jnp.where(odd, b, final)
+        hold_b[rows, :half] = jnp.where(odd, side, a)
+        hold_b[rows, half:] = jnp.where(odd, final, b)
+        for j, (hold, out) in enumerate(((hold_a, alpha), (hold_b, beta))):
+            copy = pltpu.make_async_copy(hold.at[rows, :], out.at[rows, :], sems.at[j, i])
+            copy.start()
+            copies.append(copy)
+    for copy in copies:
+        copy.wait()
 
 
 def last(*arrays):
     aux, half = arrays[0].shape
-    step = 256 if aux % 256 == 0 else aux
-    spec = lambda width: pl.BlockSpec((step, width), lambda i: (i, 0))
+    parts = 3
+    anywhere = pl.BlockSpec(memory_space=pl.ANY)
     return pl.pallas_call(
         last_rows,
-        grid=(aux // step,),
         out_shape=[shape_of(aux, 2 * half)] * 2,
-        in_specs=[spec(half)] * len(arrays),
-        out_specs=[spec(2 * half)] * 2,
+        in_specs=[VMEM] * len(arrays),
+        out_specs=[anywhere] * 2,
+        scratch_shapes=[pltpu.VMEM((aux, 2 * half), BF16)] * 2
+        + [pltpu.SemaphoreType.DMA((2, parts))],
         compiler_params=pltpu.CompilerParams(vmem_limit_bytes=8 << 20),
     )(*arrays)
 

time: 142 us -> 141 us (level)
  no operation moved by 1% of the time
where the time goes in v3:
time: 141 us
  waiting for transfers between devices  75.3 us (53%)
  starting transfers between devices  42.3 us (30%)
  Pallas kernels  20.1 us (14%)
  local copies, waits for them, and re-layouts  2.09 us (1%)
    ppermute x30, waiting for transfers between devices, swap(): return lax.ppermute(value, axis, pairs)  58.6 us
    ppermute x30, starting transfers between devices, swap(): return lax.ppermute(value, axis, pairs)  36 us
    pallas_call x24, Pallas kernels, call(): pl.pallas_call(kernel, out_shape=shapes, in_specs=specs or [VMEM] * len(a...  18.8 us
    ppermute x4, waiting for transfers between devices, back(): return lax.ppermute(send, ('occ', 'vir'), pairs)  14.1 us
    ppermute x4, starting transfers between devices, back(): return lax.ppermute(send, ('occ', 'vir'), pairs)  4.2 us
  transfers between devices with their start and end apart: 35, of which 15 were waited for; matrix products, arithmetic and copies ran while one was open for 0% of the time, Pallas kernels for 8%

profile of v3, /device:TPU:11, one launch (start us, length us, event | category | flops | bytes accessed | tf_op | source)
XLA Modules:
  0.0 140.9 jit_solution(8093155064066631081)
XLA Ops:
  8.2 1.5 %collective-permute-done.2.refs_2_ = bf16[48,1536]{1,0:T(8,128)(2,1)S(1)} collective-permute-done((bf16[48,1536]{1,0:T(8,128)(2,1)S(1)}, bf16[48,1536]{1,0:T(8,128)(2,1)S(1)}, u32[]{:S(2)}, u32[]{:S(2)}) %collective-permute-start.2) | collective-permute-done | bytes 147488 | tf_op jit(solution)/shard_map/ppermute | solution.py:15
  9.7 5.2 %collective-permute-done.1.refs_1_ = bf16[48,1536]{1,0:T(8,128)(2,1)S(1)} collective-permute-done((bf16[48,1536]{1,0:T(8,128)(2,1)S(1)}, bf16[48,1536]{1,0:T(8,128)(2,1)S(1)}, u32[]{:S(2)}, u32[]{:S(2)}) %collective-permute-start.1) | collective-permute-done | bytes 147488 | tf_op jit(solution)/shard_map/ppermute | solution.py:15
  17.1 3.4 %collective-permute-start.20 = (bf16[4,192,256]{2,1,0:T(8,128)(2,1)S(1)}, bf16[4,192,256]{2,1,0:T(8,128)(2,1)S(1)}, u32[]{:S(2)}, u32[]{:S(2)}) collective-permute-start(bf16[4,192,256]{2,1,0:T(8,128)(2,1)S(1)} %shard_map.95), channel_id=1, source_target_pairs={{0,4},{4,0},{8,12},{12,8},{16,20},{20,16},{24,28},{28,24},{1,5},{5... | collective-permute-start | bytes 1179656 | tf_op jit(solution)/shard_map/ppermute | solution.py:15
  21.9 1.5 %collective-permute-start.21 = (bf16[1536,256]{1,0:T(8,128)(2,1)S(1)}, bf16[1536,256]{1,0:T(8,128)(2,1)S(1)}, u32[]{:S(2)}, u32[]{:S(2)}) collective-permute-start(bf16[1536,256]{1,0:T(8,128)(2,1)S(1)} %shard_map.96.refs_0_), channel_id=1, source_target_pairs={{0,1},{1,0},{2,3},{3,2},{4,5},{5,4},{6,7},{7,6},{8,9},{9,8},{10,11... | collective-permute-start | bytes 2359304 | tf_op jit(solution)/shard_map/ppermute | solution.py:15
  26.6 4.2 %collective-permute-done.12.refs_1_ = bf16[2,192,256]{2,1,0:T(8,128)(2,1)S(1)} collective-permute-done((bf16[2,192,256]{2,1,0:T(8,128)(2,1)S(1)}, bf16[2,192,256]{2,1,0:T(8,128)(2,1)S(1)}, u32[]{:S(2)}, u32[]{:S(2)}) %collective-permute-start.12) | collective-permute-done | bytes 196640 | tf_op jit(solution)/shard_map/ppermute | solution.py:15
  32.1 3.8 %collective-permute-start.9 = (bf16[3,48,1536]{2,1,0:T(8,128)(2,1)S(1)}, bf16[3,48,1536]{2,1,0:T(8,128)(2,1)S(1)}, u32[]{:S(2)}, u32[]{:S(2)}) collective-permute-start(bf16[3,48,1536]{2,1,0:T(8,128)(2,1)S(1)} %collective-permute-done.4.by_y.refs_2_), channel_id=1, source_target_pairs={{0,4},{4,0},{8,12},{12,8},{16,20},{20,16},{24,28},{28,24},{1,5},{5... | collective-permute-start | bytes 1327112 | tf_op jit(solution)/shard_map/ppermute | solution.py:15
  35.8 1.4 %collective-permute-start.6 = (bf16[3,48,768]{2,1,0:T(8,128)(2,1)S(1)}, bf16[3,48,768]{2,1,0:T(8,128)(2,1)S(1)}, u32[]{:S(2)}, u32[]{:S(2)}) collective-permute-start(bf16[3,48,768]{2,1,0:T(8,128)(2,1)S(1)} %get-tuple-element.37), channel_id=1, source_target_pairs={{0,16},{4,20},{8,24},{12,28},{16,0},{20,4},{24,8},{28,12},{1,17},{... | collective-permute-start | bytes 663560 | tf_op jit(solution)/shard_map/ppermute | solution.py:15
  37.3 4.2 %collective-permute-start.8 = (bf16[3,48,1536]{2,1,0:T(8,128)(2,1)S(1)}, bf16[3,48,1536]{2,1,0:T(8,128)(2,1)S(1)}, u32[]{:S(2)}, u32[]{:S(2)}) collective-permute-start(bf16[3,48,1536]{2,1,0:T(8,128)(2,1)S(1)} %collective-permute-done.3.by_x.refs_1_), channel_id=1, source_target_pairs={{0,4},{4,0},{8,12},{12,8},{16,20},{20,16},{24,28},{28,24},{1,5},{5... | collective-permute-start | bytes 1327112 | tf_op jit(solution)/shard_map/ppermute | solution.py:15
  42.5 3.6 %collective-permute-start.11 = (bf16[3,48,768]{2,1,0:T(8,128)(2,1)S(1)}, bf16[3,48,768]{2,1,0:T(8,128)(2,1)S(1)}, u32[]{:S(2)}, u32[]{:S(2)}) collective-permute-start(bf16[3,48,768]{2,1,0:T(8,128)(2,1)S(1)} %collective-permute-done.6.refs_4_), channel_id=1, source_target_pairs={{0,4},{4,0},{8,12},{12,8},{16,20},{20,16},{24,28},{28,24},{1,5},{5... | collective-permute-start | bytes 663560 | tf_op jit(solution)/shard_map/ppermute | solution.py:15
  52.7 2.1 %collective-permute-start.24 = (f32[1]{0:T(128)}, f32[1]{0:T(128)}, u32[]{:S(2)}, u32[]{:S(2)}) collective-permute-start(f32[1]{0:T(128)} %param.10), channel_id=1, source_target_pairs={{0,0},{12,4},{8,8},{4,12},{16,16},{28,20},{24,24},{20,28},{1,1},{1... | collective-permute-start | bytes 20 | tf_op jit(solution)/shard_map/ppermute | solution.py:351
  54.8 2.6 %collective-permute-done.24.occ_a = f32[1]{0:T(128)} collective-permute-done((f32[1]{0:T(128)}, f32[1]{0:T(128)}, u32[]{:S(2)}, u32[]{:S(2)}) %collective-permute-start.24) | collective-permute-done | bytes 36 | tf_op jit(solution)/shard_map/ppermute | solution.py:351
  60.1 26.8 %collective-permute-done.26 = f32[256]{0:T(256)S(1)} collective-permute-done((f32[256]{0:T(256)S(1)}, f32[256]{0:T(256)S(1)}, u32[]{:S(2)}, u32[]{:S(2)}) %collective-permute-start.26) | collective-permute-done | bytes 1056 | tf_op jit(solution)/shard_map/ppermute | solution.py:15
  86.8 1.9 %shard_map.99 = (f32[4,256]{1,0:T(4,128)S(1)}, f32[256,128]{1,0:T(8,128)S(1)}, f32[128,128]{1,0:T(8,128)S(1)}, f32[128,128]{1,0:T(8,128)S(1)}) custom-call(f32[1]{0:T(128)} %collective-permute-done.24.occ_a, f32[1]{0:T(128)} %collective-permute-done.25.occ_o, f32[8]{0:T(128)S(1)} %copy-done.5, f32[1024]{0:T(1024)S(1)} %copy-done.3, f32[1,256]{1,0:T(1,128)S(1)} %bitcast.4, ...), custom_call_target="tpu_custom_call" | custom-call | bytes 1048576 | tf_op jit(solution)/shard_map/pallas_call | solution.py:31
  92.9 1.5 %shard_map.101 = (bf16[4,128,256]{2,1,0:T(8,128)(2,1)S(1)}, bf16[1536,128]{1,0:T(8,128)(2,1)S(1)}) custom-call(bf16[1536,256]{1,0:T(8,128)(2,1)S(1)} %shard_map.97.a0, bf16[1536,256]{1,0:T(8,128)(2,1)S(1)} %shard_map.98.a1, bf16[1536,256]{1,0:T(8,128)(2,1)S(1)} %collective-permute-done.22.o0, bf16[1536,256]{1,0:T(8,128)(2,1)S(1)} %collective-permute-done.23.o1, ...), custom_call_target="tpu_custom_call" | custom-call | flops 805306368 | bytes 1048576 | tf_op jit(solution)/shard_map/pallas_call | solution.py:31
  94.5 1.9 %shard_map.100 = (bf16[4,256,256]{2,1,0:T(8,128)(2,1)S(1)}, f32[1536,256]{1,0:T(8,128)S(1)}) custom-call(bf16[1536,256]{1,0:T(8,128)(2,1)S(1)} %shard_map.97.a0, bf16[1536,256]{1,0:T(8,128)(2,1)S(1)} %shard_map.98.a1, bf16[1536,256]{1,0:T(8,128)(2,1)S(1)} %collective-permute-done.22.o0, bf16[1536,256]{1,0:T(8,128)(2,1)S(1)} %collective-permute-done.23.o1, ...), custom_call_target="tpu_custom_call" | custom-call | flops 1610612736 | bytes 1048576 | tf_op jit(solution)/shard_map/pallas_call | solution.py:31
  96.4 1.8 %shard_map.102.early = f32[1536,1024]{1,0:T(8,128)S(1)} custom-call(bf16[1536,256]{1,0:T(8,128)(2,1)S(1)} %shard_map.92.beta.own, bf16[1536,128]{1,0:T(8,128)(2,1)S(1)} %shard_map.93.beta.near, bf16[4,256,256]{2,1,0:T(8,128)(2,1)S(1)} %get-tuple-element.50.amp_own, bf16[4,128,256]{2,1,0:T(8,128)(2,1)S(1)} %get-tuple-element.52.amp_near), custom_call_target="tpu_custom_call" | custom-call | flops 1207959552 | bytes 1048576 | tf_op jit(solution)/shard_map/pallas_call | solution.py:31
  98.2 1.6 %shard_map.104 = (bf16[4,128,256]{2,1,0:T(8,128)(2,1)S(1)}, bf16[1536,128]{1,0:T(8,128)(2,1)S(1)}) custom-call(bf16[1536,256]{1,0:T(8,128)(2,1)S(1)} %shard_map.97.a0, bf16[1536,256]{1,0:T(8,128)(2,1)S(1)} %shard_map.98.a1, bf16[1536,256]{1,0:T(8,128)(2,1)S(1)} %collective-permute-done.22.o0, bf16[1536,256]{1,0:T(8,128)(2,1)S(1)} %collective-permute-done.23.o1, ...), custom_call_target="tpu_custom_call" | custom-call | flops 805306368 | bytes 1048576 | tf_op jit(solution)/shard_map/pallas_call | solution.py:31
  103.0 1.7 %collective-permute-done.28.core_term = bf16[1536,512]{1,0:T(8,128)(2,1)S(1)} collective-permute-done((bf16[1536,512]{1,0:T(8,128)(2,1)S(1)}, bf16[1536,512]{1,0:T(8,128)(2,1)S(1)}, u32[]{:S(2)}, u32[]{:S(2)}) %collective-permute-start.28) | collective-permute-done | bytes 1572896 | tf_op jit(solution)/shard_map/ppermute | solution.py:15
  105.6 1.5 %collective-permute-start.31 = (bf16[1536,128]{1,0:T(8,128)(2,1)S(1)}, bf16[1536,128]{1,0:T(8,128)(2,1)S(1)}, u32[]{:S(2)}, u32[]{:S(2)}) collective-permute-start(bf16[1536,128]{1,0:T(8,128)(2,1)S(1)} %get-tuple-element.61), channel_id=1, source_target_pairs={{0,1},{1,0},{2,3},{3,2},{4,5},{5,4},{6,7},{7,6},{8,9},{9,8},{10,11... | collective-permute-start | bytes 1179656 | tf_op jit(solution)/shard_map/ppermute | solution.py:387
  107.1 5.2 %collective-permute-done.30.got = bf16[1536,128]{1,0:T(8,128)(2,1)S(1)} collective-permute-done((bf16[1536,128]{1,0:T(8,128)(2,1)S(1)}, bf16[1536,128]{1,0:T(8,128)(2,1)S(1)}, u32[]{:S(2)}, u32[]{:S(2)}) %collective-permute-start.30) | collective-permute-done | bytes 393248 | tf_op jit(solution)/shard_map/ppermute | solution.py:387
  114.4 8.3 %collective-permute-done.31.got = bf16[1536,128]{1,0:T(8,128)(2,1)S(1)} collective-permute-done((bf16[1536,128]{1,0:T(8,128)(2,1)S(1)}, bf16[1536,128]{1,0:T(8,128)(2,1)S(1)}, u32[]{:S(2)}, u32[]{:S(2)}) %collective-permute-start.31) | collective-permute-done | bytes 393248 | tf_op jit(solution)/shard_map/ppermute | solution.py:387
  123.0 1.4 collective-permute-start.33
  124.4 9.7 %collective-permute-done.34.move_b = bf16[1536,128]{1,0:T(8,128)(2,1)S(1)} collective-permute-done((bf16[1536,128]{1,0:T(8,128)(2,1)S(1)}, bf16[1536,128]{1,0:T(8,128)(2,1)S(1)}, u32[]{:S(2)}, u32[]{:S(2)}) %collective-permute-start.34) | collective-permute-done | bytes 393248 | tf_op jit(solution)/shard_map/ppermute | solution.py:15
  134.1 5.4 %collective-permute-done.33.move_a = bf16[1536,128]{1,0:T(8,128)(2,1)S(1)} collective-permute-done((bf16[1536,128]{1,0:T(8,128)(2,1)S(1)}, bf16[1536,128]{1,0:T(8,128)(2,1)S(1)}, u32[]{:S(2)}, u32[]{:S(2)}) %collective-permute-start.33) | collective-permute-done | bytes 393248 | tf_op jit(solution)/shard_map/ppermute | solution.py:15
  (84 shorter events, 37.6 us)
Async XLA Ops:
  1.6 8.1 %collective-permute-start.2 = (bf16[48,1536]{1,0:T(8,128)(2,1)S(1)}, bf16[48,1536]{1,0:T(8,128)(2,1)S(1)}, u32[]{:S(2)}, u32[]{:S(2)}) collective-permute-start(bf16[48,1536]{1,0:T(8,128)(2,1)S(1)} %constant_dynamic-slice_fusion), channel_id=1, source_target_pairs={{0,3},{1,2},{2,1},{3,0},{4,7},{5,6},{6,5},{7,4},{8,11},{9,10},{10,... | collective-permute-start | bytes 442376 | tf_op jit(solution)/shard_map/ppermute | solution.py:15
  4.5 12.5 %collective-permute-start.17 = (bf16[2,192,256]{2,1,0:T(8,128)(2,1)S(1)}, bf16[2,192,256]{2,1,0:T(8,128)(2,1)S(1)}, u32[]{:S(2)}, u32[]{:S(2)}) collective-permute-start(bf16[2,192,256]{2,1,0:T(8,128)(2,1)S(1)} %get-tuple-element.45), channel_id=1, source_target_pairs={{0,8},{4,12},{8,0},{12,4},{16,24},{20,28},{24,16},{28,20},{1,9},{5... | collective-permute-start | bytes 589832 | tf_op jit(solution)/shard_map/ppermute | solution.py:15
  4.8 12.2 %collective-permute-start.18 = (bf16[2,192,256]{2,1,0:T(8,128)(2,1)S(1)}, bf16[2,192,256]{2,1,0:T(8,128)(2,1)S(1)}, u32[]{:S(2)}, u32[]{:S(2)}) collective-permute-start(bf16[2,192,256]{2,1,0:T(8,128)(2,1)S(1)} %get-tuple-element.46), channel_id=1, source_target_pairs={{0,16},{4,20},{8,24},{12,28},{16,0},{20,4},{24,8},{28,12},{1,17},{... | collective-permute-start | bytes 589832 | tf_op jit(solution)/shard_map/ppermute | solution.py:15
  6.0 11.0 %collective-permute-start.19 = (bf16[2,192,256]{2,1,0:T(8,128)(2,1)S(1)}, bf16[2,192,256]{2,1,0:T(8,128)(2,1)S(1)}, u32[]{:S(2)}, u32[]{:S(2)}) collective-permute-start(bf16[2,192,256]{2,1,0:T(8,128)(2,1)S(1)} %get-tuple-element.47), channel_id=1, source_target_pairs={{0,24},{4,28},{8,16},{12,20},{16,8},{20,12},{24,0},{28,4},{1,25},{... | collective-permute-start | bytes 589832 | tf_op jit(solution)/shard_map/ppermute | solution.py:15
  7.2 7.7 %collective-permute-start.1 = (bf16[48,1536]{1,0:T(8,128)(2,1)S(1)}, bf16[48,1536]{1,0:T(8,128)(2,1)S(1)}, u32[]{:S(2)}, u32[]{:S(2)}) collective-permute-start(bf16[48,1536]{1,0:T(8,128)(2,1)S(1)} %constant_dynamic-slice_fusion), channel_id=1, source_target_pairs={{0,2},{1,3},{2,0},{3,1},{4,6},{5,7},{6,4},{7,5},{8,10},{9,11},{10,... | collective-permute-start | bytes 442376 | tf_op jit(solution)/shard_map/ppermute | solution.py:15
  15.4 9.7 %collective-permute-start.4 = (bf16[3,48,1536]{2,1,0:T(8,128)(2,1)S(1)}, bf16[3,48,1536]{2,1,0:T(8,128)(2,1)S(1)}, u32[]{:S(2)}, u32[]{:S(2)}) collective-permute-start(bf16[3,48,1536]{2,1,0:T(8,128)(2,1)S(1)} %shard_map.86.refs_0_), channel_id=1, source_target_pairs={{0,16},{4,20},{8,24},{12,28},{16,0},{20,4},{24,8},{28,12},{1,17},{... | collective-permute-start | bytes 1327112 | tf_op jit(solution)/shard_map/ppermute | solution.py:15
  16.7 8.9 %collective-permute-start.3 = (bf16[3,48,1536]{2,1,0:T(8,128)(2,1)S(1)}, bf16[3,48,1536]{2,1,0:T(8,128)(2,1)S(1)}, u32[]{:S(2)}, u32[]{:S(2)}) collective-permute-start(bf16[3,48,1536]{2,1,0:T(8,128)(2,1)S(1)} %shard_map.86.refs_0_), channel_id=1, source_target_pairs={{0,8},{4,12},{8,0},{12,4},{16,24},{20,28},{24,16},{28,20},{1,9},{5... | collective-permute-start | bytes 1327112 | tf_op jit(solution)/shard_map/ppermute | solution.py:15
  20.5 16.8 %collective-permute-start.7 = (bf16[3,48,1536]{2,1,0:T(8,128)(2,1)S(1)}, bf16[3,48,1536]{2,1,0:T(8,128)(2,1)S(1)}, u32[]{:S(2)}, u32[]{:S(2)}) collective-permute-start(bf16[3,48,1536]{2,1,0:T(8,128)(2,1)S(1)} %shard_map.86.refs_0_), channel_id=1, source_target_pairs={{0,4},{4,0},{8,12},{12,8},{16,20},{20,16},{24,28},{28,24},{1,5},{5... | collective-permute-start | bytes 1327112 | tf_op jit(solution)/shard_map/ppermute | solution.py:15
  21.9 27.5 %collective-permute-start.21 = (bf16[1536,256]{1,0:T(8,128)(2,1)S(1)}, bf16[1536,256]{1,0:T(8,128)(2,1)S(1)}, u32[]{:S(2)}, u32[]{:S(2)}) collective-permute-start(bf16[1536,256]{1,0:T(8,128)(2,1)S(1)} %shard_map.96.refs_0_), channel_id=1, source_target_pairs={{0,1},{1,0},{2,3},{3,2},{4,5},{5,4},{6,7},{7,6},{8,9},{9,8},{10,11... | collective-permute-start | bytes 2359304 | tf_op jit(solution)/shard_map/ppermute | solution.py:15
  25.7 10.2 %collective-permute-start.14 = (bf16[2,192,256]{2,1,0:T(8,128)(2,1)S(1)}, bf16[2,192,256]{2,1,0:T(8,128)(2,1)S(1)}, u32[]{:S(2)}, u32[]{:S(2)}) collective-permute-start(bf16[2,192,256]{2,1,0:T(8,128)(2,1)S(1)} %get-tuple-element.41), channel_id=1, source_target_pairs={{0,24},{4,28},{8,16},{12,20},{16,8},{20,12},{24,0},{28,4},{1,25},{... | collective-permute-start | bytes 589832 | tf_op jit(solution)/shard_map/ppermute | solution.py:15
  30.8 10.7 %collective-permute-start.5 = (bf16[3,48,768]{2,1,0:T(8,128)(2,1)S(1)}, bf16[3,48,768]{2,1,0:T(8,128)(2,1)S(1)}, u32[]{:S(2)}, u32[]{:S(2)}) collective-permute-start(bf16[3,48,768]{2,1,0:T(8,128)(2,1)S(1)} %get-tuple-element.36), channel_id=1, source_target_pairs={{0,8},{4,12},{8,0},{12,4},{16,24},{20,28},{24,16},{28,20},{1,9},{5... | collective-permute-start | bytes 663560 | tf_op jit(solution)/shard_map/ppermute | solution.py:15
  32.1 14.1 %collective-permute-start.9 = (bf16[3,48,1536]{2,1,0:T(8,128)(2,1)S(1)}, bf16[3,48,1536]{2,1,0:T(8,128)(2,1)S(1)}, u32[]{:S(2)}, u32[]{:S(2)}) collective-permute-start(bf16[3,48,1536]{2,1,0:T(8,128)(2,1)S(1)} %collective-permute-done.4.by_y.refs_2_), channel_id=1, source_target_pairs={{0,4},{4,0},{8,12},{12,8},{16,20},{20,16},{24,28},{28,24},{1,5},{5... | collective-permute-start | bytes 1327112 | tf_op jit(solution)/shard_map/ppermute | solution.py:15
  37.3 9.9 %collective-permute-start.8 = (bf16[3,48,1536]{2,1,0:T(8,128)(2,1)S(1)}, bf16[3,48,1536]{2,1,0:T(8,128)(2,1)S(1)}, u32[]{:S(2)}, u32[]{:S(2)}) collective-permute-start(bf16[3,48,1536]{2,1,0:T(8,128)(2,1)S(1)} %collective-permute-done.3.by_x.refs_1_), channel_id=1, source_target_pairs={{0,4},{4,0},{8,12},{12,8},{16,20},{20,16},{24,28},{28,24},{1,5},{5... | collective-permute-start | bytes 1327112 | tf_op jit(solution)/shard_map/ppermute | solution.py:15
  48.9 43.9 %collective-permute-start.22 = (bf16[1536,256]{1,0:T(8,128)(2,1)S(1)}, bf16[1536,256]{1,0:T(8,128)(2,1)S(1)}, u32[]{:S(2)}, u32[]{:S(2)}) collective-permute-start(bf16[1536,256]{1,0:T(8,128)(2,1)S(1)} %shard_map.97.a0), channel_id=1, source_target_pairs={{0,4},{4,0},{8,12},{12,8},{16,20},{20,16},{24,28},{28,24},{1,5},{5... | collective-permute-start | bytes 2359304 | tf_op jit(solution)/shard_map/ppermute | solution.py:15
  50.8 42.1 %collective-permute-start.23 = (bf16[1536,256]{1,0:T(8,128)(2,1)S(1)}, bf16[1536,256]{1,0:T(8,128)(2,1)S(1)}, u32[]{:S(2)}, u32[]{:S(2)}) collective-permute-start(bf16[1536,256]{1,0:T(8,128)(2,1)S(1)} %shard_map.98.a1), channel_id=1, source_target_pairs={{0,4},{4,0},{8,12},{12,8},{16,20},{20,16},{24,28},{28,24},{1,5},{5... | collective-permute-start | bytes 2359304 | tf_op jit(solution)/shard_map/ppermute | solution.py:15
  51.1 37.6 %collective-permute-start.27 = (bf16[1536,128]{1,0:T(8,128)(2,1)S(1)}, bf16[1536,128]{1,0:T(8,128)(2,1)S(1)}, u32[]{:S(2)}, u32[]{:S(2)}) collective-permute-start(bf16[1536,128]{1,0:T(8,128)(2,1)S(1)} %get-tuple-element.43.refs_1_), channel_id=1, source_target_pairs={{0,3},{1,2},{2,1},{3,0},{4,7},{5,6},{6,5},{7,4},{8,11},{9,10},{10,... | collective-permute-start | bytes 1179656 | tf_op jit(solution)/shard_map/ppermute | solution.py:15
  52.5 37.6 %collective-permute-start.16 = (bf16[1536,128]{1,0:T(8,128)(2,1)S(1)}, bf16[1536,128]{1,0:T(8,128)(2,1)S(1)}, u32[]{:S(2)}, u32[]{:S(2)}) collective-permute-start(bf16[1536,128]{1,0:T(8,128)(2,1)S(1)} %get-tuple-element.42.refs_0_), channel_id=1, source_target_pairs={{0,3},{1,2},{2,1},{3,0},{4,7},{5,6},{6,5},{7,4},{8,11},{9,10},{10,... | collective-permute-start | bytes 1179656 | tf_op jit(solution)/shard_map/ppermute | solution.py:15
  58.8 28.1 %collective-permute-start.26 = (f32[256]{0:T(256)S(1)}, f32[256]{0:T(256)S(1)}, u32[]{:S(2)}, u32[]{:S(2)}) collective-permute-start(f32[256]{0:T(256)S(1)} %copy-done.4), channel_id=1, source_target_pairs={{0,3},{1,2},{2,1},{3,0},{4,7},{5,6},{6,5},{7,4},{8,11},{9,10},{10,... | collective-permute-start | bytes 3080 | tf_op jit(solution)/shard_map/ppermute | solution.py:15
  101.7 10.6 %collective-permute-start.30 = (bf16[1536,128]{1,0:T(8,128)(2,1)S(1)}, bf16[1536,128]{1,0:T(8,128)(2,1)S(1)}, u32[]{:S(2)}, u32[]{:S(2)}) collective-permute-start(bf16[1536,128]{1,0:T(8,128)(2,1)S(1)} %get-tuple-element.59), channel_id=1, source_target_pairs={{0,3},{1,2},{2,1},{3,0},{4,7},{5,6},{6,5},{7,4},{8,11},{9,10},{10,... | collective-permute-start | bytes 1179656 | tf_op jit(solution)/shard_map/ppermute | solution.py:387
  105.5 8.8 %collective-permute-start.32 = (bf16[1536,128]{1,0:T(8,128)(2,1)S(1)}, bf16[1536,128]{1,0:T(8,128)(2,1)S(1)}, u32[]{:S(2)}, u32[]{:S(2)}) collective-permute-start(bf16[1536,128]{1,0:T(8,128)(2,1)S(1)} %get-tuple-element.63), channel_id=1, source_target_pairs={{0,3},{1,2},{2,1},{3,0},{4,5},{5,4},{6,7},{7,6},{8,11},{9,10},{10,... | collective-permute-start | bytes 1179656 | tf_op jit(solution)/shard_map/ppermute | solution.py:387
  105.6 17.1 %collective-permute-start.31 = (bf16[1536,128]{1,0:T(8,128)(2,1)S(1)}, bf16[1536,128]{1,0:T(8,128)(2,1)S(1)}, u32[]{:S(2)}, u32[]{:S(2)}) collective-permute-start(bf16[1536,128]{1,0:T(8,128)(2,1)S(1)} %get-tuple-element.61), channel_id=1, source_target_pairs={{0,1},{1,0},{2,3},{3,2},{4,5},{5,4},{6,7},{7,6},{8,9},{9,8},{10,11... | collective-permute-start | bytes 1179656 | tf_op jit(solution)/shard_map/ppermute | solution.py:387
  112.4 12.0 %collective-permute-start.29 = (bf16[1536,128]{1,0:T(8,128)(2,1)S(1)}, bf16[1536,128]{1,0:T(8,128)(2,1)S(1)}, u32[]{:S(2)}, u32[]{:S(2)}) collective-permute-start(bf16[1536,128]{1,0:T(8,128)(2,1)S(1)} %get-tuple-element.58), channel_id=1, source_target_pairs={{0,1},{1,0},{2,3},{3,2},{4,7},{5,6},{6,5},{7,4},{8,9},{9,8},{10,11... | collective-permute-start | bytes 1179656 | tf_op jit(solution)/shard_map/ppermute | solution.py:387
  122.9 11.2 %collective-permute-start.34 = (bf16[1536,128]{1,0:T(8,128)(2,1)S(1)}, bf16[1536,128]{1,0:T(8,128)(2,1)S(1)}, u32[]{:S(2)}, u32[]{:S(2)}) collective-permute-start(bf16[1536,128]{1,0:T(8,128)(2,1)S(1)} %get-tuple-element.67), channel_id=1, source_target_pairs={{0,8},{4,12},{8,0},{12,4},{16,24},{20,28},{24,16},{28,20},{1,9},{5... | collective-permute-start | bytes 1179656 | tf_op jit(solution)/shard_map/ppermute | solution.py:15
  123.0 16.4 %collective-permute-start.33 = (bf16[1536,128]{1,0:T(8,128)(2,1)S(1)}, bf16[1536,128]{1,0:T(8,128)(2,1)S(1)}, u32[]{:S(2)}, u32[]{:S(2)}) collective-permute-start(bf16[1536,128]{1,0:T(8,128)(2,1)S(1)} %get-tuple-element.66), channel_id=1, source_target_pairs={{0,8},{4,12},{8,0},{12,4},{16,24},{20,28},{24,16},{28,20},{1,9},{5... | collective-permute-start | bytes 1179656 | tf_op jit(solution)/shard_map/ppermute | solution.py:15
  (17 other events, 174.3 us)

commit v4 on v3

v4 whole, which is shorter than its diff:
```python
import jax
import jax.numpy as jnp
from jax import lax
from jax.experimental import pallas as pl
from jax.experimental.pallas import tpu as pltpu
from jax.sharding import PartitionSpec as P

BF16, F32 = jnp.bfloat16, jnp.float32
TAIL = 16
VMEM = pl.BlockSpec(memory_space=pltpu.VMEM)
SMEM = pl.BlockSpec(memory_space=pltpu.SMEM)


def swap(value, axis, mask):
    pairs = [(source, source ^ mask) for source in range(lax.axis_size(axis))]
    return lax.ppermute(value, axis, pairs)


def alpha_of(device):
    return device ^ (2 * (device & 1))


def beta_of(device):
    return device ^ (2 * (1 - (device & 1)))


def shape_of(*dims, dtype=BF16):
    return jax.ShapeDtypeStruct(dims, dtype)


def call(kernel, shapes, *args, scratch=(), flops=0, specs=None):
    return pl.pallas_call(
        kernel,
        out_shape=shapes,
        in_specs=specs or [VMEM] * len(args),
        out_specs=jax.tree.map(lambda _: VMEM, shapes),
        scratch_shapes=scratch,
        cost_estimate=pl.CostEstimate(
            flops=flops, bytes_accessed=1 << 20, transcendentals=0
        ),
        compiler_params=pltpu.CompilerParams(vmem_limit_bytes=16 << 20),
    )(*args)


def dots(a, b, da, db):
    return lax.dot_general(a, b, (((da,), (db,)), ((), ())), preferred_element_type=F32)


def at(start, size):
    return pl.ds(pl.multiple_of(start, size), size)


def split_rows(index_of, chips, source, *refs):
    outs, table = refs[:-1], refs[-1]
    rows, blocks, cols = source.shape
    step = 16
    wide = step * blocks
    to = lax.broadcasted_iota(jnp.int32, (wide, wide), 0)
    by = lax.broadcasted_iota(jnp.int32, (wide, wide), 1)
    pick = jnp.where(by == (to % step) * blocks + to // step, 1.0, 0.0).astype(BF16)
    for q in range(0, rows, step):
        tile = dots(pick, source[q : q + step].reshape(wide, cols), 1, 0).astype(BF16)
        for d in range(blocks):
            table[d, q : q + step, :] = tile[d * step : (d + 1) * step]
    chip = lax.axis_index("occ") // 2
    for m in range(chips):
        for c in (0, 1):
            outs[m][c] = table[index_of(2 * (chip ^ m) + c)]


def give_rows(*refs):
    held, out = refs[:-1], refs[-1]
    core = lax.axis_index("occ") % 2
    for m, ref in enumerate(held):
        out[m] = ref[1 - core]


def energy_tail(value, width):
    parts = []
    for _ in range(3):
        parts.append(value.astype(BF16).astype(F32))
        value = value - parts[-1]
    lines = [p[:, k : k + width] for p in parts for k in range(0, value.shape[1], width)]
    row = lax.broadcasted_iota(jnp.int32, (TAIL, width), 0)
    tail = jnp.zeros((TAIL, width), F32)
    for i, line in enumerate(lines):
        tail = jnp.where(row == i, jnp.broadcast_to(line, (TAIL, width)), tail)
    return tail.astype(BF16)


def energy_of(tail, unit):
    value = tail.astype(F32)
    step = unit // tail.shape[1]
    line = lambda i: value[i : i + 1] + value[i + step : i + step + 1] + value[i + 2 * step : i + 2 * step + 1]
    return jnp.concatenate([line(i) for i in range(step)], axis=1)


def tail_rows(energy, out):
    out[...] = energy_tail(energy[...], out.shape[1])


def place_rows(chips, extra, *refs):
    held, take, outs = refs[:chips], refs[chips], refs[chips + 1 + extra :]
    rows = take.shape[1]
    me = lax.axis_index("occ")
    chip, core = me // 2, me % 2
    for m in range(chips):
        start = 2 * (chip ^ m) * rows
        for i, out in enumerate(outs):
            cols = slice(i * out.shape[1], (i + 1) * out.shape[1])
            out[at(start + core * rows, rows), :] = held[m][core, :, cols]
            out[at(start + (1 - core) * rows, rows), :] = take[m, :, cols]
    if extra:
        out = outs[0]
        out[2 * chips * rows :, :] = energy_tail(refs[chips + 1][...], out.shape[1])


def regroup(ints, index_of, parts, *extra):
    blocks = lax.axis_size("occ")
    chips = blocks // 2
    rows, _, cols = ints.shape
    if chips > 4:
        table = ints.transpose(1, 0, 2)
        table = jnp.stack([table[index_of(d)] for d in range(blocks)])
        got = lax.all_to_all(table, "occ", split_axis=0, concat_axis=0, tiled=True)
        got = jnp.split(got.reshape(blocks * rows, cols), parts, axis=1)
        for energy in extra:
            tail = call(tail_rows, shape_of(TAIL, cols // parts), energy)
            got[0] = jnp.concatenate([got[0], tail], axis=0)
        return got
    held = [*call(
        lambda *refs: split_rows(index_of, chips, *refs),
        [shape_of(2, rows, cols)] * chips,
        ints,
        scratch=[pltpu.VMEM((blocks, rows, cols), BF16)],
    )]
    for m in range(1, chips):
        held[m] = swap(held[m], "occ", 2 * m)
    give = call(give_rows, shape_of(chips, rows, cols), *held)
    take = swap(give, "occ", 1)
    place = lambda *refs: place_rows(chips, len(extra), *refs)
    tails = [TAIL * len(extra)] + [0] * (parts - 1)
    shapes = [shape_of(blocks * rows + tail, cols // parts) for tail in tails]
    return call(place, shapes, *held, take, *extra)


def halves_metric(metric):
    rows = metric.shape[0]
    half = rows // 2
    core, layer = lax.axis_index("occ") % 2, lax.axis_index("vir")
    mine = lax.dynamic_slice_in_dim(metric, core * half, half, 0)
    got = jnp.stack([swap(mine, "vir", k) for k in (1, 2, 3)])
    other = swap(got, "occ", 1)
    lo, hi = jnp.where(core == 0, got, other), jnp.where(core == 0, other, got)
    rest = jnp.concatenate([lo, hi], axis=1)
    pieces = [metric, rest[0], rest[1], rest[2]]
    return jnp.concatenate([lax.select_n(layer ^ k, *pieces) for k in range(4)], axis=0)


def near_of(k):
    return k - 1 if k > 1 else 3


def cut_own(metric, *refs):
    outs, sems = refs[:-1], refs[-1]
    part, wide = outs[0].shape[0], outs[0].shape[1] // 2
    layer = lax.axis_index("vir")
    rows = at(lax.axis_index("occ") * part, part)
    copies = []
    for k, out in zip((1, 2, 3), outs):
        for i, block in enumerate((layer, layer ^ k ^ near_of(k))):
            source = metric.at[rows, at(block * wide, wide)]
            target = out.at[:, i * wide : (i + 1) * wide]
            copies.append(pltpu.make_async_copy(source, target, sems.at[k - 1, i]))
            copies[-1].start()
    for copy in copies:
        copy.wait()


def pack_metric(*refs):
    for k, ref in enumerate(refs[:-1]):
        refs[-1][k] = ref[...]


def cut_metric(by_x, by_y, via_x, via_y):
    half = via_x.shape[2]
    via_x[...] = by_y[:, :, :half]
    via_y[...] = by_x[:, :, half:]


def place_metric(own, *refs):
    refs, out, same, cross = refs[:-3], *refs[-3:]
    mine, other = refs[: len(refs) // 2], refs[len(refs) // 2 :]
    rows = own.shape[0]
    part = mine[0].shape[1]
    me, layer = lax.axis_index("occ"), lax.axis_index("vir")
    chip, core = me // 2, me % 2
    for k in (0, 1, 2):
        for c, held in ((core, mine), (1 - core, other)):
            for m in range(4):
                here = at((2 * (chip ^ m) + c) * part, part)
                same[k, here, :] = held[m][k, :, :rows]
                cross[k, here, :] = held[4 if m == 3 else m][k, :, -rows:]
    block = lambda u: at(u * rows, rows)
    out[block(layer), :] = own[...]
    for k in (1, 2, 3):
        there, third = layer ^ k, layer ^ near_of(k)
        out[block(there), block(there)] = same[k - 1]
        out[block(there), block(third)] = cross[k - 1]
        out[block(third), block(there)] = cross[k - 1].T
        out[block(there), block(layer)] = own[:, block(there)].T


def whole_metric(metric):
    rows, aux = metric.shape
    blocks = lax.axis_size("occ")
    if blocks != 8 or rows % (16 * blocks) or rows % 128 or aux != 4 * rows:
        return halves_metric(metric)
    part = rows // blocks
    mine = call(
        cut_own,
        [shape_of(part, 2 * rows)] * 3,
        metric,
        specs=[pl.BlockSpec(memory_space=pl.ANY)],
        scratch=[pltpu.SemaphoreType.DMA((3, 2))],
    )
    got = [swap(piece, "vir", k) for k, piece in zip((1, 2, 3), mine)]
    got = call(pack_metric, shape_of(3, part, 2 * rows), *got)
    by_x, by_y = swap(got, "occ", 2), swap(got, "occ", 4)
    halves = call(cut_metric, [shape_of(3, part, rows)] * 2, by_x, by_y)
    via_x, via_y = swap(halves[0], "occ", 2), swap(halves[1], "occ", 4)
    plane = [got, by_x, by_y, via_x, via_y]
    other = [swap(p, "occ", 1) for p in plane]
    half = pltpu.VMEM((3, rows, rows), BF16)
    whole = shape_of(aux, aux)
    return call(place_metric, whole, metric, *plane, *other, scratch=[half] * 2)


def row_chunks(rows, body, step=512):
    step = step if rows % step == 0 else rows
    for start in range(0, rows, step):
        body(slice(start, start + step))


def fit_rows(square, *refs):
    raws, out = refs[:-1], refs[-1]
    raw = jnp.concatenate([r[: square.shape[0], :] for r in raws], axis=1)

    def body(rows):
        out[rows, :] = dots(square[rows, :], raw, 1, 0).astype(BF16)

    row_chunks(square.shape[0], body)


def fit(square, *raws):
    aux = square.shape[0]
    unit = sum(raw.shape[1] for raw in raws)
    return call(fit_rows, shape_of(aux, unit), square, *raws, flops=2 * aux * aux * unit)


def energy_rows(occ_a, occ_o, occ_b, vir_a, vir_b, vir_n, left, right, *near):
    layer, me = lax.axis_index("vir"), lax.axis_index("occ")
    unit = vir_b.shape[1]
    for u, occ in enumerate((occ_a, occ_a, occ_o, occ_o)):
        row = vir_a[at((layer ^ (u % 2)) * unit, unit)].reshape(1, unit)
        left[u : u + 1, :] = occ[0] - row
    column = lambda vir: jnp.broadcast_to(occ_b[beta_of(me)] - vir, (128, unit)).T
    right[...] = column(vir_b[...])
    far = energy_of(vir_n[vir_n.shape[0] - TAIL :, :], unit)
    half = unit // 2
    for i, out in enumerate(near):
        out[...] = column(far)[i * half : (i + 1) * half]


def tile_rows(a0, a1, o0, o1, beta, left, right, mine, other, gamma, flip):
    alphas = (a0, a1, o0, o1)
    amp = [mine.at[0], mine.at[1], other.at[0], other.at[1]]
    flip[...] = beta[...].T
    column = right[:, :1]
    for u, alpha in enumerate(alphas):
        pair = dots(flip[...], alpha[...], 1, 0)
        amp[u][...] = (pair / (left[u : u + 1, :] + column)).astype(BF16)

    def body(rows):
        total = dots(a0[rows, :], amp[0][...], 1, 1)
        for u in (1, 2, 3):
            total = total + dots(alphas[u][rows, :], amp[u][...], 1, 1)
        gamma[rows, :] = total.astype(gamma.dtype)

    row_chunks(beta.shape[0], body)


def tile(alphas, beta, left, right, dtype):
    aux, width = beta.shape
    unit = alphas[0].shape[1]
    return call(
        tile_rows,
        [shape_of(2, width, unit)] * 2 + [shape_of(aux, width, dtype=dtype)],
        *alphas,
        beta,
        left,
        right,
        scratch=[pltpu.VMEM((width, aux), BF16)],
        flops=16 * aux * unit * width,
    )


def early_rows(*refs):
    betas, amps, out = refs[:4], refs[4:8], refs[8]
    unit = amps[0].shape[2]

    def body(rows):
        for u in (0, 1):
            total = dots(betas[0][rows, :], amps[0][u], 1, 0)
            for beta, amp in zip(betas[1:], amps[1:]):
                total = total + dots(beta[rows, :], amp[u], 1, 0)
            out[rows, u * unit : (u + 1) * unit] = total

    row_chunks(out.shape[0], body)


def mix_rows(early, beta_mine, beta_other, amp_mine, amp_other, own, near_zero, near_one, *outs):
    unit = amp_mine.shape[2]
    half = unit // 2
    odd = lax.axis_index("occ") % 2 == 1
    send2, send3, send4, keep2, keep3, keep4 = outs

    def body(rows):
        alpha = []
        for u in (0, 1):
            total = early[rows, u * unit : (u + 1) * unit]
            total = total + dots(beta_mine[rows, :], amp_mine[u], 1, 0)
            alpha.append(total + dots(beta_other[rows, :], amp_other[u], 1, 0))
        here, there = alpha[0], alpha[1].astype(BF16)
        beta, far = own[rows, :], near_one[rows, :]
        pick = lambda a, b: jnp.where(odd, a, b)
        send2[rows, :] = pick(there[:, :half], far)
        send3[rows, :] = there[:, half:]
        send4[rows, :half] = pick(near_zero[rows, :], there[:, :half])
        send4[rows, half:] = pick(far, there[:, half:])
        keep2[rows, :] = pick(here[:, :half], beta[:, half:])
        keep3[rows, :] = here[:, half:]
        keep4[rows, :] = pick(beta, here)

    row_chunks(early.shape[0], body, 256)


def sum_one(own_gamma, got, out):
    out[...] = (own_gamma[:, : out.shape[1]] + got[...].astype(F32)).astype(BF16)


def sum_keep(keep, got, out):
    out[...] = (keep[...] + got[...].astype(F32)).astype(BF16)


def last_rows(*refs):
    keep, got, move_a, move_b, move_c, alpha, beta, hold_a, hold_b, sems = refs
    odd = lax.axis_index("occ") % 2 == 1
    aux, half = move_a.shape
    step = aux // sems.shape[1]
    copies = []
    for i, start in enumerate(range(0, aux, step)):
        rows = slice(start, start + step)
        final = (keep[rows, :] + got[rows, :].astype(F32)).astype(BF16)
        low, high = final[:, :half], final[:, half:]
        hold_a[rows, :half] = jnp.where(odd, move_b[rows, :], low)
        hold_a[rows, half:] = jnp.where(odd, move_c[rows, :], high)
        hold_b[rows, :half] = jnp.where(odd, low, move_a[rows, :])
        hold_b[rows, half:] = jnp.where(odd, high, move_b[rows, :])
        for j, (hold, out) in enumerate(((hold_a, alpha), (hold_b, beta))):
            copy = pltpu.make_async_copy(hold.at[rows, :], out.at[rows, :], sems.at[j, i])
            copy.start()
            copies.append(copy)
    for copy in copies:
        copy.wait()


def last(*arrays):
    aux, half = arrays[-1].shape
    parts = 3
    anywhere = pl.BlockSpec(memory_space=pl.ANY)
    return pl.pallas_call(
        last_rows,
        out_shape=[shape_of(aux, 2 * half)] * 2,
        in_specs=[VMEM] * len(arrays),
        out_specs=[anywhere] * 2,
        scratch_shapes=[pltpu.VMEM((aux, 2 * half), BF16)] * 2
        + [pltpu.SemaphoreType.DMA((2, parts))],
        compiler_params=pltpu.CompilerParams(vmem_limit_bytes=8 << 20),
    )(*arrays)


def ring(ints_alpha, ints_beta, metric, e_occ_alpha, e_occ_beta, e_vir_alpha, e_vir_beta):
    aux = metric.shape[1]
    unit = e_vir_beta.shape[0]
    half = unit // 2
    blocks, layers = lax.axis_size("occ"), lax.axis_size("vir")
    assert layers == 4 and e_occ_alpha.shape[0] == 1

    square = whole_metric(metric)
    raw_beta = regroup(ints_beta, beta_of, 2, e_vir_beta[None])
    (raw_alpha,) = regroup(ints_alpha, alpha_of, 1)

    occ_mine = lax.ppermute(e_occ_alpha, "occ", [(alpha_of(d), d) for d in range(blocks)])
    occ_other = swap(occ_mine, "occ", 1)
    near_beta = []
    for raw in raw_beta:
        near_beta.append(swap(raw, "vir", 3))
    near_alpha = swap(raw_alpha, "vir", 1)

    left, right, right_zero, right_one = call(
        energy_rows,
        [shape_of(4, unit, dtype=F32)] + [shape_of(n, 128, dtype=F32) for n in (unit, half, half)],
        occ_mine,
        occ_other,
        e_occ_beta,
        e_vir_alpha,
        e_vir_beta[None],
        near_beta[0],
        specs=[SMEM] * 3 + [VMEM] * 3,
    )

    a0 = fit(square, raw_alpha)
    o0 = swap(a0, "occ", 1)
    b0 = fit(square, *raw_beta)
    a1 = fit(square, near_alpha)
    o1 = swap(a1, "occ", 1)
    alphas = (a0, a1, o0, o1)

    def both(array):
        return array, swap(array, "occ", 1)

    def tiles(beta, column, dtype):
        mine, other, gamma = tile(alphas, beta, left, column, dtype)
        return (mine, both(other)[1]), gamma

    b0, b0_other = both(b0)
    b1, b1_other = both(fit(square, near_beta[0]))
    amp_own, gamma_own = tiles(b0, right, F32)
    amp_zero, gamma_zero = tiles(b1, right_zero, BF16)

    def back(send, odd, even):
        pairs = [
            (d * layers + v, d * layers + (v ^ step))
            for d in range(blocks)
            for v in range(layers)
            for step in [odd if d % 2 else even]
            if step
        ]
        return lax.ppermute(send, ("occ", "vir"), pairs)

    got_one = back(gamma_zero, 0, 3)
    b2, b2_other = both(fit(square, near_beta[1]))
    amp_one, gamma_one = tiles(b2, right_one, BF16)
    betas, amps = (b0, b0_other, b1, b1_other), (*amp_own, *amp_zero)
    pair = shape_of(aux, 2 * unit, dtype=F32)
    early = call(early_rows, pair, *betas, *amps, flops=12 * aux * unit * unit)
    thin, thin32 = shape_of(aux, half), shape_of(aux, half, dtype=F32)
    send2, send3, send4, keep2, keep3, keep4 = call(
        mix_rows,
        [thin, thin, shape_of(aux, unit), thin32, thin32, shape_of(aux, unit, dtype=F32)],
        early,
        b2,
        b2_other,
        *amp_one,
        gamma_own,
        gamma_zero,
        gamma_one,
        flops=4 * aux * unit * unit,
    )
    got_two = back(send2, 1, 3)
    got_three = back(send3, 1, 0)
    got_four = back(send4, 3, 1)

    def move(value, cores):
        pairs = [(d, d ^ 2) for d in range(blocks) if d % 2 in cores]
        return lax.ppermute(value, "occ", pairs)

    first = call(sum_one, thin, gamma_own, got_one)
    second = call(sum_keep, thin, keep2, got_two)
    third = call(sum_keep, thin, keep3, got_three)
    moves = move(first, (0,)), move(second, (0, 1)), move(third, (1,))
    out_alpha, out_beta = last(keep4, got_four, *moves)
    return out_alpha.reshape(aux, 1, unit), out_beta.reshape(aux, 1, unit)


def solution(mesh):
    in_specs = (
        P("occ", None, "vir"),
        P("occ", None, "vir"),
        P("vir", None),
        P("occ"),
        P(),
        P(),
        P("vir"),
    )
    out_specs = (P(None, "occ", "vir"), P(None, "occ", "vir"))

    return jax.shard_map(ring, mesh=mesh, in_specs=in_specs, out_specs=out_specs, check_vma=False)
```

time: 141 us -> 136 us (0.965)
  the two profiles are of different devices: /device:TPU:11 before, /device:TPU:1 now
where the time goes in v4:
time: 136 us
  starting transfers between devices  66.7 us (49%)
  waiting for transfers between devices  46.6 us (34%)
  Pallas kernels  20.5 us (15%)
    ppermute x32, starting transfers between devices, swap(): return lax.ppermute(value, axis, pairs)  37.6 us
    ppermute x32, waiting for transfers between devices, swap(): return lax.ppermute(value, axis, pairs)  27.6 us
    ppermute x4, starting transfers between devices, back(): return lax.ppermute(send, ('occ', 'vir'), pairs)  21.1 us
    pallas_call x24, Pallas kernels, call(): pl.pallas_call(kernel, out_shape=shapes, in_specs=specs or [VMEM] * len(a...  19.2 us
    ppermute x4, waiting for transfers between devices, back(): return lax.ppermute(send, ('occ', 'vir'), pairs)  11.4 us
    ppermute x3, waiting for transfers between devices, move(): return lax.ppermute(value, 'occ', pairs)  7.68 us
    ppermute x3, starting transfers between devices, move(): return lax.ppermute(value, 'occ', pairs)  4.95 us
    ppermute x1, starting transfers between devices, ring(): lax.ppermute(e_occ_alpha, 'occ', [(alpha_of(d), d) for d in range(blocks)])  2.99 us
  transfers between devices with their start and end apart: 40, of which 13 were waited for; matrix products, arithmetic and copies ran while one was open for 0% of the time, Pallas kernels for 14%

profile of v4, /device:TPU:1, one launch (start us, length us, event | category | flops | bytes accessed | tf_op | source)
XLA Modules:
  0.0 136.2 jit_solution(6246361280635528094)
XLA Ops:
  2.3 2.1 %collective-permute-start.19 = (bf16[2,192,256]{2,1,0:T(8,128)(2,1)S(1)}, bf16[2,192,256]{2,1,0:T(8,128)(2,1)S(1)}, u32[]{:S(2)}, u32[]{:S(2)}) collective-permute-start(bf16[2,192,256]{2,1,0:T(8,128)(2,1)S(1)} %get-tuple-element.50), channel_id=1, source_target_pairs={{0,8},{4,12},{8,0},{12,4},{16,24},{20,28},{24,16},{28,20},{1,9},{5... | collective-permute-start | bytes 589832 | tf_op jit(solution)/shard_map/ppermute | solution.py:16
  5.6 3.3 %collective-permute-done.19.refs_1_ = bf16[2,192,256]{2,1,0:T(8,128)(2,1)S(1)} collective-permute-done((bf16[2,192,256]{2,1,0:T(8,128)(2,1)S(1)}, bf16[2,192,256]{2,1,0:T(8,128)(2,1)S(1)}, u32[]{:S(2)}, u32[]{:S(2)}) %collective-permute-start.19) | collective-permute-done | bytes 196640 | tf_op jit(solution)/shard_map/ppermute | solution.py:16
  9.9 4.3 %collective-permute-done.21.refs_3_ = bf16[2,192,256]{2,1,0:T(8,128)(2,1)S(1)} collective-permute-done((bf16[2,192,256]{2,1,0:T(8,128)(2,1)S(1)}, bf16[2,192,256]{2,1,0:T(8,128)(2,1)S(1)}, u32[]{:S(2)}, u32[]{:S(2)}) %collective-permute-start.21) | collective-permute-done | bytes 196640 | tf_op jit(solution)/shard_map/ppermute | solution.py:16
  17.5 2.3 %collective-permute-start.1 = (bf16[48,768]{1,0:T(8,128)(2,1)S(1)}, bf16[48,768]{1,0:T(8,128)(2,1)S(1)}, u32[]{:S(2)}, u32[]{:S(2)}) collective-permute-start(bf16[48,768]{1,0:T(8,128)(2,1)S(1)} %get-tuple-element.39), channel_id=1, source_target_pairs={{0,2},{1,3},{2,0},{3,1},{4,6},{5,7},{6,4},{7,5},{8,10},{9,11},{10,... | collective-permute-start | bytes 221192 | tf_op jit(solution)/shard_map/ppermute | solution.py:16
  21.9 3.0 %collective-permute-done.2.refs_2_ = bf16[48,768]{1,0:T(8,128)(2,1)S(1)} collective-permute-done((bf16[48,768]{1,0:T(8,128)(2,1)S(1)}, bf16[48,768]{1,0:T(8,128)(2,1)S(1)}, u32[]{:S(2)}, u32[]{:S(2)}) %collective-permute-start.2) | collective-permute-done | bytes 73760 | tf_op jit(solution)/shard_map/ppermute | solution.py:16
  26.5 3.0 %collective-permute-start.7 = (bf16[3,48,768]{2,1,0:T(8,128)(2,1)S(1)}, bf16[3,48,768]{2,1,0:T(8,128)(2,1)S(1)}, u32[]{:S(2)}, u32[]{:S(2)}) collective-permute-start(bf16[3,48,768]{2,1,0:T(8,128)(2,1)S(1)} %shard_map.87.refs_0_), channel_id=1, source_target_pairs={{0,4},{4,0},{8,12},{12,8},{16,20},{20,16},{24,28},{28,24},{1,5},{5... | collective-permute-start | bytes 663560 | tf_op jit(solution)/shard_map/ppermute | solution.py:16
  32.6 4.2 %collective-permute-done.12.refs_1_ = bf16[2,192,256]{2,1,0:T(8,128)(2,1)S(1)} collective-permute-done((bf16[2,192,256]{2,1,0:T(8,128)(2,1)S(1)}, bf16[2,192,256]{2,1,0:T(8,128)(2,1)S(1)}, u32[]{:S(2)}, u32[]{:S(2)}) %collective-permute-start.12) | collective-permute-done | bytes 196640 | tf_op jit(solution)/shard_map/ppermute | solution.py:16
  38.1 2.8 %collective-permute-start.9 = (bf16[3,48,768]{2,1,0:T(8,128)(2,1)S(1)}, bf16[3,48,768]{2,1,0:T(8,128)(2,1)S(1)}, u32[]{:S(2)}, u32[]{:S(2)}) collective-permute-start(bf16[3,48,768]{2,1,0:T(8,128)(2,1)S(1)} %collective-permute-done.4.by_y.refs_2_), channel_id=1, source_target_pairs={{0,4},{4,0},{8,12},{12,8},{16,20},{20,16},{24,28},{28,24},{1,5},{5... | collective-permute-start | bytes 663560 | tf_op jit(solution)/shard_map/ppermute | solution.py:16
  42.3 3.7 %collective-permute-start.8 = (bf16[3,48,768]{2,1,0:T(8,128)(2,1)S(1)}, bf16[3,48,768]{2,1,0:T(8,128)(2,1)S(1)}, u32[]{:S(2)}, u32[]{:S(2)}) collective-permute-start(bf16[3,48,768]{2,1,0:T(8,128)(2,1)S(1)} %collective-permute-done.3.by_x.refs_1_), channel_id=1, source_target_pairs={{0,4},{4,0},{8,12},{12,8},{16,20},{20,16},{24,28},{28,24},{1,5},{5... | collective-permute-start | bytes 663560 | tf_op jit(solution)/shard_map/ppermute | solution.py:16
  46.0 3.2 %collective-permute-start.11 = (bf16[3,48,384]{2,1,0:T(8,128)(2,1)S(1)}, bf16[3,48,384]{2,1,0:T(8,128)(2,1)S(1)}, u32[]{:S(2)}, u32[]{:S(2)}) collective-permute-start(bf16[3,48,384]{2,1,0:T(8,128)(2,1)S(1)} %collective-permute-done.6.refs_4_), channel_id=1, source_target_pairs={{0,4},{4,0},{8,12},{12,8},{16,20},{20,16},{24,28},{28,24},{1,5},{5... | collective-permute-start | bytes 331784 | tf_op jit(solution)/shard_map/ppermute | solution.py:16
  54.8 1.9 %collective-permute-start.30 = (bf16[1536,128]{1,0:T(8,128)(2,1)S(1)}, bf16[1536,128]{1,0:T(8,128)(2,1)S(1)}, u32[]{:S(2)}, u32[]{:S(2)}) collective-permute-start(bf16[1536,128]{1,0:T(8,128)(2,1)S(1)} %get-tuple-element.48.refs_1_), channel_id=1, source_target_pairs={{0,3},{1,2},{2,1},{3,0},{4,7},{5,6},{6,5},{7,4},{8,11},{9,10},{10,... | collective-permute-start | bytes 1179656 | tf_op jit(solution)/shard_map/ppermute | solution.py:16
  56.7 3.0 %collective-permute-start.26 = (f32[1]{0:T(128)}, f32[1]{0:T(128)}, u32[]{:S(2)}, u32[]{:S(2)}) collective-permute-start(f32[1]{0:T(128)} %param.10), channel_id=1, source_target_pairs={{0,0},{12,4},{8,8},{4,12},{16,16},{28,20},{24,24},{20,28},{1,1},{1... | collective-permute-start | bytes 20 | tf_op jit(solution)/shard_map/ppermute | solution.py:404
  62.6 4.3 %collective-permute-done.30.refs_0_ = bf16[1536,128]{1,0:T(8,128)(2,1)S(1)} collective-permute-done((bf16[1536,128]{1,0:T(8,128)(2,1)S(1)}, bf16[1536,128]{1,0:T(8,128)(2,1)S(1)}, u32[]{:S(2)}, u32[]{:S(2)}) %collective-permute-start.30) | collective-permute-done | bytes 393248 | tf_op jit(solution)/shard_map/ppermute | solution.py:16
  67.0 2.1 %collective-permute-start.27 = (f32[1]{0:T(128)}, f32[1]{0:T(128)}, u32[]{:S(2)}, u32[]{:S(2)}) collective-permute-start(f32[1]{0:T(128)} %collective-permute-done.26.occ_a), channel_id=1, source_target_pairs={{0,4},{4,0},{8,12},{12,8},{16,20},{20,16},{24,28},{28,24},{1,5},{5... | collective-permute-start | bytes 20 | tf_op jit(solution)/shard_map/ppermute | solution.py:16
  70.5 5.0 %collective-permute-done.17.refs_0_.vir_n = bf16[1552,128]{1,0:T(8,128)(2,1)S(1)} collective-permute-done((bf16[1552,128]{1,0:T(8,128)(2,1)S(1)}, bf16[1552,128]{1,0:T(8,128)(2,1)S(1)}, u32[]{:S(2)}, u32[]{:S(2)}) %collective-permute-start.17) | collective-permute-done | bytes 397344 | tf_op jit(solution)/shard_map/ppermute | solution.py:16
  78.3 2.0 %shard_map.100 = (f32[4,256]{1,0:T(4,128)S(1)}, f32[256,128]{1,0:T(8,128)S(1)}, f32[128,128]{1,0:T(8,128)S(1)}, f32[128,128]{1,0:T(8,128)S(1)}) custom-call(f32[1]{0:T(128)} %collective-permute-done.26.occ_a, f32[1]{0:T(128)} %collective-permute-done.27.occ_o, f32[8]{0:T(128)S(1)} %copy-done.5, f32[1024]{0:T(1024)S(1)} %copy-done.3, f32[1,256]{1,0:T(1,128)S(1)} %bitcast.4, ...), custom_call_target="tpu_custom_call" | custom-call | bytes 1048576 | tf_op jit(solution)/shard_map/pallas_call | solution.py:32
  80.3 2.0 %shard_map.101 = (bf16[2,256,256]{2,1,0:T(8,128)(2,1)S(1)}, bf16[2,256,256]{2,1,0:T(8,128)(2,1)S(1)}, f32[1536,256]{1,0:T(8,128)S(1)}) custom-call(bf16[1536,256]{1,0:T(8,128)(2,1)S(1)} %shard_map.98.a0, bf16[1536,256]{1,0:T(8,128)(2,1)S(1)} %shard_map.99.a1, bf16[1536,256]{1,0:T(8,128)(2,1)S(1)} %collective-permute-done.24.o0, ...), custom_call_target="tpu_custom_call" | custom-call | flops 1610612736 | bytes 1048576 | tf_op jit(solution)/shard_map/pallas_call | solution.py:32
  90.1 16.5 %collective-permute-start.36 = (bf16[1536,128]{1,0:T(8,128)(2,1)S(1)}, bf16[1536,128]{1,0:T(8,128)(2,1)S(1)}, u32[]{:S(2)}, u32[]{:S(2)}) collective-permute-start(bf16[1536,128]{1,0:T(8,128)(2,1)S(1)} %get-tuple-element.69), channel_id=1, source_target_pairs={{0,3},{1,2},{2,1},{3,0},{4,5},{5,4},{6,7},{7,6},{8,11},{9,10},{10,... | collective-permute-start | bytes 1179656 | tf_op jit(solution)/shard_map/ppermute | solution.py:450
  106.7 1.9 %collective-permute-start.38 = (bf16[1536,128]{1,0:T(8,128)(2,1)S(1)}, bf16[1536,128]{1,0:T(8,128)(2,1)S(1)}, u32[]{:S(2)}, u32[]{:S(2)}) collective-permute-start(bf16[1536,128]{1,0:T(8,128)(2,1)S(1)} %get-tuple-element.71), channel_id=1, source_target_pairs={{4,5},{5,4},{6,7},{7,6},{12,13},{13,12},{14,15},{15,14},{20,21},{2... | collective-permute-start | bytes 1179656 | tf_op jit(solution)/shard_map/ppermute | solution.py:450
  108.6 2.0 %collective-permute-start.33 = (bf16[1536,256]{1,0:T(8,128)(2,1)S(1)}, bf16[1536,256]{1,0:T(8,128)(2,1)S(1)}, u32[]{:S(2)}, u32[]{:S(2)}) collective-permute-start(bf16[1536,256]{1,0:T(8,128)(2,1)S(1)} %get-tuple-element.67), channel_id=1, source_target_pairs={{0,1},{1,0},{2,3},{3,2},{4,7},{5,6},{6,5},{7,4},{8,9},{9,8},{10,11... | collective-permute-start | bytes 2359304 | tf_op jit(solution)/shard_map/ppermute | solution.py:450
  113.3 7.3 %collective-permute-done.38.got = bf16[1536,128]{1,0:T(8,128)(2,1)S(1)} collective-permute-done((bf16[1536,128]{1,0:T(8,128)(2,1)S(1)}, bf16[1536,128]{1,0:T(8,128)(2,1)S(1)}, u32[]{:S(2)}, u32[]{:S(2)}) %collective-permute-start.38) | collective-permute-done | bytes 393248 | tf_op jit(solution)/shard_map/ppermute | solution.py:450
  120.6 2.9 %collective-permute-start.39 = (bf16[1536,128]{1,0:T(8,128)(2,1)S(1)}, bf16[1536,128]{1,0:T(8,128)(2,1)S(1)}, u32[]{:S(2)}, u32[]{:S(2)}) collective-permute-start(bf16[1536,128]{1,0:T(8,128)(2,1)S(1)} %shard_map.109), channel_id=1, source_target_pairs={{4,12},{12,4},{20,28},{28,20},{5,13},{13,5},{21,29},{29,21},{6,14}... | collective-permute-start | bytes 1179656 | tf_op jit(solution)/shard_map/ppermute | solution.py:477
  123.5 7.7 %collective-permute-done.39.refs_4_ = bf16[1536,128]{1,0:T(8,128)(2,1)S(1)} collective-permute-done((bf16[1536,128]{1,0:T(8,128)(2,1)S(1)}, bf16[1536,128]{1,0:T(8,128)(2,1)S(1)}, u32[]{:S(2)}, u32[]{:S(2)}) %collective-permute-start.39) | collective-permute-done | bytes 393248 | tf_op jit(solution)/shard_map/ppermute | solution.py:477
  131.2 3.6 %collective-permute-done.33.refs_1_ = bf16[1536,256]{1,0:T(8,128)(2,1)S(1)} collective-permute-done((bf16[1536,256]{1,0:T(8,128)(2,1)S(1)}, bf16[1536,256]{1,0:T(8,128)(2,1)S(1)}, u32[]{:S(2)}, u32[]{:S(2)}) %collective-permute-start.33) | collective-permute-done | bytes 786464 | tf_op jit(solution)/shard_map/ppermute | solution.py:450
  (93 shorter events, 40.9 us)
Async XLA Ops:
  5.6 8.5 %collective-permute-start.21 = (bf16[2,192,256]{2,1,0:T(8,128)(2,1)S(1)}, bf16[2,192,256]{2,1,0:T(8,128)(2,1)S(1)}, u32[]{:S(2)}, u32[]{:S(2)}) collective-permute-start(bf16[2,192,256]{2,1,0:T(8,128)(2,1)S(1)} %get-tuple-element.52), channel_id=1, source_target_pairs={{0,24},{4,28},{8,16},{12,20},{16,8},{20,12},{24,0},{28,4},{1,25},{... | collective-permute-start | bytes 589832 | tf_op jit(solution)/shard_map/ppermute | solution.py:16
  19.9 33.1 %collective-permute-start.23 = (bf16[1536,256]{1,0:T(8,128)(2,1)S(1)}, bf16[1536,256]{1,0:T(8,128)(2,1)S(1)}, u32[]{:S(2)}, u32[]{:S(2)}) collective-permute-start(bf16[1536,256]{1,0:T(8,128)(2,1)S(1)} %shard_map.97.refs_0_), channel_id=1, source_target_pairs={{0,1},{1,0},{2,3},{3,2},{4,5},{5,4},{6,7},{7,6},{8,9},{9,8},{10,11... | collective-permute-start | bytes 2359304 | tf_op jit(solution)/shard_map/ppermute | solution.py:16
  26.5 15.8 %collective-permute-start.7 = (bf16[3,48,768]{2,1,0:T(8,128)(2,1)S(1)}, bf16[3,48,768]{2,1,0:T(8,128)(2,1)S(1)}, u32[]{:S(2)}, u32[]{:S(2)}) collective-permute-start(bf16[3,48,768]{2,1,0:T(8,128)(2,1)S(1)} %shard_map.87.refs_0_), channel_id=1, source_target_pairs={{0,4},{4,0},{8,12},{12,8},{16,20},{20,16},{24,28},{28,24},{1,5},{5... | collective-permute-start | bytes 663560 | tf_op jit(solution)/shard_map/ppermute | solution.py:16
  29.9 7.0 %collective-permute-start.12 = (bf16[2,192,256]{2,1,0:T(8,128)(2,1)S(1)}, bf16[2,192,256]{2,1,0:T(8,128)(2,1)S(1)}, u32[]{:S(2)}, u32[]{:S(2)}) collective-permute-start(bf16[2,192,256]{2,1,0:T(8,128)(2,1)S(1)} %get-tuple-element.44), channel_id=1, source_target_pairs={{0,8},{4,12},{8,0},{12,4},{16,24},{20,28},{24,16},{28,20},{1,9},{5... | collective-permute-start | bytes 589832 | tf_op jit(solution)/shard_map/ppermute | solution.py:16
  31.2 6.9 %collective-permute-start.13 = (bf16[2,192,256]{2,1,0:T(8,128)(2,1)S(1)}, bf16[2,192,256]{2,1,0:T(8,128)(2,1)S(1)}, u32[]{:S(2)}, u32[]{:S(2)}) collective-permute-start(bf16[2,192,256]{2,1,0:T(8,128)(2,1)S(1)} %get-tuple-element.45), channel_id=1, source_target_pairs={{0,16},{4,20},{8,24},{12,28},{16,0},{20,4},{24,8},{28,12},{1,17},{... | collective-permute-start | bytes 589832 | tf_op jit(solution)/shard_map/ppermute | solution.py:16
  31.4 9.5 %collective-permute-start.14 = (bf16[2,192,256]{2,1,0:T(8,128)(2,1)S(1)}, bf16[2,192,256]{2,1,0:T(8,128)(2,1)S(1)}, u32[]{:S(2)}, u32[]{:S(2)}) collective-permute-start(bf16[2,192,256]{2,1,0:T(8,128)(2,1)S(1)} %get-tuple-element.46), channel_id=1, source_target_pairs={{0,24},{4,28},{8,16},{12,20},{16,8},{20,12},{24,0},{28,4},{1,25},{... | collective-permute-start | bytes 589832 | tf_op jit(solution)/shard_map/ppermute | solution.py:16
  36.9 9.1 %collective-permute-start.5 = (bf16[3,48,384]{2,1,0:T(8,128)(2,1)S(1)}, bf16[3,48,384]{2,1,0:T(8,128)(2,1)S(1)}, u32[]{:S(2)}, u32[]{:S(2)}) collective-permute-start(bf16[3,48,384]{2,1,0:T(8,128)(2,1)S(1)} %get-tuple-element.41), channel_id=1, source_target_pairs={{0,8},{4,12},{8,0},{12,4},{16,24},{20,28},{24,16},{28,20},{1,9},{5... | collective-permute-start | bytes 331784 | tf_op jit(solution)/shard_map/ppermute | solution.py:16
  38.1 11.2 %collective-permute-start.9 = (bf16[3,48,768]{2,1,0:T(8,128)(2,1)S(1)}, bf16[3,48,768]{2,1,0:T(8,128)(2,1)S(1)}, u32[]{:S(2)}, u32[]{:S(2)}) collective-permute-start(bf16[3,48,768]{2,1,0:T(8,128)(2,1)S(1)} %collective-permute-done.4.by_y.refs_2_), channel_id=1, source_target_pairs={{0,4},{4,0},{8,12},{12,8},{16,20},{20,16},{24,28},{28,24},{1,5},{5... | collective-permute-start | bytes 663560 | tf_op jit(solution)/shard_map/ppermute | solution.py:16
  42.3 7.9 %collective-permute-start.8 = (bf16[3,48,768]{2,1,0:T(8,128)(2,1)S(1)}, bf16[3,48,768]{2,1,0:T(8,128)(2,1)S(1)}, u32[]{:S(2)}, u32[]{:S(2)}) collective-permute-start(bf16[3,48,768]{2,1,0:T(8,128)(2,1)S(1)} %collective-permute-done.3.by_x.refs_1_), channel_id=1, source_target_pairs={{0,4},{4,0},{8,12},{12,8},{16,20},{20,16},{24,28},{28,24},{1,5},{5... | collective-permute-start | bytes 663560 | tf_op jit(solution)/shard_map/ppermute | solution.py:16
  52.6 27.7 %collective-permute-start.24 = (bf16[1536,256]{1,0:T(8,128)(2,1)S(1)}, bf16[1536,256]{1,0:T(8,128)(2,1)S(1)}, u32[]{:S(2)}, u32[]{:S(2)}) collective-permute-start(bf16[1536,256]{1,0:T(8,128)(2,1)S(1)} %shard_map.98.a0), channel_id=1, source_target_pairs={{0,4},{4,0},{8,12},{12,8},{16,20},{20,16},{24,28},{28,24},{1,5},{5... | collective-permute-start | bytes 2359304 | tf_op jit(solution)/shard_map/ppermute | solution.py:16
  54.4 25.9 %collective-permute-start.25 = (bf16[1536,256]{1,0:T(8,128)(2,1)S(1)}, bf16[1536,256]{1,0:T(8,128)(2,1)S(1)}, u32[]{:S(2)}, u32[]{:S(2)}) collective-permute-start(bf16[1536,256]{1,0:T(8,128)(2,1)S(1)} %shard_map.99.a1), channel_id=1, source_target_pairs={{0,4},{4,0},{8,12},{12,8},{16,20},{20,16},{24,28},{28,24},{1,5},{5... | collective-permute-start | bytes 2359304 | tf_op jit(solution)/shard_map/ppermute | solution.py:16
  54.8 12.2 %collective-permute-start.30 = (bf16[1536,128]{1,0:T(8,128)(2,1)S(1)}, bf16[1536,128]{1,0:T(8,128)(2,1)S(1)}, u32[]{:S(2)}, u32[]{:S(2)}) collective-permute-start(bf16[1536,128]{1,0:T(8,128)(2,1)S(1)} %get-tuple-element.48.refs_1_), channel_id=1, source_target_pairs={{0,3},{1,2},{2,1},{3,0},{4,7},{5,6},{6,5},{7,4},{8,11},{9,10},{10,... | collective-permute-start | bytes 1179656 | tf_op jit(solution)/shard_map/ppermute | solution.py:16
  59.7 15.8 %collective-permute-start.17 = (bf16[1552,128]{1,0:T(8,128)(2,1)S(1)}, bf16[1552,128]{1,0:T(8,128)(2,1)S(1)}, u32[]{:S(2)}, u32[]{:S(2)}) collective-permute-start(bf16[1552,128]{1,0:T(8,128)(2,1)S(1)} %get-tuple-element.47.refs_0_), channel_id=1, source_target_pairs={{0,3},{1,2},{2,1},{3,0},{4,7},{5,6},{6,5},{7,4},{8,11},{9,10},{10,... | collective-permute-start | bytes 1191944 | tf_op jit(solution)/shard_map/ppermute | solution.py:16
  62.6 23.5 %collective-permute-start.16 = (bf16[1536,256]{1,0:T(8,128)(2,1)S(1)}, bf16[1536,256]{1,0:T(8,128)(2,1)S(1)}, u32[]{:S(2)}, u32[]{:S(2)}) collective-permute-start(bf16[1536,256]{1,0:T(8,128)(2,1)S(1)} %shard_map.93.beta.refs_0_), channel_id=1, source_target_pairs={{0,4},{4,0},{8,12},{12,8},{16,20},{20,16},{24,28},{28,24},{1,5},{5... | collective-permute-start | bytes 2359304 | tf_op jit(solution)/shard_map/ppermute | solution.py:16
  67.0 11.2 %collective-permute-start.27 = (f32[1]{0:T(128)}, f32[1]{0:T(128)}, u32[]{:S(2)}, u32[]{:S(2)}) collective-permute-start(f32[1]{0:T(128)} %collective-permute-done.26.occ_a), channel_id=1, source_target_pairs={{0,4},{4,0},{8,12},{12,8},{16,20},{20,16},{24,28},{28,24},{1,5},{5... | collective-permute-start | bytes 20 | tf_op jit(solution)/shard_map/ppermute | solution.py:16
  75.5 13.6 %collective-permute-start.31 = (bf16[1536,128]{1,0:T(8,128)(2,1)S(1)}, bf16[1536,128]{1,0:T(8,128)(2,1)S(1)}, u32[]{:S(2)}, u32[]{:S(2)}) collective-permute-start(bf16[1536,128]{1,0:T(8,128)(2,1)S(1)} %shard_map.104.beta.beta_mine), channel_id=1, source_target_pairs={{0,4},{4,0},{8,12},{12,8},{16,20},{20,16},{24,28},{28,24},{1,5},{5... | collective-permute-start | bytes 1179656 | tf_op jit(solution)/shard_map/ppermute | solution.py:16
  78.2 8.4 %collective-permute-start.18 = (bf16[1536,128]{1,0:T(8,128)(2,1)S(1)}, bf16[1536,128]{1,0:T(8,128)(2,1)S(1)}, u32[]{:S(2)}, u32[]{:S(2)}) collective-permute-start(bf16[1536,128]{1,0:T(8,128)(2,1)S(1)} %shard_map.94.beta.refs_2_), channel_id=1, source_target_pairs={{0,4},{4,0},{8,12},{12,8},{16,20},{20,16},{24,28},{28,24},{1,5},{5... | collective-permute-start | bytes 1179656 | tf_op jit(solution)/shard_map/ppermute | solution.py:16
  86.6 24.0 %collective-permute-start.34 = (bf16[1536,128]{1,0:T(8,128)(2,1)S(1)}, bf16[1536,128]{1,0:T(8,128)(2,1)S(1)}, u32[]{:S(2)}, u32[]{:S(2)}) collective-permute-start(bf16[1536,128]{1,0:T(8,128)(2,1)S(1)} %get-tuple-element.64.near_zero), channel_id=1, source_target_pairs={{0,3},{1,2},{2,1},{3,0},{8,11},{9,10},{10,9},{11,8},{16,19},{17,18... | collective-permute-start | bytes 1179656 | tf_op jit(solution)/shard_map/ppermute | solution.py:450
  90.1 21.7 %collective-permute-start.36 = (bf16[1536,128]{1,0:T(8,128)(2,1)S(1)}, bf16[1536,128]{1,0:T(8,128)(2,1)S(1)}, u32[]{:S(2)}, u32[]{:S(2)}) collective-permute-start(bf16[1536,128]{1,0:T(8,128)(2,1)S(1)} %get-tuple-element.69), channel_id=1, source_target_pairs={{0,3},{1,2},{2,1},{3,0},{4,5},{5,4},{6,7},{7,6},{8,11},{9,10},{10,... | collective-permute-start | bytes 1179656 | tf_op jit(solution)/shard_map/ppermute | solution.py:450
  106.7 13.9 %collective-permute-start.38 = (bf16[1536,128]{1,0:T(8,128)(2,1)S(1)}, bf16[1536,128]{1,0:T(8,128)(2,1)S(1)}, u32[]{:S(2)}, u32[]{:S(2)}) collective-permute-start(bf16[1536,128]{1,0:T(8,128)(2,1)S(1)} %get-tuple-element.71), channel_id=1, source_target_pairs={{4,5},{5,4},{6,7},{7,6},{12,13},{13,12},{14,15},{15,14},{20,21},{2... | collective-permute-start | bytes 1179656 | tf_op jit(solution)/shard_map/ppermute | solution.py:450
  108.6 26.2 %collective-permute-start.33 = (bf16[1536,256]{1,0:T(8,128)(2,1)S(1)}, bf16[1536,256]{1,0:T(8,128)(2,1)S(1)}, u32[]{:S(2)}, u32[]{:S(2)}) collective-permute-start(bf16[1536,256]{1,0:T(8,128)(2,1)S(1)} %get-tuple-element.67), channel_id=1, source_target_pairs={{0,1},{1,0},{2,3},{3,2},{4,7},{5,6},{6,5},{7,4},{8,9},{9,8},{10,11... | collective-permute-start | bytes 2359304 | tf_op jit(solution)/shard_map/ppermute | solution.py:450
  110.6 12.9 %collective-permute-start.35 = (bf16[1536,128]{1,0:T(8,128)(2,1)S(1)}, bf16[1536,128]{1,0:T(8,128)(2,1)S(1)}, u32[]{:S(2)}, u32[]{:S(2)}) collective-permute-start(bf16[1536,128]{1,0:T(8,128)(2,1)S(1)} %shard_map.107), channel_id=1, source_target_pairs={{0,8},{8,0},{16,24},{24,16},{1,9},{9,1},{17,25},{25,17},{2,10},{10... | collective-permute-start | bytes 1179656 | tf_op jit(solution)/shard_map/ppermute | solution.py:477
  111.9 11.6 %collective-permute-start.37 = (bf16[1536,128]{1,0:T(8,128)(2,1)S(1)}, bf16[1536,128]{1,0:T(8,128)(2,1)S(1)}, u32[]{:S(2)}, u32[]{:S(2)}) collective-permute-start(bf16[1536,128]{1,0:T(8,128)(2,1)S(1)} %shard_map.108), channel_id=1, source_target_pairs={{0,8},{4,12},{8,0},{12,4},{16,24},{20,28},{24,16},{28,20},{1,9},{5... | collective-permute-start | bytes 1179656 | tf_op jit(solution)/shard_map/ppermute | solution.py:477
  120.6 10.6 %collective-permute-start.39 = (bf16[1536,128]{1,0:T(8,128)(2,1)S(1)}, bf16[1536,128]{1,0:T(8,128)(2,1)S(1)}, u32[]{:S(2)}, u32[]{:S(2)}) collective-permute-start(bf16[1536,128]{1,0:T(8,128)(2,1)S(1)} %shard_map.109), channel_id=1, source_target_pairs={{4,12},{12,4},{20,28},{28,20},{5,13},{13,5},{21,29},{29,21},{6,14}... | collective-permute-start | bytes 1179656 | tf_op jit(solution)/shard_map/ppermute | solution.py:477
  (22 other events, 127.3 us)

commit v5 on v4

--- a/solution.py
+++ b/solution.py
@@ -319,7 +319,7 @@
     row_chunks(out.shape[0], body)
 
 
-def mix_rows(early, beta_mine, beta_other, amp_mine, amp_other, own, near_zero, near_one, *outs):
+def mix_rows(early, beta_mine, beta_other, amp_mine, amp_other, own, near_one, *outs):
     unit = amp_mine.shape[2]
     half = unit // 2
     odd = lax.axis_index("occ") % 2 == 1
@@ -336,8 +336,7 @@
         pick = lambda a, b: jnp.where(odd, a, b)
         send2[rows, :] = pick(there[:, :half], far)
         send3[rows, :] = there[:, half:]
-        send4[rows, :half] = pick(near_zero[rows, :], there[:, :half])
-        send4[rows, half:] = pick(far, there[:, half:])
+        send4[rows, :] = there
         keep2[rows, :] = pick(here[:, :half], beta[:, half:])
         keep3[rows, :] = here[:, half:]
         keep4[rows, :] = pick(beta, here)
@@ -354,15 +353,19 @@
 
 
 def last_rows(*refs):
-    keep, got, move_a, move_b, move_c, alpha, beta, hold_a, hold_b, sems = refs
+    keep, got, one, six, four, move_a, move_b, move_c = refs[:8]
+    alpha, beta, hold_a, hold_b, sems = refs[8:]
     odd = lax.axis_index("occ") % 2 == 1
     aux, half = move_a.shape
     step = aux // sems.shape[1]
     copies = []
     for i, start in enumerate(range(0, aux, step)):
         rows = slice(start, start + step)
-        final = (keep[rows, :] + got[rows, :].astype(F32)).astype(BF16)
-        low, high = final[:, :half], final[:, half:]
+        wide = got[rows, :].astype(F32)
+        zero = one[rows, :].astype(F32) + six[rows, :].astype(F32)
+        low = keep[rows, :half] + jnp.where(odd, zero, wide[:, :half])
+        high = keep[rows, half:] + jnp.where(odd, four[rows, :].astype(F32), wide[:, half:])
+        low, high = low.astype(BF16), high.astype(BF16)
         hold_a[rows, :half] = jnp.where(odd, move_b[rows, :], low)
         hold_a[rows, half:] = jnp.where(odd, move_c[rows, :], high)
         hold_b[rows, :half] = jnp.where(odd, low, move_a[rows, :])
@@ -439,17 +442,17 @@
     amp_own, gamma_own = tiles(b0, right, F32)
     amp_zero, gamma_zero = tiles(b1, right_zero, BF16)
 
-    def back(send, odd, even):
+    def back(send, step_of):
         pairs = [
             (d * layers + v, d * layers + (v ^ step))
             for d in range(blocks)
             for v in range(layers)
-            for step in [odd if d % 2 else even]
+            for step in [step_of(d % 2, v in (0, layers - 1))]
             if step
         ]
         return lax.ppermute(send, ("occ", "vir"), pairs)
 
-    got_one = back(gamma_zero, 0, 3)
+    got_one = back(gamma_zero, lambda odd, outer: 3 if outer or not odd else 0)
     b2, b2_other = both(fit(square, near_beta[1]))
     amp_one, gamma_one = tiles(b2, right_one, BF16)
     betas, amps = (b0, b0_other, b1, b1_other), (*amp_own, *amp_zero)
@@ -464,13 +467,14 @@
         b2_other,
         *amp_one,
         gamma_own,
-        gamma_zero,
         gamma_one,
         flops=4 * aux * unit * unit,
     )
-    got_two = back(send2, 1, 3)
-    got_three = back(send3, 1, 0)
-    got_four = back(send4, 3, 1)
+    got_two = back(send2, lambda odd, outer: 1 if odd else 3)
+    got_three = back(send3, lambda odd, outer: 1 if odd else 0)
+    got_four = back(gamma_one, lambda odd, outer: 3 if odd else 0)
+    got_five = back(send4, lambda odd, outer: 0 if odd else 1)
+    got_six = back(gamma_zero, lambda odd, outer: 3 if odd and not outer else 0)
 
     def move(value, cores):
         pairs = [(d, d ^ 2) for d in range(blocks) if d % 2 in cores]
@@ -480,7 +484,7 @@
     second = call(sum_keep, thin, keep2, got_two)
     third = call(sum_keep, thin, keep3, got_three)
     moves = move(first, (0,)), move(second, (0, 1)), move(third, (1,))
-    out_alpha, out_beta = last(keep4, got_four, *moves)
+    out_alpha, out_beta = last(keep4, got_five, got_one, got_six, got_four, *moves)
     return out_alpha.reshape(aux, 1, unit), out_beta.reshape(aux, 1, unit)
 
 

time: 136 us -> 153 us (1.12)
  starting transfers between devices: 66.7 us -> 80.1 us
  waiting for transfers between devices: 46.6 us -> 49.6 us
    ppermute x4 -> x6, starting transfers between devices: 21.1 us -> 37.6 us  [back(): return lax.ppermute(send, ('occ', 'vir'), pairs)]
    ppermute x32, starting transfers between devices: 37.6 us -> 34.9 us  [swap(): return lax.ppermute(value, axis, pairs)]
    ppermute x32, waiting for transfers between devices: 27.6 us -> 30.2 us  [swap(): return lax.ppermute(value, axis, pairs)]
    ppermute x4 -> x6, waiting for transfers between devices: 11.4 us -> 13.8 us  [back(): return lax.ppermute(send, ('occ', 'vir'), pairs)]
    ppermute x3, waiting for transfers between devices: 7.68 us -> 5.64 us  [move(): return lax.ppermute(value, 'occ', pairs)]
  transfers between devices with their start and end apart: 40 -> 42, of which waited for: 13 -> 13; matrix products, arithmetic and copies ran while one was open for 0% -> 0% of each run, Pallas kernels for 14% -> 12%
where the time goes in v5:
time: 153 us
  starting transfers between devices  80.1 us (52%)
  waiting for transfers between devices  49.6 us (32%)
  Pallas kernels  20.5 us (13%)
    ppermute x6, starting transfers between devices, back(): return lax.ppermute(send, ('occ', 'vir'), pairs)  37.6 us
    ppermute x32, starting transfers between devices, swap(): return lax.ppermute(value, axis, pairs)  34.9 us
    ppermute x32, waiting for transfers between devices, swap(): return lax.ppermute(value, axis, pairs)  30.2 us
    pallas_call x24, Pallas kernels, call(): pl.pallas_call(kernel, out_shape=shapes, in_specs=specs or [VMEM] * len(a...  19.2 us
    ppermute x6, waiting for transfers between devices, back(): return lax.ppermute(send, ('occ', 'vir'), pairs)  13.8 us
    ppermute x3, waiting for transfers between devices, move(): return lax.ppermute(value, 'occ', pairs)  5.64 us
    ppermute x3, starting transfers between devices, move(): return lax.ppermute(value, 'occ', pairs)  4.53 us
  transfers between devices with their start and end apart: 42, of which 13 were waited for; matrix products, arithmetic and copies ran while one was open for 0% of the time, Pallas kernels for 12%

profile of v5, /device:TPU:1, one launch (start us, length us, event | category | flops | bytes accessed | tf_op | source)
XLA Modules:
  0.0 152.7 jit_solution(12884379514060658409)
XLA Ops:
  2.3 2.1 %collective-permute-start.19 = (bf16[2,192,256]{2,1,0:T(8,128)(2,1)S(1)}, bf16[2,192,256]{2,1,0:T(8,128)(2,1)S(1)}, u32[]{:S(2)}, u32[]{:S(2)}) collective-permute-start(bf16[2,192,256]{2,1,0:T(8,128)(2,1)S(1)} %get-tuple-element.50), channel_id=1, source_target_pairs={{0,8},{4,12},{8,0},{12,4},{16,24},{20,28},{24,16},{28,20},{1,9},{5... | collective-permute-start | bytes 589832 | tf_op jit(solution)/shard_map/ppermute | solution.py:16
  5.6 3.3 %collective-permute-done.19.refs_1_ = bf16[2,192,256]{2,1,0:T(8,128)(2,1)S(1)} collective-permute-done((bf16[2,192,256]{2,1,0:T(8,128)(2,1)S(1)}, bf16[2,192,256]{2,1,0:T(8,128)(2,1)S(1)}, u32[]{:S(2)}, u32[]{:S(2)}) %collective-permute-start.19) | collective-permute-done | bytes 196640 | tf_op jit(solution)/shard_map/ppermute | solution.py:16
  9.9 4.3 %collective-permute-done.21.refs_3_ = bf16[2,192,256]{2,1,0:T(8,128)(2,1)S(1)} collective-permute-done((bf16[2,192,256]{2,1,0:T(8,128)(2,1)S(1)}, bf16[2,192,256]{2,1,0:T(8,128)(2,1)S(1)}, u32[]{:S(2)}, u32[]{:S(2)}) %collective-permute-start.21) | collective-permute-done | bytes 196640 | tf_op jit(solution)/shard_map/ppermute | solution.py:16
  17.5 2.3 %collective-permute-start.1 = (bf16[48,768]{1,0:T(8,128)(2,1)S(1)}, bf16[48,768]{1,0:T(8,128)(2,1)S(1)}, u32[]{:S(2)}, u32[]{:S(2)}) collective-permute-start(bf16[48,768]{1,0:T(8,128)(2,1)S(1)} %get-tuple-element.39), channel_id=1, source_target_pairs={{0,2},{1,3},{2,0},{3,1},{4,6},{5,7},{6,4},{7,5},{8,10},{9,11},{10,... | collective-permute-start | bytes 221192 | tf_op jit(solution)/shard_map/ppermute | solution.py:16
  21.9 3.0 %collective-permute-done.2.refs_2_ = bf16[48,768]{1,0:T(8,128)(2,1)S(1)} collective-permute-done((bf16[48,768]{1,0:T(8,128)(2,1)S(1)}, bf16[48,768]{1,0:T(8,128)(2,1)S(1)}, u32[]{:S(2)}, u32[]{:S(2)}) %collective-permute-start.2) | collective-permute-done | bytes 73760 | tf_op jit(solution)/shard_map/ppermute | solution.py:16
  26.5 3.0 %collective-permute-start.7 = (bf16[3,48,768]{2,1,0:T(8,128)(2,1)S(1)}, bf16[3,48,768]{2,1,0:T(8,128)(2,1)S(1)}, u32[]{:S(2)}, u32[]{:S(2)}) collective-permute-start(bf16[3,48,768]{2,1,0:T(8,128)(2,1)S(1)} %shard_map.87.refs_0_), channel_id=1, source_target_pairs={{0,4},{4,0},{8,12},{12,8},{16,20},{20,16},{24,28},{28,24},{1,5},{5... | collective-permute-start | bytes 663560 | tf_op jit(solution)/shard_map/ppermute | solution.py:16
  32.6 4.2 %collective-permute-done.12.refs_1_ = bf16[2,192,256]{2,1,0:T(8,128)(2,1)S(1)} collective-permute-done((bf16[2,192,256]{2,1,0:T(8,128)(2,1)S(1)}, bf16[2,192,256]{2,1,0:T(8,128)(2,1)S(1)}, u32[]{:S(2)}, u32[]{:S(2)}) %collective-permute-start.12) | collective-permute-done | bytes 196640 | tf_op jit(solution)/shard_map/ppermute | solution.py:16
  38.3 2.6 %collective-permute-done.14.refs_3_ = bf16[2,192,256]{2,1,0:T(8,128)(2,1)S(1)} collective-permute-done((bf16[2,192,256]{2,1,0:T(8,128)(2,1)S(1)}, bf16[2,192,256]{2,1,0:T(8,128)(2,1)S(1)}, u32[]{:S(2)}, u32[]{:S(2)}) %collective-permute-start.14) | collective-permute-done | bytes 196640 | tf_op jit(solution)/shard_map/ppermute | solution.py:16
  41.0 5.4 %collective-permute-start.8 = (bf16[3,48,768]{2,1,0:T(8,128)(2,1)S(1)}, bf16[3,48,768]{2,1,0:T(8,128)(2,1)S(1)}, u32[]{:S(2)}, u32[]{:S(2)}) collective-permute-start(bf16[3,48,768]{2,1,0:T(8,128)(2,1)S(1)} %collective-permute-done.3.by_x.refs_1_), channel_id=1, source_target_pairs={{0,4},{4,0},{8,12},{12,8},{16,20},{20,16},{24,28},{28,24},{1,5},{5... | collective-permute-start | bytes 663560 | tf_op jit(solution)/shard_map/ppermute | solution.py:16
  46.9 2.2 %collective-permute-start.11 = (bf16[3,48,384]{2,1,0:T(8,128)(2,1)S(1)}, bf16[3,48,384]{2,1,0:T(8,128)(2,1)S(1)}, u32[]{:S(2)}, u32[]{:S(2)}) collective-permute-start(bf16[3,48,384]{2,1,0:T(8,128)(2,1)S(1)} %collective-permute-done.6.refs_4_), channel_id=1, source_target_pairs={{0,4},{4,0},{8,12},{12,8},{16,20},{20,16},{24,28},{28,24},{1,5},{5... | collective-permute-start | bytes 331784 | tf_op jit(solution)/shard_map/ppermute | solution.py:16
  54.7 1.9 %collective-permute-start.30 = (bf16[1536,128]{1,0:T(8,128)(2,1)S(1)}, bf16[1536,128]{1,0:T(8,128)(2,1)S(1)}, u32[]{:S(2)}, u32[]{:S(2)}) collective-permute-start(bf16[1536,128]{1,0:T(8,128)(2,1)S(1)} %get-tuple-element.48.refs_1_), channel_id=1, source_target_pairs={{0,3},{1,2},{2,1},{3,0},{4,7},{5,6},{6,5},{7,4},{8,11},{9,10},{10,... | collective-permute-start | bytes 1179656 | tf_op jit(solution)/shard_map/ppermute | solution.py:16
  56.6 3.1 %collective-permute-start.26 = (f32[1]{0:T(128)}, f32[1]{0:T(128)}, u32[]{:S(2)}, u32[]{:S(2)}) collective-permute-start(f32[1]{0:T(128)} %param.10), channel_id=1, source_target_pairs={{0,0},{12,4},{8,8},{4,12},{16,16},{28,20},{24,24},{20,28},{1,1},{1... | collective-permute-start | bytes 20 | tf_op jit(solution)/shard_map/ppermute | solution.py:407
  62.6 4.3 %collective-permute-done.30.refs_0_ = bf16[1536,128]{1,0:T(8,128)(2,1)S(1)} collective-permute-done((bf16[1536,128]{1,0:T(8,128)(2,1)S(1)}, bf16[1536,128]{1,0:T(8,128)(2,1)S(1)}, u32[]{:S(2)}, u32[]{:S(2)}) %collective-permute-start.30) | collective-permute-done | bytes 393248 | tf_op jit(solution)/shard_map/ppermute | solution.py:16
  66.9 2.1 %collective-permute-start.27 = (f32[1]{0:T(128)}, f32[1]{0:T(128)}, u32[]{:S(2)}, u32[]{:S(2)}) collective-permute-start(f32[1]{0:T(128)} %collective-permute-done.26.occ_a), channel_id=1, source_target_pairs={{0,4},{4,0},{8,12},{12,8},{16,20},{20,16},{24,28},{28,24},{1,5},{5... | collective-permute-start | bytes 20 | tf_op jit(solution)/shard_map/ppermute | solution.py:16
  70.4 5.0 %collective-permute-done.17.refs_0_.vir_n = bf16[1552,128]{1,0:T(8,128)(2,1)S(1)} collective-permute-done((bf16[1552,128]{1,0:T(8,128)(2,1)S(1)}, bf16[1552,128]{1,0:T(8,128)(2,1)S(1)}, u32[]{:S(2)}, u32[]{:S(2)}) %collective-permute-start.17) | collective-permute-done | bytes 397344 | tf_op jit(solution)/shard_map/ppermute | solution.py:16
  78.2 2.0 %shard_map.100 = (f32[4,256]{1,0:T(4,128)S(1)}, f32[256,128]{1,0:T(8,128)S(1)}, f32[128,128]{1,0:T(8,128)S(1)}, f32[128,128]{1,0:T(8,128)S(1)}) custom-call(f32[1]{0:T(128)} %collective-permute-done.26.occ_a, f32[1]{0:T(128)} %collective-permute-done.27.occ_o, f32[8]{0:T(128)S(1)} %copy-done.5, f32[1024]{0:T(1024)S(1)} %copy-done.3, f32[1,256]{1,0:T(1,128)S(1)} %bitcast.4, ...), custom_call_target="tpu_custom_call" | custom-call | bytes 1048576 | tf_op jit(solution)/shard_map/pallas_call | solution.py:32
  80.2 2.0 %shard_map.101 = (bf16[2,256,256]{2,1,0:T(8,128)(2,1)S(1)}, bf16[2,256,256]{2,1,0:T(8,128)(2,1)S(1)}, f32[1536,256]{1,0:T(8,128)S(1)}) custom-call(bf16[1536,256]{1,0:T(8,128)(2,1)S(1)} %shard_map.98.a0, bf16[1536,256]{1,0:T(8,128)(2,1)S(1)} %shard_map.99.a1, bf16[1536,256]{1,0:T(8,128)(2,1)S(1)} %collective-permute-done.24.o0, ...), custom_call_target="tpu_custom_call" | custom-call | flops 1610612736 | bytes 1048576 | tf_op jit(solution)/shard_map/pallas_call | solution.py:32
  86.5 3.8 %collective-permute-start.34 = (bf16[1536,128]{1,0:T(8,128)(2,1)S(1)}, bf16[1536,128]{1,0:T(8,128)(2,1)S(1)}, u32[]{:S(2)}, u32[]{:S(2)}) collective-permute-start(bf16[1536,128]{1,0:T(8,128)(2,1)S(1)} %get-tuple-element.67), channel_id=1, source_target_pairs={{0,3},{1,2},{2,1},{3,0},{4,7},{7,4},{8,11},{9,10},{10,9},{11,8},{1... | collective-permute-start | bytes 1179656 | tf_op jit(solution)/shard_map/ppermute | solution.py:453
  93.2 28.6 %collective-permute-start.40 = (bf16[1536,128]{1,0:T(8,128)(2,1)S(1)}, bf16[1536,128]{1,0:T(8,128)(2,1)S(1)}, u32[]{:S(2)}, u32[]{:S(2)}) collective-permute-start(bf16[1536,128]{1,0:T(8,128)(2,1)S(1)} %get-tuple-element.71), channel_id=1, source_target_pairs={{4,5},{5,4},{6,7},{7,6},{12,13},{13,12},{14,15},{15,14},{20,21},{2... | collective-permute-start | bytes 1179656 | tf_op jit(solution)/shard_map/ppermute | solution.py:453
  121.8 3.8 %collective-permute-start.36 = (bf16[1536,128]{1,0:T(8,128)(2,1)S(1)}, bf16[1536,128]{1,0:T(8,128)(2,1)S(1)}, u32[]{:S(2)}, u32[]{:S(2)}) collective-permute-start(bf16[1536,128]{1,0:T(8,128)(2,1)S(1)} %get-tuple-element.64.near_one), channel_id=1, source_target_pairs={{4,7},{5,6},{6,5},{7,4},{12,15},{13,14},{14,13},{15,12},{20,23},{2... | collective-permute-start | bytes 1179656 | tf_op jit(solution)/shard_map/ppermute | solution.py:453
  127.9 7.0 %collective-permute-done.38.got = bf16[1536,128]{1,0:T(8,128)(2,1)S(1)} collective-permute-done((bf16[1536,128]{1,0:T(8,128)(2,1)S(1)}, bf16[1536,128]{1,0:T(8,128)(2,1)S(1)}, u32[]{:S(2)}, u32[]{:S(2)}) %collective-permute-start.38) | collective-permute-done | bytes 393248 | tf_op jit(solution)/shard_map/ppermute | solution.py:453
  134.9 2.9 %collective-permute-start.41 = (bf16[1536,128]{1,0:T(8,128)(2,1)S(1)}, bf16[1536,128]{1,0:T(8,128)(2,1)S(1)}, u32[]{:S(2)}, u32[]{:S(2)}) collective-permute-start(bf16[1536,128]{1,0:T(8,128)(2,1)S(1)} %shard_map.109), channel_id=1, source_target_pairs={{4,12},{12,4},{20,28},{28,20},{5,13},{13,5},{21,29},{29,21},{6,14}... | collective-permute-start | bytes 1179656 | tf_op jit(solution)/shard_map/ppermute | solution.py:481
  137.8 6.8 %collective-permute-done.36.refs_4_ = bf16[1536,128]{1,0:T(8,128)(2,1)S(1)} collective-permute-done((bf16[1536,128]{1,0:T(8,128)(2,1)S(1)}, bf16[1536,128]{1,0:T(8,128)(2,1)S(1)}, u32[]{:S(2)}, u32[]{:S(2)}) %collective-permute-start.36) | collective-permute-done | bytes 393248 | tf_op jit(solution)/shard_map/ppermute | solution.py:453
  145.6 5.6 %collective-permute-done.39.refs_6_ = bf16[1536,128]{1,0:T(8,128)(2,1)S(1)} collective-permute-done((bf16[1536,128]{1,0:T(8,128)(2,1)S(1)}, bf16[1536,128]{1,0:T(8,128)(2,1)S(1)}, u32[]{:S(2)}, u32[]{:S(2)}) %collective-permute-start.39) | collective-permute-done | bytes 393248 | tf_op jit(solution)/shard_map/ppermute | solution.py:481
  (97 shorter events, 40.2 us)
Async XLA Ops:
  5.6 8.5 %collective-permute-start.21 = (bf16[2,192,256]{2,1,0:T(8,128)(2,1)S(1)}, bf16[2,192,256]{2,1,0:T(8,128)(2,1)S(1)}, u32[]{:S(2)}, u32[]{:S(2)}) collective-permute-start(bf16[2,192,256]{2,1,0:T(8,128)(2,1)S(1)} %get-tuple-element.52), channel_id=1, source_target_pairs={{0,24},{4,28},{8,16},{12,20},{16,8},{20,12},{24,0},{28,4},{1,25},{... | collective-permute-start | bytes 589832 | tf_op jit(solution)/shard_map/ppermute | solution.py:16
  19.9 33.0 %collective-permute-start.23 = (bf16[1536,256]{1,0:T(8,128)(2,1)S(1)}, bf16[1536,256]{1,0:T(8,128)(2,1)S(1)}, u32[]{:S(2)}, u32[]{:S(2)}) collective-permute-start(bf16[1536,256]{1,0:T(8,128)(2,1)S(1)} %shard_map.97.refs_0_), channel_id=1, source_target_pairs={{0,1},{1,0},{2,3},{3,2},{4,5},{5,4},{6,7},{7,6},{8,9},{9,8},{10,11... | collective-permute-start | bytes 2359304 | tf_op jit(solution)/shard_map/ppermute | solution.py:16
  26.5 19.9 %collective-permute-start.7 = (bf16[3,48,768]{2,1,0:T(8,128)(2,1)S(1)}, bf16[3,48,768]{2,1,0:T(8,128)(2,1)S(1)}, u32[]{:S(2)}, u32[]{:S(2)}) collective-permute-start(bf16[3,48,768]{2,1,0:T(8,128)(2,1)S(1)} %shard_map.87.refs_0_), channel_id=1, source_target_pairs={{0,4},{4,0},{8,12},{12,8},{16,20},{20,16},{24,28},{28,24},{1,5},{5... | collective-permute-start | bytes 663560 | tf_op jit(solution)/shard_map/ppermute | solution.py:16
  31.4 9.6 %collective-permute-start.14 = (bf16[2,192,256]{2,1,0:T(8,128)(2,1)S(1)}, bf16[2,192,256]{2,1,0:T(8,128)(2,1)S(1)}, u32[]{:S(2)}, u32[]{:S(2)}) collective-permute-start(bf16[2,192,256]{2,1,0:T(8,128)(2,1)S(1)} %get-tuple-element.46), channel_id=1, source_target_pairs={{0,24},{4,28},{8,16},{12,20},{16,8},{20,12},{24,0},{28,4},{1,25},{... | collective-permute-start | bytes 589832 | tf_op jit(solution)/shard_map/ppermute | solution.py:16
  36.9 9.6 %collective-permute-start.5 = (bf16[3,48,384]{2,1,0:T(8,128)(2,1)S(1)}, bf16[3,48,384]{2,1,0:T(8,128)(2,1)S(1)}, u32[]{:S(2)}, u32[]{:S(2)}) collective-permute-start(bf16[3,48,384]{2,1,0:T(8,128)(2,1)S(1)} %get-tuple-element.41), channel_id=1, source_target_pairs={{0,8},{4,12},{8,0},{12,4},{16,24},{20,28},{24,16},{28,20},{1,9},{5... | collective-permute-start | bytes 331784 | tf_op jit(solution)/shard_map/ppermute | solution.py:16
  37.7 9.2 %collective-permute-start.6 = (bf16[3,48,384]{2,1,0:T(8,128)(2,1)S(1)}, bf16[3,48,384]{2,1,0:T(8,128)(2,1)S(1)}, u32[]{:S(2)}, u32[]{:S(2)}) collective-permute-start(bf16[3,48,384]{2,1,0:T(8,128)(2,1)S(1)} %get-tuple-element.42), channel_id=1, source_target_pairs={{0,16},{4,20},{8,24},{12,28},{16,0},{20,4},{24,8},{28,12},{1,17},{... | collective-permute-start | bytes 331784 | tf_op jit(solution)/shard_map/ppermute | solution.py:16
  41.0 9.1 %collective-permute-start.8 = (bf16[3,48,768]{2,1,0:T(8,128)(2,1)S(1)}, bf16[3,48,768]{2,1,0:T(8,128)(2,1)S(1)}, u32[]{:S(2)}, u32[]{:S(2)}) collective-permute-start(bf16[3,48,768]{2,1,0:T(8,128)(2,1)S(1)} %collective-permute-done.3.by_x.refs_1_), channel_id=1, source_target_pairs={{0,4},{4,0},{8,12},{12,8},{16,20},{20,16},{24,28},{28,24},{1,5},{5... | collective-permute-start | bytes 663560 | tf_op jit(solution)/shard_map/ppermute | solution.py:16
  52.5 27.7 %collective-permute-start.24 = (bf16[1536,256]{1,0:T(8,128)(2,1)S(1)}, bf16[1536,256]{1,0:T(8,128)(2,1)S(1)}, u32[]{:S(2)}, u32[]{:S(2)}) collective-permute-start(bf16[1536,256]{1,0:T(8,128)(2,1)S(1)} %shard_map.98.a0), channel_id=1, source_target_pairs={{0,4},{4,0},{8,12},{12,8},{16,20},{20,16},{24,28},{28,24},{1,5},{5... | collective-permute-start | bytes 2359304 | tf_op jit(solution)/shard_map/ppermute | solution.py:16
  54.3 25.9 %collective-permute-start.25 = (bf16[1536,256]{1,0:T(8,128)(2,1)S(1)}, bf16[1536,256]{1,0:T(8,128)(2,1)S(1)}, u32[]{:S(2)}, u32[]{:S(2)}) collective-permute-start(bf16[1536,256]{1,0:T(8,128)(2,1)S(1)} %shard_map.99.a1), channel_id=1, source_target_pairs={{0,4},{4,0},{8,12},{12,8},{16,20},{20,16},{24,28},{28,24},{1,5},{5... | collective-permute-start | bytes 2359304 | tf_op jit(solution)/shard_map/ppermute | solution.py:16
  54.7 12.2 %collective-permute-start.30 = (bf16[1536,128]{1,0:T(8,128)(2,1)S(1)}, bf16[1536,128]{1,0:T(8,128)(2,1)S(1)}, u32[]{:S(2)}, u32[]{:S(2)}) collective-permute-start(bf16[1536,128]{1,0:T(8,128)(2,1)S(1)} %get-tuple-element.48.refs_1_), channel_id=1, source_target_pairs={{0,3},{1,2},{2,1},{3,0},{4,7},{5,6},{6,5},{7,4},{8,11},{9,10},{10,... | collective-permute-start | bytes 1179656 | tf_op jit(solution)/shard_map/ppermute | solution.py:16
  59.7 15.7 %collective-permute-start.17 = (bf16[1552,128]{1,0:T(8,128)(2,1)S(1)}, bf16[1552,128]{1,0:T(8,128)(2,1)S(1)}, u32[]{:S(2)}, u32[]{:S(2)}) collective-permute-start(bf16[1552,128]{1,0:T(8,128)(2,1)S(1)} %get-tuple-element.47.refs_0_), channel_id=1, source_target_pairs={{0,3},{1,2},{2,1},{3,0},{4,7},{5,6},{6,5},{7,4},{8,11},{9,10},{10,... | collective-permute-start | bytes 1191944 | tf_op jit(solution)/shard_map/ppermute | solution.py:16
  62.5 23.4 %collective-permute-start.16 = (bf16[1536,256]{1,0:T(8,128)(2,1)S(1)}, bf16[1536,256]{1,0:T(8,128)(2,1)S(1)}, u32[]{:S(2)}, u32[]{:S(2)}) collective-permute-start(bf16[1536,256]{1,0:T(8,128)(2,1)S(1)} %shard_map.93.beta.refs_0_), channel_id=1, source_target_pairs={{0,4},{4,0},{8,12},{12,8},{16,20},{20,16},{24,28},{28,24},{1,5},{5... | collective-permute-start | bytes 2359304 | tf_op jit(solution)/shard_map/ppermute | solution.py:16
  66.9 11.2 %collective-permute-start.27 = (f32[1]{0:T(128)}, f32[1]{0:T(128)}, u32[]{:S(2)}, u32[]{:S(2)}) collective-permute-start(f32[1]{0:T(128)} %collective-permute-done.26.occ_a), channel_id=1, source_target_pairs={{0,4},{4,0},{8,12},{12,8},{16,20},{20,16},{24,28},{28,24},{1,5},{5... | collective-permute-start | bytes 20 | tf_op jit(solution)/shard_map/ppermute | solution.py:16
  75.4 16.7 %collective-permute-start.31 = (bf16[1536,128]{1,0:T(8,128)(2,1)S(1)}, bf16[1536,128]{1,0:T(8,128)(2,1)S(1)}, u32[]{:S(2)}, u32[]{:S(2)}) collective-permute-start(bf16[1536,128]{1,0:T(8,128)(2,1)S(1)} %shard_map.104.beta.beta_mine), channel_id=1, source_target_pairs={{0,4},{4,0},{8,12},{12,8},{16,20},{20,16},{24,28},{28,24},{1,5},{5... | collective-permute-start | bytes 1179656 | tf_op jit(solution)/shard_map/ppermute | solution.py:16
  78.1 8.4 %collective-permute-start.18 = (bf16[1536,128]{1,0:T(8,128)(2,1)S(1)}, bf16[1536,128]{1,0:T(8,128)(2,1)S(1)}, u32[]{:S(2)}, u32[]{:S(2)}) collective-permute-start(bf16[1536,128]{1,0:T(8,128)(2,1)S(1)} %shard_map.94.beta.refs_2_), channel_id=1, source_target_pairs={{0,4},{4,0},{8,12},{12,8},{16,20},{20,16},{24,28},{28,24},{1,5},{5... | collective-permute-start | bytes 1179656 | tf_op jit(solution)/shard_map/ppermute | solution.py:16
  82.1 8.2 %collective-permute-start.28 = (bf16[2,256,256]{2,1,0:T(8,128)(2,1)S(1)}, bf16[2,256,256]{2,1,0:T(8,128)(2,1)S(1)}, u32[]{:S(2)}, u32[]{:S(2)}) collective-permute-start(bf16[2,256,256]{2,1,0:T(8,128)(2,1)S(1)} %get-tuple-element.56), channel_id=1, source_target_pairs={{0,4},{4,0},{8,12},{12,8},{16,20},{20,16},{24,28},{28,24},{1,5},{5... | collective-permute-start | bytes 786440 | tf_op jit(solution)/shard_map/ppermute | solution.py:16
  86.5 39.8 %collective-permute-start.34 = (bf16[1536,128]{1,0:T(8,128)(2,1)S(1)}, bf16[1536,128]{1,0:T(8,128)(2,1)S(1)}, u32[]{:S(2)}, u32[]{:S(2)}) collective-permute-start(bf16[1536,128]{1,0:T(8,128)(2,1)S(1)} %get-tuple-element.67), channel_id=1, source_target_pairs={{0,3},{1,2},{2,1},{3,0},{4,7},{7,4},{8,11},{9,10},{10,9},{11,8},{1... | collective-permute-start | bytes 1179656 | tf_op jit(solution)/shard_map/ppermute | solution.py:453
  93.2 33.9 %collective-permute-start.40 = (bf16[1536,128]{1,0:T(8,128)(2,1)S(1)}, bf16[1536,128]{1,0:T(8,128)(2,1)S(1)}, u32[]{:S(2)}, u32[]{:S(2)}) collective-permute-start(bf16[1536,128]{1,0:T(8,128)(2,1)S(1)} %get-tuple-element.71), channel_id=1, source_target_pairs={{4,5},{5,4},{6,7},{7,6},{12,13},{13,12},{14,15},{15,14},{20,21},{2... | collective-permute-start | bytes 1179656 | tf_op jit(solution)/shard_map/ppermute | solution.py:453
  121.7 13.2 %collective-permute-start.38 = (bf16[1536,128]{1,0:T(8,128)(2,1)S(1)}, bf16[1536,128]{1,0:T(8,128)(2,1)S(1)}, u32[]{:S(2)}, u32[]{:S(2)}) collective-permute-start(bf16[1536,128]{1,0:T(8,128)(2,1)S(1)} %get-tuple-element.69), channel_id=1, source_target_pairs={{0,3},{1,2},{2,1},{3,0},{4,5},{5,4},{6,7},{7,6},{8,11},{9,10},{10,... | collective-permute-start | bytes 1179656 | tf_op jit(solution)/shard_map/ppermute | solution.py:453
  121.8 22.8 %collective-permute-start.36 = (bf16[1536,128]{1,0:T(8,128)(2,1)S(1)}, bf16[1536,128]{1,0:T(8,128)(2,1)S(1)}, u32[]{:S(2)}, u32[]{:S(2)}) collective-permute-start(bf16[1536,128]{1,0:T(8,128)(2,1)S(1)} %get-tuple-element.64.near_one), channel_id=1, source_target_pairs={{4,7},{5,6},{6,5},{7,4},{12,15},{13,14},{14,13},{15,12},{20,23},{2... | collective-permute-start | bytes 1179656 | tf_op jit(solution)/shard_map/ppermute | solution.py:453
  125.6 25.7 %collective-permute-start.33 = (bf16[1536,256]{1,0:T(8,128)(2,1)S(1)}, bf16[1536,256]{1,0:T(8,128)(2,1)S(1)}, u32[]{:S(2)}, u32[]{:S(2)}) collective-permute-start(bf16[1536,256]{1,0:T(8,128)(2,1)S(1)} %get-tuple-element.66), channel_id=1, source_target_pairs={{0,1},{1,0},{2,3},{3,2},{8,9},{9,8},{10,11},{11,10},{16,17},{17,16... | collective-permute-start | bytes 2359304 | tf_op jit(solution)/shard_map/ppermute | solution.py:453
  126.3 19.3 %collective-permute-start.35 = (bf16[1536,128]{1,0:T(8,128)(2,1)S(1)}, bf16[1536,128]{1,0:T(8,128)(2,1)S(1)}, u32[]{:S(2)}, u32[]{:S(2)}) collective-permute-start(bf16[1536,128]{1,0:T(8,128)(2,1)S(1)} %get-tuple-element.67), channel_id=1, source_target_pairs={{5,6},{6,5},{13,14},{14,13},{21,22},{22,21},{29,30},{30,29}} | collective-permute-start | bytes 1179656 | tf_op jit(solution)/shard_map/ppermute | solution.py:453
  127.1 18.5 %collective-permute-start.37 = (bf16[1536,128]{1,0:T(8,128)(2,1)S(1)}, bf16[1536,128]{1,0:T(8,128)(2,1)S(1)}, u32[]{:S(2)}, u32[]{:S(2)}) collective-permute-start(bf16[1536,128]{1,0:T(8,128)(2,1)S(1)} %shard_map.107), channel_id=1, source_target_pairs={{0,8},{8,0},{16,24},{24,16},{1,9},{9,1},{17,25},{25,17},{2,10},{10... | collective-permute-start | bytes 1179656 | tf_op jit(solution)/shard_map/ppermute | solution.py:481
  134.9 10.7 %collective-permute-start.41 = (bf16[1536,128]{1,0:T(8,128)(2,1)S(1)}, bf16[1536,128]{1,0:T(8,128)(2,1)S(1)}, u32[]{:S(2)}, u32[]{:S(2)}) collective-permute-start(bf16[1536,128]{1,0:T(8,128)(2,1)S(1)} %shard_map.109), channel_id=1, source_target_pairs={{4,12},{12,4},{20,28},{28,20},{5,13},{13,5},{21,29},{29,21},{6,14}... | collective-permute-start | bytes 1179656 | tf_op jit(solution)/shard_map/ppermute | solution.py:481
  (24 other events, 145.9 us)

commit v6 on v5

--- a/solution.py
+++ b/solution.py
@@ -305,43 +305,50 @@
     )
 
 
+def alpha_rows(u, rows, betas, amps, total=None):
+    for beta, amp in zip(betas, amps):
+        term = dots(beta[rows, :], amp[u], 1, 0)
+        total = term if total is None else total + term
+    return total
+
+
 def early_rows(*refs):
     betas, amps, out = refs[:4], refs[4:8], refs[8]
-    unit = amps[0].shape[2]
 
     def body(rows):
-        for u in (0, 1):
-            total = dots(betas[0][rows, :], amps[0][u], 1, 0)
-            for beta, amp in zip(betas[1:], amps[1:]):
-                total = total + dots(beta[rows, :], amp[u], 1, 0)
-            out[rows, u * unit : (u + 1) * unit] = total
+        out[rows, :] = alpha_rows(1, rows, betas, amps)
 
     row_chunks(out.shape[0], body)
 
 
-def mix_rows(early, beta_mine, beta_other, amp_mine, amp_other, own, near_one, *outs):
-    unit = amp_mine.shape[2]
-    half = unit // 2
+def mix_rows(early, near_one, *refs):
+    betas, amps = refs[:2], refs[2:4]
+    send2, send3, send4 = refs[4:]
+    half = near_one.shape[1]
     odd = lax.axis_index("occ") % 2 == 1
-    send2, send3, send4, keep2, keep3, keep4 = outs
 
     def body(rows):
-        alpha = []
-        for u in (0, 1):
-            total = early[rows, u * unit : (u + 1) * unit]
-            total = total + dots(beta_mine[rows, :], amp_mine[u], 1, 0)
-            alpha.append(total + dots(beta_other[rows, :], amp_other[u], 1, 0))
-        here, there = alpha[0], alpha[1].astype(BF16)
-        beta, far = own[rows, :], near_one[rows, :]
-        pick = lambda a, b: jnp.where(odd, a, b)
-        send2[rows, :] = pick(there[:, :half], far)
+        there = alpha_rows(1, rows, betas, amps, early[rows, :]).astype(BF16)
+        send2[rows, :] = jnp.where(odd, there[:, :half], near_one[rows, :])
         send3[rows, :] = there[:, half:]
         send4[rows, :] = there
-        keep2[rows, :] = pick(here[:, :half], beta[:, half:])
+
+    row_chunks(early.shape[0], body)
+
+
+def keep_rows(own, *refs):
+    betas, amps = refs[:6], refs[6:12]
+    keep2, keep3, keep4 = refs[12:]
+    half = keep2.shape[1]
+    odd = lax.axis_index("occ") % 2 == 1
+
+    def body(rows):
+        here, beta = alpha_rows(0, rows, betas, amps), own[rows, :]
+        keep2[rows, :] = jnp.where(odd, here[:, :half], beta[:, half:])
         keep3[rows, :] = here[:, half:]
-        keep4[rows, :] = pick(beta, here)
-
-    row_chunks(early.shape[0], body, 256)
+        keep4[rows, :] = jnp.where(odd, beta, here)
+
+    row_chunks(own.shape[0], body)
 
 
 def sum_one(own_gamma, got, out):
@@ -456,20 +463,16 @@
     b2, b2_other = both(fit(square, near_beta[1]))
     amp_one, gamma_one = tiles(b2, right_one, BF16)
     betas, amps = (b0, b0_other, b1, b1_other), (*amp_own, *amp_zero)
-    pair = shape_of(aux, 2 * unit, dtype=F32)
-    early = call(early_rows, pair, *betas, *amps, flops=12 * aux * unit * unit)
-    thin, thin32 = shape_of(aux, half), shape_of(aux, half, dtype=F32)
-    send2, send3, send4, keep2, keep3, keep4 = call(
-        mix_rows,
-        [thin, thin, shape_of(aux, unit), thin32, thin32, shape_of(aux, unit, dtype=F32)],
-        early,
-        b2,
-        b2_other,
-        *amp_one,
-        gamma_own,
-        gamma_one,
-        flops=4 * aux * unit * unit,
-    )
+    work = 2 * aux * unit * unit
+    thin, wide = shape_of(aux, half), shape_of(aux, unit)
+    thin32, wide32 = shape_of(aux, half, dtype=F32), shape_of(aux, unit, dtype=F32)
+    early = call(early_rows, wide32, *betas, *amps, flops=3 * work)
+    ends = (b2, b2_other, *amp_one)
+    sends = call(mix_rows, [thin, thin, wide], early, gamma_one, *ends, flops=work)
+    send2, send3, send4 = sends
+    keeps = [thin32, thin32, wide32]
+    arrays = (*betas, *ends[:2], *amps, *ends[2:])
+    keep2, keep3, keep4 = call(keep_rows, keeps, gamma_own, *arrays, flops=4 * work)
     got_two = back(send2, lambda odd, outer: 1 if odd else 3)
     got_three = back(send3, lambda odd, outer: 1 if odd else 0)
     got_four = back(gamma_one, lambda odd, outer: 3 if odd else 0)

time: 153 us -> 155 us (1.013)
  the two profiles are of different devices: /device:TPU:1 before, /device:TPU:22 now
where the time goes in v6:
time: 155 us; the launch traced here: 154 us
  waiting for transfers between devices  78.6 us (51%)
  starting transfers between devices  52.5 us (34%)
  Pallas kernels  20.6 us (13%)
    ppermute x32, waiting for transfers between devices, swap(): return lax.ppermute(value, axis, pairs)  56 us
    ppermute x32, starting transfers between devices, swap(): return lax.ppermute(value, axis, pairs)  38 us
    pallas_call x25, Pallas kernels, call(): pl.pallas_call(kernel, out_shape=shapes, in_specs=specs or [VMEM] * len(a...  19.2 us
    ppermute x3, waiting for transfers between devices, move(): return lax.ppermute(value, 'occ', pairs)  13.2 us
    ppermute x6, waiting for transfers between devices, back(): return lax.ppermute(send, ('occ', 'vir'), pairs)  9.43 us
    ppermute x6, starting transfers between devices, back(): return lax.ppermute(send, ('occ', 'vir'), pairs)  7.96 us
    ppermute x3, starting transfers between devices, move(): return lax.ppermute(value, 'occ', pairs)  4.67 us
  transfers between devices with their start and end apart: 42, of which 16 were waited for; matrix products, arithmetic and copies ran while one was open for 0% of the time, Pallas kernels for 12%

profile of v6, /device:TPU:22, one launch (start us, length us, event | category | flops | bytes accessed | tf_op | source)
XLA Modules:
  0.0 154.2 jit_solution(2285199390440322786)
XLA Ops:
  3.4 2.4 %collective-permute-start.14 = (bf16[2,192,256]{2,1,0:T(8,128)(2,1)S(1)}, bf16[2,192,256]{2,1,0:T(8,128)(2,1)S(1)}, u32[]{:S(2)}, u32[]{:S(2)}) collective-permute-start(bf16[2,192,256]{2,1,0:T(8,128)(2,1)S(1)} %get-tuple-element.46), channel_id=1, source_target_pairs={{0,24},{4,28},{8,16},{12,20},{16,8},{20,12},{24,0},{28,4},{1,25},{... | collective-permute-start | bytes 589832 | tf_op jit(solution)/shard_map/ppermute | solution.py:16
  5.8 4.3 %collective-permute-done.12.refs_1_ = bf16[2,192,256]{2,1,0:T(8,128)(2,1)S(1)} collective-permute-done((bf16[2,192,256]{2,1,0:T(8,128)(2,1)S(1)}, bf16[2,192,256]{2,1,0:T(8,128)(2,1)S(1)}, u32[]{:S(2)}, u32[]{:S(2)}) %collective-permute-start.12) | collective-permute-done | bytes 196640 | tf_op jit(solution)/shard_map/ppermute | solution.py:16
  10.1 3.3 %collective-permute-done.13.refs_2_ = bf16[2,192,256]{2,1,0:T(8,128)(2,1)S(1)} collective-permute-done((bf16[2,192,256]{2,1,0:T(8,128)(2,1)S(1)}, bf16[2,192,256]{2,1,0:T(8,128)(2,1)S(1)}, u32[]{:S(2)}, u32[]{:S(2)}) %collective-permute-start.13) | collective-permute-done | bytes 196640 | tf_op jit(solution)/shard_map/ppermute | solution.py:16
  13.7 1.6 %collective-permute-start = (bf16[48,768]{1,0:T(8,128)(2,1)S(1)}, bf16[48,768]{1,0:T(8,128)(2,1)S(1)}, u32[]{:S(2)}, u32[]{:S(2)}) collective-permute-start(bf16[48,768]{1,0:T(8,128)(2,1)S(1)} %get-tuple-element.38), channel_id=1, source_target_pairs={{0,1},{1,0},{2,3},{3,2},{4,5},{5,4},{6,7},{7,6},{8,9},{9,8},{10,11... | collective-permute-start | bytes 221192 | tf_op jit(solution)/shard_map/ppermute | solution.py:16
  17.4 2.5 %collective-permute-start.16 = (bf16[1536,256]{1,0:T(8,128)(2,1)S(1)}, bf16[1536,256]{1,0:T(8,128)(2,1)S(1)}, u32[]{:S(2)}, u32[]{:S(2)}) collective-permute-start(bf16[1536,256]{1,0:T(8,128)(2,1)S(1)} %shard_map.92.refs_0_), channel_id=1, source_target_pairs={{0,1},{1,0},{2,3},{3,2},{4,5},{5,4},{6,7},{7,6},{8,9},{9,8},{10,11... | collective-permute-start | bytes 2359304 | tf_op jit(solution)/shard_map/ppermute | solution.py:16
  21.5 2.8 %collective-permute-done.2.refs_2_ = bf16[48,768]{1,0:T(8,128)(2,1)S(1)} collective-permute-done((bf16[48,768]{1,0:T(8,128)(2,1)S(1)}, bf16[48,768]{1,0:T(8,128)(2,1)S(1)}, u32[]{:S(2)}, u32[]{:S(2)}) %collective-permute-start.2) | collective-permute-done | bytes 73760 | tf_op jit(solution)/shard_map/ppermute | solution.py:16
  28.1 3.0 %collective-permute-done.4.by_y.refs_2_ = bf16[3,48,768]{2,1,0:T(8,128)(2,1)S(1)} collective-permute-done((bf16[3,48,768]{2,1,0:T(8,128)(2,1)S(1)}, bf16[3,48,768]{2,1,0:T(8,128)(2,1)S(1)}, u32[]{:S(2)}, u32[]{:S(2)}) %collective-permute-start.4) | collective-permute-done | bytes 221216 | tf_op jit(solution)/shard_map/ppermute | solution.py:16
  33.9 1.8 %collective-permute-start.21 = (bf16[2,192,256]{2,1,0:T(8,128)(2,1)S(1)}, bf16[2,192,256]{2,1,0:T(8,128)(2,1)S(1)}, u32[]{:S(2)}, u32[]{:S(2)}) collective-permute-start(bf16[2,192,256]{2,1,0:T(8,128)(2,1)S(1)} %get-tuple-element.50), channel_id=1, source_target_pairs={{0,24},{4,28},{8,16},{12,20},{16,8},{20,12},{24,0},{28,4},{1,25},{... | collective-permute-start | bytes 589832 | tf_op jit(solution)/shard_map/ppermute | solution.py:16
  35.7 2.4 %collective-permute-done.19.refs_1_ = bf16[2,192,256]{2,1,0:T(8,128)(2,1)S(1)} collective-permute-done((bf16[2,192,256]{2,1,0:T(8,128)(2,1)S(1)}, bf16[2,192,256]{2,1,0:T(8,128)(2,1)S(1)}, u32[]{:S(2)}, u32[]{:S(2)}) %collective-permute-start.19) | collective-permute-done | bytes 196640 | tf_op jit(solution)/shard_map/ppermute | solution.py:16
  39.3 2.6 %collective-permute-done.21.refs_3_ = bf16[2,192,256]{2,1,0:T(8,128)(2,1)S(1)} collective-permute-done((bf16[2,192,256]{2,1,0:T(8,128)(2,1)S(1)}, bf16[2,192,256]{2,1,0:T(8,128)(2,1)S(1)}, u32[]{:S(2)}, u32[]{:S(2)}) %collective-permute-start.21) | collective-permute-done | bytes 196640 | tf_op jit(solution)/shard_map/ppermute | solution.py:16
  43.6 3.1 %collective-permute-done.6.refs_4_ = bf16[3,48,384]{2,1,0:T(8,128)(2,1)S(1)} collective-permute-done((bf16[3,48,384]{2,1,0:T(8,128)(2,1)S(1)}, bf16[3,48,384]{2,1,0:T(8,128)(2,1)S(1)}, u32[]{:S(2)}, u32[]{:S(2)}) %collective-permute-start.6) | collective-permute-done | bytes 110624 | tf_op jit(solution)/shard_map/ppermute | solution.py:16
  52.4 1.9 %collective-permute-start.23 = (f32[1]{0:T(128)}, f32[1]{0:T(128)}, u32[]{:S(2)}, u32[]{:S(2)}) collective-permute-start(f32[1]{0:T(128)} %param.10), channel_id=1, source_target_pairs={{0,0},{12,4},{8,8},{4,12},{16,16},{28,20},{24,24},{20,28},{1,1},{1... | collective-permute-start | bytes 20 | tf_op jit(solution)/shard_map/ppermute | solution.py:414
  59.0 23.9 %collective-permute-done.28.refs_0_ = bf16[1536,128]{1,0:T(8,128)(2,1)S(1)} collective-permute-done((bf16[1536,128]{1,0:T(8,128)(2,1)S(1)}, bf16[1536,128]{1,0:T(8,128)(2,1)S(1)}, u32[]{:S(2)}, u32[]{:S(2)}) %collective-permute-start.28) | collective-permute-done | bytes 393248 | tf_op jit(solution)/shard_map/ppermute | solution.py:16
  85.6 5.9 %collective-permute-done.25.vir_n.refs_0_ = bf16[1552,128]{1,0:T(8,128)(2,1)S(1)} collective-permute-done((bf16[1552,128]{1,0:T(8,128)(2,1)S(1)}, bf16[1552,128]{1,0:T(8,128)(2,1)S(1)}, u32[]{:S(2)}, u32[]{:S(2)}) %collective-permute-start.25) | collective-permute-done | bytes 397344 | tf_op jit(solution)/shard_map/ppermute | solution.py:16
  91.4 13.0 %collective-permute-start.29 = (bf16[1536,128]{1,0:T(8,128)(2,1)S(1)}, bf16[1536,128]{1,0:T(8,128)(2,1)S(1)}, u32[]{:S(2)}, u32[]{:S(2)}) collective-permute-start(bf16[1536,128]{1,0:T(8,128)(2,1)S(1)} %shard_map.102.beta.refs_4_.refs_0_), channel_id=1, source_target_pairs={{0,4},{4,0},{8,12},{12,8},{16,20},{20,16},{24,28},{28,24},{1,5},{5... | collective-permute-start | bytes 1179656 | tf_op jit(solution)/shard_map/ppermute | solution.py:16
  105.9 1.9 %shard_map.99 = (f32[4,256]{1,0:T(4,128)S(1)}, f32[256,128]{1,0:T(8,128)S(1)}, f32[128,128]{1,0:T(8,128)S(1)}, f32[128,128]{1,0:T(8,128)S(1)}) custom-call(f32[1]{0:T(128)} %collective-permute-done.23.occ_a, f32[1]{0:T(128)} %collective-permute-done.24.occ_o, f32[8]{0:T(128)S(1)} %copy-done.5, f32[1024]{0:T(1024)S(1)} %copy-done.3, f32[1,256]{1,0:T(1,128)S(1)} %bitcast.4, ...), custom_call_target="tpu_custom_call" | custom-call | bytes 1048576 | tf_op jit(solution)/shard_map/pallas_call | solution.py:32
  107.9 2.0 %shard_map.100 = (bf16[2,256,256]{2,1,0:T(8,128)(2,1)S(1)}, bf16[2,256,256]{2,1,0:T(8,128)(2,1)S(1)}, f32[1536,256]{1,0:T(8,128)S(1)}) custom-call(bf16[1536,256]{1,0:T(8,128)(2,1)S(1)} %shard_map.93.a0, bf16[1536,256]{1,0:T(8,128)(2,1)S(1)} %shard_map.94.a1, bf16[1536,256]{1,0:T(8,128)(2,1)S(1)} %collective-permute-done.17.o0, ...), custom_call_target="tpu_custom_call" | custom-call | flops 1610612736 | bytes 1048576 | tf_op jit(solution)/shard_map/pallas_call | solution.py:32
  114.1 2.6 %collective-permute-start.34 = (bf16[1536,128]{1,0:T(8,128)(2,1)S(1)}, bf16[1536,128]{1,0:T(8,128)(2,1)S(1)}, u32[]{:S(2)}, u32[]{:S(2)}) collective-permute-start(bf16[1536,128]{1,0:T(8,128)(2,1)S(1)} %get-tuple-element.67), channel_id=1, source_target_pairs={{0,3},{1,2},{2,1},{3,0},{4,7},{7,4},{8,11},{9,10},{10,9},{11,8},{1... | collective-permute-start | bytes 1179656 | tf_op jit(solution)/shard_map/ppermute | solution.py:460
  121.1 1.9 %collective-permute-start.33 = (bf16[1536,256]{1,0:T(8,128)(2,1)S(1)}, bf16[1536,256]{1,0:T(8,128)(2,1)S(1)}, u32[]{:S(2)}, u32[]{:S(2)}) collective-permute-start(bf16[1536,256]{1,0:T(8,128)(2,1)S(1)} %get-tuple-element.66), channel_id=1, source_target_pairs={{0,1},{1,0},{2,3},{3,2},{8,9},{9,8},{10,11},{11,10},{16,17},{17,16... | collective-permute-start | bytes 2359304 | tf_op jit(solution)/shard_map/ppermute | solution.py:460
  125.2 9.4 %collective-permute-done.38.got = bf16[1536,128]{1,0:T(8,128)(2,1)S(1)} collective-permute-done((bf16[1536,128]{1,0:T(8,128)(2,1)S(1)}, bf16[1536,128]{1,0:T(8,128)(2,1)S(1)}, u32[]{:S(2)}, u32[]{:S(2)}) %collective-permute-start.38) | collective-permute-done | bytes 393248 | tf_op jit(solution)/shard_map/ppermute | solution.py:460
  134.6 1.9 %collective-permute-start.37 = (bf16[1536,128]{1,0:T(8,128)(2,1)S(1)}, bf16[1536,128]{1,0:T(8,128)(2,1)S(1)}, u32[]{:S(2)}, u32[]{:S(2)}) collective-permute-start(bf16[1536,128]{1,0:T(8,128)(2,1)S(1)} %shard_map.108), channel_id=1, source_target_pairs={{0,8},{8,0},{16,24},{24,16},{1,9},{9,1},{17,25},{25,17},{2,10},{10... | collective-permute-start | bytes 1179656 | tf_op jit(solution)/shard_map/ppermute | solution.py:484
  136.6 2.1 %collective-permute-start.39 = (bf16[1536,128]{1,0:T(8,128)(2,1)S(1)}, bf16[1536,128]{1,0:T(8,128)(2,1)S(1)}, u32[]{:S(2)}, u32[]{:S(2)}) collective-permute-start(bf16[1536,128]{1,0:T(8,128)(2,1)S(1)} %shard_map.109), channel_id=1, source_target_pairs={{0,8},{4,12},{8,0},{12,4},{16,24},{20,28},{24,16},{28,20},{1,9},{5... | collective-permute-start | bytes 1179656 | tf_op jit(solution)/shard_map/ppermute | solution.py:484
  139.5 8.7 %collective-permute-done.37.refs_5_ = bf16[1536,128]{1,0:T(8,128)(2,1)S(1)} collective-permute-done((bf16[1536,128]{1,0:T(8,128)(2,1)S(1)}, bf16[1536,128]{1,0:T(8,128)(2,1)S(1)}, u32[]{:S(2)}, u32[]{:S(2)}) %collective-permute-start.37) | collective-permute-done | bytes 393248 | tf_op jit(solution)/shard_map/ppermute | solution.py:484
  148.2 4.5 %collective-permute-done.39.refs_6_ = bf16[1536,128]{1,0:T(8,128)(2,1)S(1)} collective-permute-done((bf16[1536,128]{1,0:T(8,128)(2,1)S(1)}, bf16[1536,128]{1,0:T(8,128)(2,1)S(1)}, u32[]{:S(2)}, u32[]{:S(2)}) %collective-permute-start.39) | collective-permute-done | bytes 393248 | tf_op jit(solution)/shard_map/ppermute | solution.py:484
  (98 shorter events, 43.4 us)
Async XLA Ops:
  2.9 10.6 %collective-permute-start.13 = (bf16[2,192,256]{2,1,0:T(8,128)(2,1)S(1)}, bf16[2,192,256]{2,1,0:T(8,128)(2,1)S(1)}, u32[]{:S(2)}, u32[]{:S(2)}) collective-permute-start(bf16[2,192,256]{2,1,0:T(8,128)(2,1)S(1)} %get-tuple-element.45), channel_id=1, source_target_pairs={{0,16},{4,20},{8,24},{12,28},{16,0},{20,4},{24,8},{28,12},{1,17},{... | collective-permute-start | bytes 589832 | tf_op jit(solution)/shard_map/ppermute | solution.py:16
  3.4 10.1 %collective-permute-start.14 = (bf16[2,192,256]{2,1,0:T(8,128)(2,1)S(1)}, bf16[2,192,256]{2,1,0:T(8,128)(2,1)S(1)}, u32[]{:S(2)}, u32[]{:S(2)}) collective-permute-start(bf16[2,192,256]{2,1,0:T(8,128)(2,1)S(1)} %get-tuple-element.46), channel_id=1, source_target_pairs={{0,24},{4,28},{8,16},{12,20},{16,8},{20,12},{24,0},{28,4},{1,25},{... | collective-permute-start | bytes 589832 | tf_op jit(solution)/shard_map/ppermute | solution.py:16
  15.7 8.7 %collective-permute-start.2 = (bf16[48,768]{1,0:T(8,128)(2,1)S(1)}, bf16[48,768]{1,0:T(8,128)(2,1)S(1)}, u32[]{:S(2)}, u32[]{:S(2)}) collective-permute-start(bf16[48,768]{1,0:T(8,128)(2,1)S(1)} %get-tuple-element.40), channel_id=1, source_target_pairs={{0,3},{1,2},{2,1},{3,0},{4,7},{5,6},{6,5},{7,4},{8,11},{9,10},{10,... | collective-permute-start | bytes 221192 | tf_op jit(solution)/shard_map/ppermute | solution.py:16
  17.4 33.2 %collective-permute-start.16 = (bf16[1536,256]{1,0:T(8,128)(2,1)S(1)}, bf16[1536,256]{1,0:T(8,128)(2,1)S(1)}, u32[]{:S(2)}, u32[]{:S(2)}) collective-permute-start(bf16[1536,256]{1,0:T(8,128)(2,1)S(1)} %shard_map.92.refs_0_), channel_id=1, source_target_pairs={{0,1},{1,0},{2,3},{3,2},{4,5},{5,4},{6,7},{7,6},{8,9},{9,8},{10,11... | collective-permute-start | bytes 2359304 | tf_op jit(solution)/shard_map/ppermute | solution.py:16
  25.6 8.3 %collective-permute-start.3 = (bf16[3,48,768]{2,1,0:T(8,128)(2,1)S(1)}, bf16[3,48,768]{2,1,0:T(8,128)(2,1)S(1)}, u32[]{:S(2)}, u32[]{:S(2)}) collective-permute-start(bf16[3,48,768]{2,1,0:T(8,128)(2,1)S(1)} %shard_map.87.refs_0_), channel_id=1, source_target_pairs={{0,8},{4,12},{8,0},{12,4},{16,24},{20,28},{24,16},{28,20},{1,9},{5... | collective-permute-start | bytes 663560 | tf_op jit(solution)/shard_map/ppermute | solution.py:16
  26.4 16.7 %collective-permute-start.7 = (bf16[3,48,768]{2,1,0:T(8,128)(2,1)S(1)}, bf16[3,48,768]{2,1,0:T(8,128)(2,1)S(1)}, u32[]{:S(2)}, u32[]{:S(2)}) collective-permute-start(bf16[3,48,768]{2,1,0:T(8,128)(2,1)S(1)} %shard_map.87.refs_0_), channel_id=1, source_target_pairs={{0,4},{4,0},{8,12},{12,8},{16,20},{20,16},{24,28},{28,24},{1,5},{5... | collective-permute-start | bytes 663560 | tf_op jit(solution)/shard_map/ppermute | solution.py:16
  26.9 11.3 %collective-permute-start.19 = (bf16[2,192,256]{2,1,0:T(8,128)(2,1)S(1)}, bf16[2,192,256]{2,1,0:T(8,128)(2,1)S(1)}, u32[]{:S(2)}, u32[]{:S(2)}) collective-permute-start(bf16[2,192,256]{2,1,0:T(8,128)(2,1)S(1)} %get-tuple-element.48), channel_id=1, source_target_pairs={{0,8},{4,12},{8,0},{12,4},{16,24},{20,28},{24,16},{28,20},{1,9},{5... | collective-permute-start | bytes 589832 | tf_op jit(solution)/shard_map/ppermute | solution.py:16
  50.4 57.5 %collective-permute-start.17 = (bf16[1536,256]{1,0:T(8,128)(2,1)S(1)}, bf16[1536,256]{1,0:T(8,128)(2,1)S(1)}, u32[]{:S(2)}, u32[]{:S(2)}) collective-permute-start(bf16[1536,256]{1,0:T(8,128)(2,1)S(1)} %shard_map.93.a0), channel_id=1, source_target_pairs={{0,4},{4,0},{8,12},{12,8},{16,20},{20,16},{24,28},{28,24},{1,5},{5... | collective-permute-start | bytes 2359304 | tf_op jit(solution)/shard_map/ppermute | solution.py:16
  52.0 55.9 %collective-permute-start.18 = (bf16[1536,256]{1,0:T(8,128)(2,1)S(1)}, bf16[1536,256]{1,0:T(8,128)(2,1)S(1)}, u32[]{:S(2)}, u32[]{:S(2)}) collective-permute-start(bf16[1536,256]{1,0:T(8,128)(2,1)S(1)} %shard_map.94.a1), channel_id=1, source_target_pairs={{0,4},{4,0},{8,12},{12,8},{16,20},{20,16},{24,28},{28,24},{1,5},{5... | collective-permute-start | bytes 2359304 | tf_op jit(solution)/shard_map/ppermute | solution.py:16
  54.5 28.4 %collective-permute-start.28 = (bf16[1536,128]{1,0:T(8,128)(2,1)S(1)}, bf16[1536,128]{1,0:T(8,128)(2,1)S(1)}, u32[]{:S(2)}, u32[]{:S(2)}) collective-permute-start(bf16[1536,128]{1,0:T(8,128)(2,1)S(1)} %get-tuple-element.52.refs_1_), channel_id=1, source_target_pairs={{0,3},{1,2},{2,1},{3,0},{4,7},{5,6},{6,5},{7,4},{8,11},{9,10},{10,... | collective-permute-start | bytes 1179656 | tf_op jit(solution)/shard_map/ppermute | solution.py:16
  55.3 36.1 %collective-permute-start.25 = (bf16[1552,128]{1,0:T(8,128)(2,1)S(1)}, bf16[1552,128]{1,0:T(8,128)(2,1)S(1)}, u32[]{:S(2)}, u32[]{:S(2)}) collective-permute-start(bf16[1552,128]{1,0:T(8,128)(2,1)S(1)} %get-tuple-element.51.refs_0_), channel_id=1, source_target_pairs={{0,3},{1,2},{2,1},{3,0},{4,7},{5,6},{6,5},{7,4},{8,11},{9,10},{10,... | collective-permute-start | bytes 1191944 | tf_op jit(solution)/shard_map/ppermute | solution.py:16
  58.0 55.6 %collective-permute-start.26 = (bf16[1536,256]{1,0:T(8,128)(2,1)S(1)}, bf16[1536,256]{1,0:T(8,128)(2,1)S(1)}, u32[]{:S(2)}, u32[]{:S(2)}) collective-permute-start(bf16[1536,256]{1,0:T(8,128)(2,1)S(1)} %shard_map.98.beta.refs_0_), channel_id=1, source_target_pairs={{0,4},{4,0},{8,12},{12,8},{16,20},{20,16},{24,28},{28,24},{1,5},{5... | collective-permute-start | bytes 2359304 | tf_op jit(solution)/shard_map/ppermute | solution.py:16
  82.9 22.9 %collective-permute-start.24 = (f32[1]{0:T(128)}, f32[1]{0:T(128)}, u32[]{:S(2)}, u32[]{:S(2)}) collective-permute-start(f32[1]{0:T(128)} %collective-permute-done.23.occ_a), channel_id=1, source_target_pairs={{0,4},{4,0},{8,12},{12,8},{16,20},{20,16},{24,28},{28,24},{1,5},{5... | collective-permute-start | bytes 20 | tf_op jit(solution)/shard_map/ppermute | solution.py:16
  91.4 26.4 %collective-permute-start.29 = (bf16[1536,128]{1,0:T(8,128)(2,1)S(1)}, bf16[1536,128]{1,0:T(8,128)(2,1)S(1)}, u32[]{:S(2)}, u32[]{:S(2)}) collective-permute-start(bf16[1536,128]{1,0:T(8,128)(2,1)S(1)} %shard_map.102.beta.refs_4_.refs_0_), channel_id=1, source_target_pairs={{0,4},{4,0},{8,12},{12,8},{16,20},{20,16},{24,28},{28,24},{1,5},{5... | collective-permute-start | bytes 1179656 | tf_op jit(solution)/shard_map/ppermute | solution.py:16
  105.8 8.3 %collective-permute-start.27 = (bf16[1536,128]{1,0:T(8,128)(2,1)S(1)}, bf16[1536,128]{1,0:T(8,128)(2,1)S(1)}, u32[]{:S(2)}, u32[]{:S(2)}) collective-permute-start(bf16[1536,128]{1,0:T(8,128)(2,1)S(1)} %shard_map.101.beta.refs_2_), channel_id=1, source_target_pairs={{0,4},{4,0},{8,12},{12,8},{16,20},{20,16},{24,28},{28,24},{1,5},{5... | collective-permute-start | bytes 1179656 | tf_op jit(solution)/shard_map/ppermute | solution.py:16
  114.1 10.3 %collective-permute-start.34 = (bf16[1536,128]{1,0:T(8,128)(2,1)S(1)}, bf16[1536,128]{1,0:T(8,128)(2,1)S(1)}, u32[]{:S(2)}, u32[]{:S(2)}) collective-permute-start(bf16[1536,128]{1,0:T(8,128)(2,1)S(1)} %get-tuple-element.67), channel_id=1, source_target_pairs={{0,3},{1,2},{2,1},{3,0},{4,7},{7,4},{8,11},{9,10},{10,9},{11,8},{1... | collective-permute-start | bytes 1179656 | tf_op jit(solution)/shard_map/ppermute | solution.py:460
  118.4 16.3 %collective-permute-start.38 = (bf16[1536,128]{1,0:T(8,128)(2,1)S(1)}, bf16[1536,128]{1,0:T(8,128)(2,1)S(1)}, u32[]{:S(2)}, u32[]{:S(2)}) collective-permute-start(bf16[1536,128]{1,0:T(8,128)(2,1)S(1)} %get-tuple-element.69), channel_id=1, source_target_pairs={{0,3},{1,2},{2,1},{3,0},{4,5},{5,4},{6,7},{7,6},{8,11},{9,10},{10,... | collective-permute-start | bytes 1179656 | tf_op jit(solution)/shard_map/ppermute | solution.py:460
  119.7 16.9 %collective-permute-start.40 = (bf16[1536,128]{1,0:T(8,128)(2,1)S(1)}, bf16[1536,128]{1,0:T(8,128)(2,1)S(1)}, u32[]{:S(2)}, u32[]{:S(2)}) collective-permute-start(bf16[1536,128]{1,0:T(8,128)(2,1)S(1)} %get-tuple-element.71), channel_id=1, source_target_pairs={{4,5},{5,4},{6,7},{7,6},{12,13},{13,12},{14,15},{15,14},{20,21},{2... | collective-permute-start | bytes 1179656 | tf_op jit(solution)/shard_map/ppermute | solution.py:460
  120.4 18.4 %collective-permute-start.36 = (bf16[1536,128]{1,0:T(8,128)(2,1)S(1)}, bf16[1536,128]{1,0:T(8,128)(2,1)S(1)}, u32[]{:S(2)}, u32[]{:S(2)}) collective-permute-start(bf16[1536,128]{1,0:T(8,128)(2,1)S(1)} %get-tuple-element.65.near_one), channel_id=1, source_target_pairs={{4,7},{5,6},{6,5},{7,4},{12,15},{13,14},{14,13},{15,12},{20,23},{2... | collective-permute-start | bytes 1179656 | tf_op jit(solution)/shard_map/ppermute | solution.py:460
  121.1 31.6 %collective-permute-start.33 = (bf16[1536,256]{1,0:T(8,128)(2,1)S(1)}, bf16[1536,256]{1,0:T(8,128)(2,1)S(1)}, u32[]{:S(2)}, u32[]{:S(2)}) collective-permute-start(bf16[1536,256]{1,0:T(8,128)(2,1)S(1)} %get-tuple-element.66), channel_id=1, source_target_pairs={{0,1},{1,0},{2,3},{3,2},{8,9},{9,8},{10,11},{11,10},{16,17},{17,16... | collective-permute-start | bytes 2359304 | tf_op jit(solution)/shard_map/ppermute | solution.py:460
  124.4 15.0 %collective-permute-start.35 = (bf16[1536,128]{1,0:T(8,128)(2,1)S(1)}, bf16[1536,128]{1,0:T(8,128)(2,1)S(1)}, u32[]{:S(2)}, u32[]{:S(2)}) collective-permute-start(bf16[1536,128]{1,0:T(8,128)(2,1)S(1)} %get-tuple-element.67), channel_id=1, source_target_pairs={{5,6},{6,5},{13,14},{14,13},{21,22},{22,21},{29,30},{30,29}} | collective-permute-start | bytes 1179656 | tf_op jit(solution)/shard_map/ppermute | solution.py:460
  134.6 13.6 %collective-permute-start.37 = (bf16[1536,128]{1,0:T(8,128)(2,1)S(1)}, bf16[1536,128]{1,0:T(8,128)(2,1)S(1)}, u32[]{:S(2)}, u32[]{:S(2)}) collective-permute-start(bf16[1536,128]{1,0:T(8,128)(2,1)S(1)} %shard_map.108), channel_id=1, source_target_pairs={{0,8},{8,0},{16,24},{24,16},{1,9},{9,1},{17,25},{25,17},{2,10},{10... | collective-permute-start | bytes 1179656 | tf_op jit(solution)/shard_map/ppermute | solution.py:484
  136.6 16.1 %collective-permute-start.39 = (bf16[1536,128]{1,0:T(8,128)(2,1)S(1)}, bf16[1536,128]{1,0:T(8,128)(2,1)S(1)}, u32[]{:S(2)}, u32[]{:S(2)}) collective-permute-start(bf16[1536,128]{1,0:T(8,128)(2,1)S(1)} %shard_map.109), channel_id=1, source_target_pairs={{0,8},{4,12},{8,0},{12,4},{16,24},{20,28},{24,16},{28,20},{1,9},{5... | collective-permute-start | bytes 1179656 | tf_op jit(solution)/shard_map/ppermute | solution.py:484
  138.8 13.9 %collective-permute-start.41 = (bf16[1536,128]{1,0:T(8,128)(2,1)S(1)}, bf16[1536,128]{1,0:T(8,128)(2,1)S(1)}, u32[]{:S(2)}, u32[]{:S(2)}) collective-permute-start(bf16[1536,128]{1,0:T(8,128)(2,1)S(1)} %shard_map.110), channel_id=1, source_target_pairs={{4,12},{12,4},{20,28},{28,20},{5,13},{13,5},{21,29},{29,21},{6,14}... | collective-permute-start | bytes 1179656 | tf_op jit(solution)/shard_map/ppermute | solution.py:484
  (24 other events, 175.4 us)
